TPU v7x, 32 devices: a whole 2x2x4 slice. The times are simulated.
32 devices in a mesh: row: 8 (over y, x, core), col: 4 (over z).
Axes of the slice: x: 2, y: 2, z: 4, core: 2. Of those that a mesh axis runs over, the one named last changes fastest.
Arguments:
- alpha_prev: float32 [48, 4096], P(None, 'row'), may hold values from 0.1 to 10
- tokens: int32 [48], replicated, may hold values from 0 to 16639
- src_emb: bfloat16 [4096, 256], P('row'), may hold values from -10 to 10
- dst_emb: bfloat16 [256, 4096], P(None, ('row', 'col')), may hold values from -7 to 7
- emission: bfloat16 [16640, 4096], P(None, ('row', 'col')), may hold values from 0.02 to 8, as said below
Outputs:
- next_alpha: float32 [48, 4096], P(None, 'row')
- log_total: float32 [48], replicated
Inputs may be any that keep to these rules, and one draw needn't show every extreme that they name: `emission`: every weight is positive.
All inputs are finite; a program needn't handle non-finite values.
Results may differ from a plain program's by a relative error of at most 0.0014.
Values may be sent and summed in bfloat16 or wider, within the bound.
No kernel may reach another device: no remote copies, remote signals or barrier semaphores. Data moves between devices by JAX's collectives and lax.ppermute only.
A program may use at most 128 MiB of HBM per device.

v0:
```python
import math

import jax
import jax.numpy as jnp
from jax import lax
from jax.sharding import PartitionSpec as P


def absorb(folded, sources, shard_piece, group_cols):
    src_rows = sources.shape[0]
    piece_groups = shard_piece.shape[1] // group_cols
    per_turn = math.gcd(piece_groups, max(1, (1 << 20) // (src_rows * group_cols)))

    def absorb_block(turn_index, tile_state):
        expo_tile, part_peak, part_total = tile_state
        offset = turn_index * (per_turn * group_cols)
        columns = lax.dynamic_slice_in_dim(shard_piece, offset, per_turn * group_cols, 1)
        logits = jnp.dot(sources, columns, preferred_element_type=jnp.float32).reshape(
            src_rows, per_turn, group_cols
        )
        block_peak = jnp.max(logits, axis=2)
        shifted = jnp.exp(logits - block_peak[:, :, None])
        block_total = jnp.sum(shifted, axis=2)
        expo_block = shifted.reshape(src_rows, per_turn * group_cols).astype(jnp.bfloat16)
        expo_tile = lax.dynamic_update_slice_in_dim(expo_tile, expo_block, offset, 1)
        group_slot = turn_index * per_turn
        part_peak = lax.dynamic_update_slice_in_dim(part_peak, block_peak, group_slot, 1)
        part_total = lax.dynamic_update_slice_in_dim(part_total, block_total, group_slot, 1)
        return (expo_tile, part_peak, part_total)

    return lax.fori_loop(0, piece_groups // per_turn, absorb_block, folded)


def start_state(src_rows, tile_cols, group_cols):
    groups = tile_cols // group_cols
    return (
        jnp.zeros((src_rows, tile_cols), jnp.bfloat16),
        jnp.zeros((src_rows, groups), jnp.float32),
        jnp.zeros((src_rows, groups), jnp.float32),
    )


def on_device(alpha_prev, tokens, src_emb, dst_emb, emission):
    group_cols = dst_emb.shape[1]
    row_count = lax.axis_size("row")
    col_count = lax.axis_size("col")
    seq_count = alpha_prev.shape[0]
    row_index = lax.axis_index("row")
    tile_cols = group_cols * row_count
    folded = absorb(
        start_state(src_emb.shape[0], tile_cols, group_cols),
        src_emb,
        lax.all_gather(dst_emb, "row", axis=1, tiled=True),
        group_cols,
    )
    expo_tile, part_peak, part_total = folded
    src_rows = src_emb.shape[0]
    local_peak = jnp.max(part_peak, axis=1)
    local_total = jnp.sum(part_total * jnp.exp(part_peak - local_peak[:, None]), axis=1)
    row_peak = lax.pmax(local_peak, "col")
    row_total = lax.psum(local_total * jnp.exp(local_peak - row_peak), "col")
    row_scale = jnp.exp(part_peak - row_peak[:, None]) / row_total[:, None]
    local_groups = tile_cols // group_cols
    per_block = math.gcd(local_groups, 16)

    def multiply(block_index, partial_value):
        group_start = block_index * per_block
        scale_cols = lax.dynamic_slice_in_dim(row_scale, group_start, per_block, 1)
        weights = (scale_cols.T[:, None, :] * alpha_prev[None, :, :]).astype(jnp.bfloat16)
        expo_cols = lax.dynamic_slice_in_dim(
            expo_tile, group_start * group_cols, per_block * group_cols, 1
        ).reshape(src_rows, per_block, group_cols)
        product = jnp.einsum("gbi,igk->bgk", weights, expo_cols, preferred_element_type=jnp.float32)
        return lax.dynamic_update_slice_in_dim(
            partial_value,
            product.reshape(seq_count, per_block * group_cols),
            group_start * group_cols,
            1,
        )

    partial_value = lax.fori_loop(
        0, local_groups // per_block, multiply, jnp.zeros((seq_count, tile_cols), jnp.float32)
    )
    summed = lax.psum(partial_value, "row")
    own_sums = lax.dynamic_slice_in_dim(summed, row_index * group_cols, group_cols, 1)
    emit_rows = jnp.take(emission, tokens, axis=0).astype(jnp.float32)
    emitted = own_sums * emit_rows
    state_count = float(group_cols * row_count * col_count)
    total = lax.psum(jnp.sum(emitted, axis=1), ("row", "col"))
    scaled = emitted * (state_count / total)[:, None]
    next_alpha = lax.all_gather(scaled, "col", axis=1, tiled=True)
    log_total = jnp.log(total)
    return (next_alpha, log_total)


def solution(mesh):
    placed = (P(None, "row"), P(), P("row", None), P(None, ("row", "col")), P(None, ("row", "col")))
    return jax.shard_map(
        on_device, mesh=mesh, in_specs=placed, out_specs=(P(None, "row"), P()), check_vma=False
    )
```

profile of v0, /device:TPU:0, one launch (start us, length us, event | category | flops | bytes accessed | tf_op | source)
XLA Modules:
  0.0 166.4 jit_solution(14309806764282524219)
XLA Ops:
  7.2 0.0 copy-start
  7.2 0.0 all-reduce.2.cloned.1.call-start
  7.2 11.9 %all_gather.6 = bf16[256,1024]{1,0:T(8,128)(2,1)S(1)} all-gather(bf16[256,128]{1,0:T(8,128)(2,1)} %param.8), channel_id=1, replica_groups=mesh['row'=8,'col'=4] {'row'}, dimensions={1}, use_global_device_ids=true | all-gather | bytes 589824 | tf_op jit(solution)/shard_map/all_gather | solution.py:53
  19.1 0.0 copy-done
  19.1 0.4 fusion.11
  19.5 1.8 %copy.20 = f32[64,8,8,128]{3,2,1,0:T(8,128)} copy(f32[64,8,8,128]{3,1,2,0:T(8,128)S(1)} %bitcast.26) | data formatting | bytes 4194304
  21.3 2.2 %reduce_max.19 = f32[512,8]{1,0:T(8,128)S(1)} reduce(f32[512,8,128]{2,1,0:T(8,128)} %bitcast.27, f32[]{:T(128)} %constant.29.clone.1), dimensions={2}, to_apply=%region_0.1 | reduce | flops 520192 | bytes 2113540 | tf_op jit(solution)/shard_map/while/body/eval_jaxpr/reduce_max | solution.py:21
  23.6 2.8 %exponential_reduce_fusion = f32[512,8]{1,0:T(8,128)S(1)} fusion(f32[512,8,128]{2,1,0:T(8,128)} %bitcast.28, f32[512,8]{1,0:T(8,128)S(1)} %reduce_max.19), kind=kLoop, calls=%fused_computation.4 | loop fusion | flops 1044480 | bytes 2129920 | tf_op jit(solution)/shard_map/while/body/eval_jaxpr/reduce_sum | solution.py:23
  26.4 0.1 copy.15
  26.5 0.6 sub.38
  27.1 0.0 copy-start.1
  27.1 1.5 fusion.9
  28.6 0.0 copy-start.2
  28.6 12.1 %pmax.7 = f32[512]{0:T(512)S(1)} all-reduce(f32[512]{0:T(512)S(1)} %get-tuple-element.29), channel_id=1, replica_groups=mesh['row'=8,'col'=4] {'col'}, use_global_device_ids=true, to_apply=%region_2.3 | all-reduce | flops 512 | bytes 4096 | tf_op jit(solution)/shard_map/pmax | solution.py:60
  40.7 0.2 multiply_reduce_fusion
  41.0 8.4 %psum.21 = f32[512]{0:T(512)S(1)} all-reduce(f32[512]{0:T(512)S(1)} %exponential_multiply_fusion), channel_id=1, replica_groups=mesh['row'=8,'col'=4] {'col'}, use_global_device_ids=true, to_apply=%region_5.0 | all-reduce | flops 512 | bytes 4096 | tf_op jit(solution)/shard_map/psum | solution.py:61
  49.4 0.0 copy-done.1
  49.4 1.6 convolution_bitcast_fusion
  51.0 0.7 copy.30
  51.7 0.0 all-reduce.2.cloned.1.call-update
  51.7 0.0 copy-done.2
  51.8 3.3 %gather_fusion = bf16[48,128]{1,0:T(8,128)(2,1)S(1)} fusion(bf16[16640,128]{1,0:T(8,128)(2,1)} %param.9, s32[1024]{0:T(1024)S(1)} %pad_clamp_fusion), kind=kCustom, calls=%fused_computation | custom fusion | bytes 24768 | tf_op jit(solution)/shard_map/jit(_take)/gather | solution.py:86
  55.1 48.8 %all-reduce.2.cloned.1.call-done = f32[48,1024]{1,0:T(8,128)} async-done(((f32[48,1024]{1,0:T(8,128)}), f32[48,1024]{1,0:T(8,128)}) %all-reduce.2.cloned.1.call-update) | async-done | bytes 196624 | tf_op jit(solution)/shard_map/psum | solution.py:84
  103.9 0.9 fusion.8
  104.8 39.3 %psum.23 = f32[48]{0:T(128)S(1)} all-reduce(f32[48]{0:T(128)S(1)} %fusion.8), channel_id=1, replica_groups=mesh['row'=8,'col'=4] {'row','col'}, use_global_device_ids=true, to_apply=%region_8.0 | all-reduce | flops 48 | bytes 384 | tf_op jit(solution)/shard_map/psum | solution.py:89
  144.2 0.5 fusion.10
  144.7 0.8 fusion.7
  145.5 13.3 %all_gather.7 = f32[48,512]{1,0:T(8,128)S(1)} all-gather(f32[48,128]{1,0:T(8,128)S(1)} %fusion.7), channel_id=1, replica_groups=mesh['row'=8,'col'=4] {'col'}, dimensions={1}, use_global_device_ids=true | all-gather | bytes 122880 | tf_op jit(solution)/shard_map/all_gather | solution.py:91
  158.9 0.6 copy.33
  (5 shorter events, 0.0 us)
Async XLA Ops:
  7.2 11.9 %copy-start = (bf16[512,256]{1,0:T(8,128)(2,1)S(1)}, bf16[512,256]{1,0:T(8,128)(2,1)}, u32[]{:S(2)}) copy-start(bf16[512,256]{1,0:T(8,128)(2,1)} %param.7) | copy-start | bytes 786436
  7.2 96.7 %all-reduce.2.cloned.1.call-start = ((), (), s32[]{:S(2)}) async-start(), calls=%async_computation | async-start | bytes 393216 | tf_op jit(solution)/shard_map/psum | solution.py:84
  27.1 22.3 %copy-start.1 = (f32[48,512]{1,0:T(8,128)S(1)}, f32[48,512]{1,0:T(8,128)}, u32[]{:S(2)}) copy-start(f32[48,512]{1,0:T(8,128)} %param.5) | copy-start | bytes 294916
  28.6 23.1 %copy-start.2 = (s32[48]{0:T(128)S(1)}, s32[48]{0:T(128)}, u32[]{:S(2)}) copy-start(s32[48]{0:T(128)} %param.6) | copy-start | bytes 580
Sparse Core Ops, SparseCore 0:
  51.8 52.0 all-reduce.1
where the time goes:
time: 167 us; the launch traced here: 166 us
  blocking collectives  85 us (51%)
  waiting for transfers between devices  48.8 us (29%)
  between operations  14.1 us (8%)
  other arithmetic  9.08 us (5%)
  local copies, waits for them, and re-layouts  7.22 us (4%)
  matrix products  2.06 us (1%)
    psum x1, waiting for transfers between devices, on_device(): summed = lax.psum(partial_value, 'row')  48.8 us
    psum x1, blocking collectives, on_device(): total = lax.psum(jnp.sum(emitted, axis=1), ('row', 'col'))  39.3 us
    all_gather x1, blocking collectives, on_device(): next_alpha = lax.all_gather(scaled, 'col', axis=1, tiled=True)  13.3 us
    pmax x1, blocking collectives, on_device(): row_peak = lax.pmax(local_peak, 'col')  12.1 us
    all_gather x1, blocking collectives, on_device(): lax.all_gather(dst_emb, 'row', axis=1, tiled=True)  11.9 us
    psum x1, blocking collectives, on_device(): row_total = lax.psum(local_total * jnp.exp(local_peak - row_peak), 'col')  8.37 us
    gather x1, local copies, waits for them, and re-layouts, on_device(): emit_rows = jnp.take(emission, tokens, axis=0).astype(jnp.float32)  3.35 us
  transfers between devices with their start and end apart: 1, of which 1 were waited for; matrix products, arithmetic and copies ran while one was open for 2% of the time, Pallas kernels for 0%

commit v1 on v0

v1 whole, which is shorter than its diff:
```python
import functools
import math

import jax
import jax.numpy as jnp
from jax import lax
from jax.experimental import pallas as pl
from jax.experimental.pallas import tpu as pltpu
from jax.sharding import PartitionSpec as P

VMEM = pltpu.MemorySpace.VMEM
SMEM = pltpu.MemorySpace.SMEM
TAIL = 8
CHUNK = 8


def whole(shape):
    return pl.BlockSpec(shape, lambda *_: (0,) * len(shape))


def pick_rows(tokens_ref, table_ref, dst_ref, out_ref, chunks, picked, sem):
    seqs = picked.shape[0]
    depth = dst_ref.shape[0]
    for b in range(seqs):
        first = pl.multiple_of((tokens_ref[b] // CHUNK) * CHUNK, CHUNK)
        pltpu.make_async_copy(
            table_ref.at[pl.ds(first, CHUNK)], chunks.at[pl.ds(b * CHUNK, CHUNK)], sem
        ).start()
    out_ref[:depth] = dst_ref[...]
    pltpu.make_async_copy(table_ref.at[pl.ds(0, seqs * CHUNK)], chunks, sem).wait()
    rows = lax.broadcasted_iota(jnp.int32, (CHUNK, chunks.shape[1]), 0)
    for b in range(seqs):
        chunk = chunks[b * CHUNK : (b + 1) * CHUNK].astype(jnp.float32)
        kept = jnp.where(rows == tokens_ref[b] % CHUNK, chunk, 0.0)
        picked[b : b + 1] = jnp.sum(kept, axis=0, keepdims=True)
    out_ref[depth:] = picked[...].astype(out_ref.dtype)


def softmax_tile(per_step, src_ref, dst_ref, expo_ref, peak_ref, stat_ref, total_ref):
    step = pl.program_id(0)
    depth = src_ref.shape[1]
    for q in range(per_step):
        logits = lax.dot_general(
            dst_ref[q, :depth], src_ref[...], (((0,), (1,)), ((), ())), preferred_element_type=jnp.float32
        )
        peak = jnp.max(logits, axis=0, keepdims=True)
        shifted = jnp.exp(logits - peak)
        slot = pl.ds(step * per_step + q, 1)
        peak_ref[slot] = peak
        total_ref[slot] = jnp.sum(shifted, axis=0, keepdims=True)
        expo_ref[q] = shifted.astype(expo_ref.dtype)

    @pl.when(step == pl.num_programs(0) - 1)
    def _():
        local_peak = jnp.max(peak_ref[...], axis=0, keepdims=True)
        stat_ref[0:1] = local_peak
        stat_ref[1:2] = jnp.sum(total_ref[...] * jnp.exp(peak_ref[...] - local_peak), axis=0, keepdims=True)


def carry_tile(per_step, n_stats, *refs):
    stat_refs = refs[:n_stats]
    alpha_ref, expo_ref, peak_ref, emit_ref, out_ref, spread = refs[n_stats:]
    step = pl.program_id(0)
    seqs = alpha_ref.shape[0]
    depth = emit_ref.shape[1] - seqs

    @pl.when(step == 0)
    def _():
        spread[...] = jnp.zeros_like(spread)

    row_peak = functools.reduce(jnp.maximum, [s[0:1] for s in stat_refs])
    row_total = tree_sum([s[1:2] * jnp.exp(s[0:1] - row_peak) for s in stat_refs])
    for q in range(per_step):
        group = step * per_step + q
        row_scale = jnp.exp(peak_ref[pl.ds(group, 1)] - row_peak) / row_total
        weights = (alpha_ref[...] * row_scale).astype(jnp.bfloat16)
        product = lax.dot_general(
            weights, expo_ref[q], (((1,), (1,)), ((), ())), preferred_element_type=jnp.float32
        )
        out_ref[group, :seqs] = product
        spread[:seqs] += product * emit_ref[q, depth:].astype(jnp.float32)

    @pl.when(step == pl.num_programs(0) - 1)
    def _():
        share = jnp.sum(spread[...].T, axis=0, keepdims=True)
        tail = jnp.broadcast_to(share, (TAIL, share.shape[1]))
        for group in range(out_ref.shape[0]):
            out_ref[group, seqs:] = tail


def tree_sum(terms):
    while len(terms) > 1:
        terms = [a + b for a, b in zip(terms[::2], terms[1::2], strict=True)]
    return terms[0]


def emit_block(parts_ref, own_ref, out_ref):
    seqs = out_ref.shape[0] - TAIL
    sums = jnp.sum(parts_ref[...], axis=0)
    out_ref[:seqs] = sums[:seqs] * own_ref[own_ref.shape[0] - seqs :].astype(jnp.float32)
    out_ref[seqs:] = sums[seqs:]


def finish(states, n_blocks, *refs):
    place_ref = refs[0]
    block_refs = refs[1 : 1 + n_blocks]
    alpha_ref, log_ref = refs[1 + n_blocks :]
    seqs, cols = alpha_ref.shape[0], block_refs[0].shape[1]
    total = tree_sum([b[seqs:] for b in block_refs])
    log_ref[...] = jnp.log(total[0, :seqs])
    scale = (states / jnp.broadcast_to(total[0:1], (cols, cols)).T)[:seqs]
    for k in range(n_blocks):
        start = pl.multiple_of((place_ref[0] ^ k) * cols, cols)
        alpha_ref[:, pl.ds(start, cols)] = block_refs[k][:seqs] * scale


def swap(x, axis, count):
    return [x] + [lax.ppermute(x, axis, [(i, i ^ k) for i in range(count)]) for k in range(1, count)]


def on_device(alpha_prev, tokens, src_emb, dst_emb, emission):
    rows = lax.axis_size("row")
    cols = lax.axis_size("col")
    seqs, sources = alpha_prev.shape
    depth, group = dst_emb.shape
    f32 = jnp.float32

    packed = pl.pallas_call(
        pick_rows,
        out_shape=jax.ShapeDtypeStruct((depth + seqs, group), jnp.bfloat16),
        in_specs=[
            pl.BlockSpec(memory_space=SMEM),
            pl.BlockSpec(memory_space=pl.ANY),
            pl.BlockSpec(memory_space=VMEM),
        ],
        out_specs=pl.BlockSpec(memory_space=VMEM),
        scratch_shapes=[
            pltpu.VMEM((seqs * CHUNK, group), jnp.bfloat16),
            pltpu.VMEM((seqs, group), f32),
            pltpu.SemaphoreType.DMA,
        ],
        name="pick_rows",
    )(tokens, emission, dst_emb)

    gathered = lax.all_gather(packed, "row", axis=0)

    per_step = math.gcd(rows, 8)
    steps = rows // per_step
    expo, peak, stat = pl.pallas_call(
        functools.partial(softmax_tile, per_step),
        out_shape=(
            jax.ShapeDtypeStruct((rows, group, sources), jnp.bfloat16),
            jax.ShapeDtypeStruct((rows, sources), f32),
            jax.ShapeDtypeStruct((2, sources), f32),
        ),
        grid=(steps,),
        in_specs=[
            whole((sources, depth)),
            pl.BlockSpec((per_step, depth + seqs, group), lambda s: (s, 0, 0)),
        ],
        out_specs=(
            pl.BlockSpec((per_step, group, sources), lambda s: (s, 0, 0)),
            whole((rows, sources)),
            whole((2, sources)),
        ),
        scratch_shapes=[pltpu.VMEM((rows, sources), f32)],
        name="softmax_tile",
    )(src_emb, gathered)

    stats = swap(stat, "col", cols)
    partial = pl.pallas_call(
        functools.partial(carry_tile, per_step, cols),
        out_shape=jax.ShapeDtypeStruct((rows, seqs + TAIL, group), f32),
        grid=(steps,),
        in_specs=[whole((2, sources))] * cols
        + [
            whole((seqs, sources)),
            pl.BlockSpec((per_step, group, sources), lambda s: (s, 0, 0)),
            whole((rows, sources)),
            pl.BlockSpec((per_step, depth + seqs, group), lambda s: (s, 0, 0)),
        ],
        out_specs=whole((rows, seqs + TAIL, group)),
        scratch_shapes=[pltpu.VMEM((group, group), f32)],
        name="carry_tile",
    )(*stats, alpha_prev, expo, peak, gathered)

    parts = lax.all_to_all(partial, "row", 0, 0)
    block = pl.pallas_call(
        emit_block,
        out_shape=jax.ShapeDtypeStruct((seqs + TAIL, group), f32),
        in_specs=[pl.BlockSpec(memory_space=VMEM)] * 2,
        out_specs=pl.BlockSpec(memory_space=VMEM),
        name="emit_block",
    )(parts, packed)

    blocks = swap(block, "col", cols)
    place = lax.axis_index("col").astype(jnp.int32).reshape(1)
    return pl.pallas_call(
        functools.partial(finish, float(group * rows * cols), cols),
        out_shape=(jax.ShapeDtypeStruct((seqs, group * cols), f32), jax.ShapeDtypeStruct((seqs,), f32)),
        in_specs=[pl.BlockSpec(memory_space=SMEM)] + [pl.BlockSpec(memory_space=VMEM)] * cols,
        out_specs=(pl.BlockSpec(memory_space=VMEM), pl.BlockSpec(memory_space=VMEM)),
        name="finish",
    )(place, *blocks)


def solution(mesh):
    placed = (P(None, "row"), P(), P("row", None), P(None, ("row", "col")), P(None, ("row", "col")))
    return jax.shard_map(
        on_device, mesh=mesh, in_specs=placed, out_specs=(P(None, "row"), P()), check_vma=False
    )
```

time: 167 us -> 54.6 us (0.33)
  blocking collectives: 85 us -> 24.1 us
  waiting for transfers between devices: 48.8 us -> 7.73 us
  between operations: 14.1 us -> 0.65 us
  Pallas kernels: 0 us -> 11.6 us
  other arithmetic: 9.08 us -> 0 us
  starting transfers between devices: 0.04 us -> 8.79 us
  local copies, waits for them, and re-layouts: 7.22 us -> 1.2 us
  matrix products: 2.06 us -> 0 us
    psum x1 -> x0, waiting for transfers between devices: 48.8 us -> none  [on_device(): summed = lax.psum(partial_value, 'row')]
    psum x2 -> x0, blocking collectives: 47.7 us -> none  [the longest x1 39.3 us: on_device(): total = lax.psum(jnp.sum(emitted, axis=1), ('row', 'col'))]
    pmax x1 -> x0, blocking collectives: 12.1 us -> none  [on_device(): row_peak = lax.pmax(local_peak, 'col')]
    all_gather x2 -> x1, blocking collectives: 25.2 us -> 13.5 us  [on_device(): gathered = lax.all_gather(packed, 'row', axis=0)]
    pallas_call x0 -> x5, Pallas kernels: none -> 11.6 us  [the longest x1 3.04 us: on_device(): pl.pallas_call(functools.partial(softmax_tile, per_step), out_shape=(jax....]
    all_to_all x0 -> x1, blocking collectives: none -> 10.6 us  [on_device(): parts = lax.all_to_all(partial, 'row', 0, 0)]
    ppermute x0 -> x6, starting transfers between devices: none -> 8.79 us  [swap(): lax.ppermute(x, axis, [(i, i ^ k) for i in range(count)])]
    ppermute x0 -> x6, waiting for transfers between devices: none -> 7.73 us  [swap(): lax.ppermute(x, axis, [(i, i ^ k) for i in range(count)])]
  transfers between devices with their start and end apart: 1 -> 6, of which waited for: 1 -> 4; matrix products, arithmetic and copies ran while one was open for 2% -> 0% of each run, Pallas kernels for 0% -> 0%
where the time goes in v1:
time: 54.6 us; the launch traced here: 54.1 us
  blocking collectives  24.1 us (44%)
  Pallas kernels  11.6 us (21%)
  starting transfers between devices  8.79 us (16%)
  waiting for transfers between devices  7.73 us (14%)
  local copies, waits for them, and re-layouts  1.2 us (2%)
  between operations  0.65 us (1%)
    all_gather x1, blocking collectives, on_device(): gathered = lax.all_gather(packed, 'row', axis=0)  13.5 us
    all_to_all x1, blocking collectives, on_device(): parts = lax.all_to_all(partial, 'row', 0, 0)  10.6 us
    ppermute x6, starting transfers between devices, swap(): lax.ppermute(x, axis, [(i, i ^ k) for i in range(count)])  8.79 us
    ppermute x6, waiting for transfers between devices, swap(): lax.ppermute(x, axis, [(i, i ^ k) for i in range(count)])  7.73 us
    pallas_call x1, Pallas kernels, on_device(): pl.pallas_call(functools.partial(softmax_tile, per_step), out_shape=(jax....  3.04 us
    pallas_call x1, Pallas kernels, on_device(): pl.pallas_call(functools.partial(carry_tile, per_step, cols), out_shape=j...  2.71 us
    pallas_call x1, Pallas kernels, on_device(): pl.pallas_call(pick_rows, out_shape=jax.ShapeDtypeStruct((depth + seqs, g...  2.69 us
    pallas_call x1, Pallas kernels, on_device(): pl.pallas_call(emit_block, out_shape=jax.ShapeDtypeStruct((seqs + TAIL, g...  1.63 us
  transfers between devices with their start and end apart: 6, of which 4 were waited for; matrix products, arithmetic and copies ran while one was open for 0% of the time, Pallas kernels for 0%

profile of v1, /device:TPU:0, one launch (start us, length us, event | category | flops | bytes accessed | tf_op | source)
XLA Modules:
  0.0 54.1 jit_solution(10798271078796423103)
XLA Ops:
  0.6 2.7 %pick_rows.1.own_ref = bf16[304,128]{1,0:T(8,128)(2,1)} custom-call(s32[48]{0:T(128)} %tokens_ref.1, bf16[16640,128]{1,0:T(8,128)(2,1)} %table_ref.1, bf16[256,128]{1,0:T(8,128)(2,1)} %dst_ref.1), custom_call_target="tpu_custom_call" | custom-call | tf_op jit(solution)/shard_map/pick_rows/pallas_call | solution.py:128
  3.3 13.5 %all-gather = bf16[2432,128]{1,0:T(8,128)(2,1)} all-gather(bf16[304,128]{1,0:T(8,128)(2,1)} %pick_rows.1.own_ref), channel_id=2, replica_groups=mesh['row'=8,'col'=4] {'row'}, dimensions={0}, use_global_device_ids=true | all-gather | bytes 700416 | tf_op jit(solution)/shard_map/all_gather | solution.py:145
  16.9 3.0 %softmax_tile.1 = (bf16[8,128,512]{2,1,0:T(8,128)(2,1)}, f32[8,512]{1,0:T(8,128)}, f32[2,512]{1,0:T(2,128)}) custom-call(bf16[512,256]{1,0:T(8,128)(2,1)} %src_ref.1, bf16[8,304,128]{2,1,0:T(8,128)(2,1)} %bitcast.2), custom_call_target="tpu_custom_call" | custom-call | tf_op jit(solution)/shard_map/softmax_tile/pallas_call | solution.py:149
  19.9 1.6 %collective-permute-start = (f32[2,512]{1,0:T(2,128)}, f32[2,512]{1,0:T(2,128)S(1)}, u32[]{:S(2)}, u32[]{:S(2)}) collective-permute-start(f32[2,512]{1,0:T(2,128)} %get-tuple-element.5.refs_0_), channel_id=1, source_target_pairs={{0,1},{1,0},{2,3},{3,2},{4,5},{5,4},{6,7},{7,6},{8,9},{9,8},{10,11... | collective-permute-start | bytes 12296 | tf_op jit(solution)/shard_map/ppermute | solution.py:118
  21.5 2.6 %collective-permute-start.1 = (f32[2,512]{1,0:T(2,128)}, f32[2,512]{1,0:T(2,128)S(1)}, u32[]{:S(2)}, u32[]{:S(2)}) collective-permute-start(f32[2,512]{1,0:T(2,128)} %get-tuple-element.5.refs_0_), channel_id=1, source_target_pairs={{0,2},{1,3},{2,0},{3,1},{4,6},{5,7},{6,4},{7,5},{8,10},{9,11},{10,... | collective-permute-start | bytes 12296 | tf_op jit(solution)/shard_map/ppermute | solution.py:118
  24.1 0.2 collective-permute-start.2
  24.3 0.0 collective-permute-done.refs_1_
  24.3 0.0 copy-start.3
  24.3 1.9 %collective-permute-done.1.refs_2_ = f32[2,512]{1,0:T(2,128)S(1)} collective-permute-done((f32[2,512]{1,0:T(2,128)}, f32[2,512]{1,0:T(2,128)S(1)}, u32[]{:S(2)}, u32[]{:S(2)}) %collective-permute-start.1) | collective-permute-done | bytes 4128 | tf_op jit(solution)/shard_map/ppermute | solution.py:118
  26.2 0.0 copy-start.4
  26.2 3.5 %collective-permute-done.2.refs_3_ = f32[2,512]{1,0:T(2,128)S(1)} collective-permute-done((f32[2,512]{1,0:T(2,128)}, f32[2,512]{1,0:T(2,128)S(1)}, u32[]{:S(2)}, u32[]{:S(2)}) %collective-permute-start.2) | collective-permute-done | bytes 4128 | tf_op jit(solution)/shard_map/ppermute | solution.py:118
  29.7 0.0 copy-start.5
  29.7 0.0 copy-done.3
  29.7 0.0 copy-done.4
  29.7 0.6 %copy-done.5 = f32[2,512]{1,0:T(2,128)} copy-done((f32[2,512]{1,0:T(2,128)}, f32[2,512]{1,0:T(2,128)S(1)}, u32[]{:S(2)}) %copy-start.5) | copy-done | bytes 4120
  30.3 2.7 %carry_tile.1 = f32[8,56,128]{2,1,0:T(8,128)} custom-call(f32[2,512]{1,0:T(2,128)} %get-tuple-element.5.refs_0_, f32[2,512]{1,0:T(2,128)} %copy-done.3, f32[2,512]{1,0:T(2,128)} %copy-done.4, f32[2,512]{1,0:T(2,128)} %copy-done.5, f32[48,512]{1,0:T(8,128)} %refs_4_.1, bf16[8,128,512]{2,1,0:T(8,128)(2,1)} %get-tuple-element.6.refs_5_, ...), custom_call_target="tpu_custom_call" | custom-call | tf_op jit(solution)/shard_map/carry_tile/pallas_call | solution.py:171
  33.0 10.6 %all_to_all.5.parts_ref = f32[8,56,128]{2,1,0:T(8,128)} all-to-all(f32[8,56,128]{2,1,0:T(8,128)} %carry_tile.1), channel_id=1, replica_groups=mesh['row'=8,'col'=4] {'row'}, dimensions={0} | all-to-all | bytes 458752 | tf_op jit(solution)/shard_map/all_to_all | solution.py:187
  43.6 1.6 %emit_block.1.refs_1_ = f32[56,128]{1,0:T(8,128)} custom-call(f32[8,56,128]{2,1,0:T(8,128)} %all_to_all.5.parts_ref, bf16[304,128]{1,0:T(8,128)(2,1)} %pick_rows.1.own_ref), custom_call_target="tpu_custom_call" | custom-call | tf_op jit(solution)/shard_map/emit_block/pallas_call | solution.py:188
  45.2 0.0 collective-permute-start.3
  45.2 0.8 %collective-permute-start.4 = (f32[56,128]{1,0:T(8,128)}, f32[56,128]{1,0:T(8,128)S(1)}, u32[]{:S(2)}, u32[]{:S(2)}) collective-permute-start(f32[56,128]{1,0:T(8,128)} %emit_block.1.refs_1_), channel_id=1, source_target_pairs={{0,2},{1,3},{2,0},{3,1},{4,6},{5,7},{6,4},{7,5},{8,10},{9,11},{10,... | collective-permute-start | bytes 86024 | tf_op jit(solution)/shard_map/ppermute | solution.py:118
  46.0 3.6 %collective-permute-start.5 = (f32[56,128]{1,0:T(8,128)}, f32[56,128]{1,0:T(8,128)S(1)}, u32[]{:S(2)}, u32[]{:S(2)}) collective-permute-start(f32[56,128]{1,0:T(8,128)} %emit_block.1.refs_1_), channel_id=1, source_target_pairs={{0,3},{1,2},{2,1},{3,0},{4,7},{5,6},{6,5},{7,4},{8,11},{9,10},{10,... | collective-permute-start | bytes 86024 | tf_op jit(solution)/shard_map/ppermute | solution.py:118
  49.6 0.0 collective-permute-done.3.refs_2_
  49.6 0.0 copy-start
  49.6 0.8 %collective-permute-done.4.refs_3_ = f32[56,128]{1,0:T(8,128)S(1)} collective-permute-done((f32[56,128]{1,0:T(8,128)}, f32[56,128]{1,0:T(8,128)S(1)}, u32[]{:S(2)}, u32[]{:S(2)}) %collective-permute-start.4) | collective-permute-done | bytes 28704 | tf_op jit(solution)/shard_map/ppermute | solution.py:118
  50.4 0.0 copy-start.1
  50.4 1.6 %collective-permute-done.5.refs_4_ = f32[56,128]{1,0:T(8,128)S(1)} collective-permute-done((f32[56,128]{1,0:T(8,128)}, f32[56,128]{1,0:T(8,128)S(1)}, u32[]{:S(2)}, u32[]{:S(2)}) %collective-permute-start.5) | collective-permute-done | bytes 28704 | tf_op jit(solution)/shard_map/ppermute | solution.py:118
  52.0 0.0 copy-start.2
  52.0 0.0 copy-done
  52.0 0.0 copy-done.1
  52.0 0.6 %copy-done.2 = f32[56,128]{1,0:T(8,128)} copy-done((f32[56,128]{1,0:T(8,128)}, f32[56,128]{1,0:T(8,128)S(1)}, u32[]{:S(2)}) %copy-start.2) | copy-done | bytes 28696
  52.6 1.5 %finish.1 = (f32[48,512]{1,0:T(8,128)}, f32[48]{0:T(128)}) custom-call(s32[1]{0:T(128)} %bitcast.refs_0_, f32[56,128]{1,0:T(8,128)} %emit_block.1.refs_1_, f32[56,128]{1,0:T(8,128)} %copy-done, f32[56,128]{1,0:T(8,128)} %copy-done.1, f32[56,128]{1,0:T(8,128)} %copy-done.2), custom_call_target="tpu_custom_call" | custom-call | tf_op jit(solution)/shard_map/finish/pallas_call | solution.py:198
Async XLA Ops:
  19.9 4.4 %collective-permute-start = (f32[2,512]{1,0:T(2,128)}, f32[2,512]{1,0:T(2,128)S(1)}, u32[]{:S(2)}, u32[]{:S(2)}) collective-permute-start(f32[2,512]{1,0:T(2,128)} %get-tuple-element.5.refs_0_), channel_id=1, source_target_pairs={{0,1},{1,0},{2,3},{3,2},{4,5},{5,4},{6,7},{7,6},{8,9},{9,8},{10,11... | collective-permute-start | bytes 12296 | tf_op jit(solution)/shard_map/ppermute | solution.py:118
  21.5 4.7 %collective-permute-start.1 = (f32[2,512]{1,0:T(2,128)}, f32[2,512]{1,0:T(2,128)S(1)}, u32[]{:S(2)}, u32[]{:S(2)}) collective-permute-start(f32[2,512]{1,0:T(2,128)} %get-tuple-element.5.refs_0_), channel_id=1, source_target_pairs={{0,2},{1,3},{2,0},{3,1},{4,6},{5,7},{6,4},{7,5},{8,10},{9,11},{10,... | collective-permute-start | bytes 12296 | tf_op jit(solution)/shard_map/ppermute | solution.py:118
  24.1 5.6 %collective-permute-start.2 = (f32[2,512]{1,0:T(2,128)}, f32[2,512]{1,0:T(2,128)S(1)}, u32[]{:S(2)}, u32[]{:S(2)}) collective-permute-start(f32[2,512]{1,0:T(2,128)} %get-tuple-element.5.refs_0_), channel_id=1, source_target_pairs={{0,3},{1,2},{2,1},{3,0},{4,7},{5,6},{6,5},{7,4},{8,11},{9,10},{10,... | collective-permute-start | bytes 12296 | tf_op jit(solution)/shard_map/ppermute | solution.py:118
  24.3 5.4 %copy-start.3 = (f32[2,512]{1,0:T(2,128)}, f32[2,512]{1,0:T(2,128)S(1)}, u32[]{:S(2)}) copy-start(f32[2,512]{1,0:T(2,128)S(1)} %collective-permute-done.refs_1_) | copy-start | bytes 12292
  26.2 3.5 %copy-start.4 = (f32[2,512]{1,0:T(2,128)}, f32[2,512]{1,0:T(2,128)S(1)}, u32[]{:S(2)}) copy-start(f32[2,512]{1,0:T(2,128)S(1)} %collective-permute-done.1.refs_2_) | copy-start | bytes 12292
  29.7 0.6 %copy-start.5 = (f32[2,512]{1,0:T(2,128)}, f32[2,512]{1,0:T(2,128)S(1)}, u32[]{:S(2)}) copy-start(f32[2,512]{1,0:T(2,128)S(1)} %collective-permute-done.2.refs_3_) | copy-start | bytes 12292
  45.2 4.4 %collective-permute-start.3 = (f32[56,128]{1,0:T(8,128)}, f32[56,128]{1,0:T(8,128)S(1)}, u32[]{:S(2)}, u32[]{:S(2)}) collective-permute-start(f32[56,128]{1,0:T(8,128)} %emit_block.1.refs_1_), channel_id=1, source_target_pairs={{0,1},{1,0},{2,3},{3,2},{4,5},{5,4},{6,7},{7,6},{8,9},{9,8},{10,11... | collective-permute-start | bytes 86024 | tf_op jit(solution)/shard_map/ppermute | solution.py:118
  45.2 5.2 %collective-permute-start.4 = (f32[56,128]{1,0:T(8,128)}, f32[56,128]{1,0:T(8,128)S(1)}, u32[]{:S(2)}, u32[]{:S(2)}) collective-permute-start(f32[56,128]{1,0:T(8,128)} %emit_block.1.refs_1_), channel_id=1, source_target_pairs={{0,2},{1,3},{2,0},{3,1},{4,6},{5,7},{6,4},{7,5},{8,10},{9,11},{10,... | collective-permute-start | bytes 86024 | tf_op jit(solution)/shard_map/ppermute | solution.py:118
  46.0 5.9 %collective-permute-start.5 = (f32[56,128]{1,0:T(8,128)}, f32[56,128]{1,0:T(8,128)S(1)}, u32[]{:S(2)}, u32[]{:S(2)}) collective-permute-start(f32[56,128]{1,0:T(8,128)} %emit_block.1.refs_1_), channel_id=1, source_target_pairs={{0,3},{1,2},{2,1},{3,0},{4,7},{5,6},{6,5},{7,4},{8,11},{9,10},{10,... | collective-permute-start | bytes 86024 | tf_op jit(solution)/shard_map/ppermute | solution.py:118
  49.6 2.4 %copy-start = (f32[56,128]{1,0:T(8,128)}, f32[56,128]{1,0:T(8,128)S(1)}, u32[]{:S(2)}) copy-start(f32[56,128]{1,0:T(8,128)S(1)} %collective-permute-done.3.refs_2_) | copy-start | bytes 86020
  50.4 1.6 %copy-start.1 = (f32[56,128]{1,0:T(8,128)}, f32[56,128]{1,0:T(8,128)S(1)}, u32[]{:S(2)}) copy-start(f32[56,128]{1,0:T(8,128)S(1)} %collective-permute-done.4.refs_3_) | copy-start | bytes 86020
  52.0 0.6 %copy-start.2 = (f32[56,128]{1,0:T(8,128)}, f32[56,128]{1,0:T(8,128)S(1)}, u32[]{:S(2)}) copy-start(f32[56,128]{1,0:T(8,128)S(1)} %collective-permute-done.5.refs_4_) | copy-start | bytes 86020

commit v2 on v1

--- a/solution.py
+++ b/solution.py
@@ -10,12 +10,22 @@
 
 VMEM = pltpu.MemorySpace.VMEM
 SMEM = pltpu.MemorySpace.SMEM
+HBM = pltpu.MemorySpace.HBM
 TAIL = 8
 CHUNK = 8
 
 
-def whole(shape):
-    return pl.BlockSpec(shape, lambda *_: (0,) * len(shape))
+def room(mebibytes):
+    return pltpu.CompilerParams(vmem_limit_bytes=mebibytes << 20)
+
+
+def block_specs(steps, shapes):
+    if steps == 1:
+        return [pl.BlockSpec(memory_space=VMEM) for _ in shapes]
+    return [
+        pl.BlockSpec(shape, lambda s, n=len(shape), moves=moves: (s if moves else 0,) + (0,) * (n - 1))
+        for shape, moves in shapes
+    ]
 
 
 def pick_rows(tokens_ref, table_ref, dst_ref, out_ref, chunks, picked, sem):
@@ -36,8 +46,8 @@
     out_ref[depth:] = picked[...].astype(out_ref.dtype)
 
 
-def softmax_tile(per_step, src_ref, dst_ref, expo_ref, peak_ref, stat_ref, total_ref):
-    step = pl.program_id(0)
+def softmax_tile(steps, per_step, src_ref, dst_ref, expo_ref, peak_ref, stat_ref, total_ref):
+    step = pl.program_id(0) if steps > 1 else 0
     depth = src_ref.shape[1]
     for q in range(per_step):
         logits = lax.dot_general(
@@ -50,17 +60,17 @@
         total_ref[slot] = jnp.sum(shifted, axis=0, keepdims=True)
         expo_ref[q] = shifted.astype(expo_ref.dtype)
 
-    @pl.when(step == pl.num_programs(0) - 1)
+    @pl.when(step == steps - 1)
     def _():
         local_peak = jnp.max(peak_ref[...], axis=0, keepdims=True)
         stat_ref[0:1] = local_peak
         stat_ref[1:2] = jnp.sum(total_ref[...] * jnp.exp(peak_ref[...] - local_peak), axis=0, keepdims=True)
 
 
-def carry_tile(per_step, n_stats, *refs):
+def carry_tile(steps, per_step, n_stats, *refs):
     stat_refs = refs[:n_stats]
     alpha_ref, expo_ref, peak_ref, emit_ref, out_ref, spread = refs[n_stats:]
-    step = pl.program_id(0)
+    step = pl.program_id(0) if steps > 1 else 0
     seqs = alpha_ref.shape[0]
     depth = emit_ref.shape[1] - seqs
 
@@ -80,7 +90,7 @@
         out_ref[group, :seqs] = product
         spread[:seqs] += product * emit_ref[q, depth:].astype(jnp.float32)
 
-    @pl.when(step == pl.num_programs(0) - 1)
+    @pl.when(step == steps - 1)
     def _():
         share = jnp.sum(spread[...].T, axis=0, keepdims=True)
         tail = jnp.broadcast_to(share, (TAIL, share.shape[1]))
@@ -130,7 +140,7 @@
         out_shape=jax.ShapeDtypeStruct((depth + seqs, group), jnp.bfloat16),
         in_specs=[
             pl.BlockSpec(memory_space=SMEM),
-            pl.BlockSpec(memory_space=pl.ANY),
+            pl.BlockSpec(memory_space=HBM),
             pl.BlockSpec(memory_space=VMEM),
         ],
         out_specs=pl.BlockSpec(memory_space=VMEM),
@@ -140,48 +150,45 @@
             pltpu.SemaphoreType.DMA,
         ],
         name="pick_rows",
-    )(tokens, emission, dst_emb)
+        compiler_params=room(8),
+    )(tokens, pltpu.with_memory_space_constraint(emission, HBM), dst_emb)
 
     gathered = lax.all_gather(packed, "row", axis=0)
 
     per_step = math.gcd(rows, 8)
     steps = rows // per_step
+    grid = (steps,) if steps > 1 else ()
+    arrived = ((per_step, depth + seqs, group), True)
+    tile = ((per_step, group, sources), True)
     expo, peak, stat = pl.pallas_call(
-        functools.partial(softmax_tile, per_step),
+        functools.partial(softmax_tile, steps, per_step),
         out_shape=(
             jax.ShapeDtypeStruct((rows, group, sources), jnp.bfloat16),
             jax.ShapeDtypeStruct((rows, sources), f32),
             jax.ShapeDtypeStruct((2, sources), f32),
         ),
-        grid=(steps,),
-        in_specs=[
-            whole((sources, depth)),
-            pl.BlockSpec((per_step, depth + seqs, group), lambda s: (s, 0, 0)),
-        ],
-        out_specs=(
-            pl.BlockSpec((per_step, group, sources), lambda s: (s, 0, 0)),
-            whole((rows, sources)),
-            whole((2, sources)),
-        ),
+        grid=grid,
+        in_specs=block_specs(steps, [((sources, depth), False), arrived]),
+        out_specs=block_specs(steps, [tile, ((rows, sources), False), ((2, sources), False)]),
         scratch_shapes=[pltpu.VMEM((rows, sources), f32)],
         name="softmax_tile",
+        compiler_params=room(16),
     )(src_emb, gathered)
 
     stats = swap(stat, "col", cols)
-    partial = pl.pallas_call(
-        functools.partial(carry_tile, per_step, cols),
-        out_shape=jax.ShapeDtypeStruct((rows, seqs + TAIL, group), f32),
-        grid=(steps,),
-        in_specs=[whole((2, sources))] * cols
-        + [
-            whole((seqs, sources)),
-            pl.BlockSpec((per_step, group, sources), lambda s: (s, 0, 0)),
-            whole((rows, sources)),
-            pl.BlockSpec((per_step, depth + seqs, group), lambda s: (s, 0, 0)),
-        ],
-        out_specs=whole((rows, seqs + TAIL, group)),
+    stat_block = ((2, sources), False)
+    (partial,) = pl.pallas_call(
+        functools.partial(carry_tile, steps, per_step, cols),
+        out_shape=(jax.ShapeDtypeStruct((rows, seqs + TAIL, group), f32),),
+        grid=grid,
+        in_specs=block_specs(
+            steps,
+            [stat_block] * cols + [((seqs, sources), False), tile, ((rows, sources), False), arrived],
+        ),
+        out_specs=block_specs(steps, [((rows, seqs + TAIL, group), False)]),
         scratch_shapes=[pltpu.VMEM((group, group), f32)],
         name="carry_tile",
+        compiler_params=room(16),
     )(*stats, alpha_prev, expo, peak, gathered)
 
     parts = lax.all_to_all(partial, "row", 0, 0)
@@ -191,6 +198,7 @@
         in_specs=[pl.BlockSpec(memory_space=VMEM)] * 2,
         out_specs=pl.BlockSpec(memory_space=VMEM),
         name="emit_block",
+        compiler_params=room(8),
     )(parts, packed)
 
     blocks = swap(block, "col", cols)
@@ -201,6 +209,7 @@
         in_specs=[pl.BlockSpec(memory_space=SMEM)] + [pl.BlockSpec(memory_space=VMEM)] * cols,
         out_specs=(pl.BlockSpec(memory_space=VMEM), pl.BlockSpec(memory_space=VMEM)),
         name="finish",
+        compiler_params=room(8),
     )(place, *blocks)
 
 

time: 54.6 us -> 43.4 us (0.79)
  Pallas kernels: 11.6 us -> 3.98 us
  blocking collectives: 24.1 us -> 20.7 us
    pallas_call x2, Pallas kernels: 5.76 us -> 1.49 us  [the longest x1 0.93 us: on_device(): pl.pallas_call(functools.partial(softmax_tile, steps, per_step), out_shap...]
    all_gather x1, blocking collectives: 13.5 us -> 11.6 us  [on_device(): gathered = lax.all_gather(packed, 'row', axis=0)]
    pallas_call x1, Pallas kernels: 1.63 us -> 0.02 us  [on_device(): pl.pallas_call(emit_block, out_shape=jax.ShapeDtypeStruct((seqs + TAIL, g...]
    all_to_all x1, blocking collectives: 10.6 us -> 9.16 us  [on_device(): parts = lax.all_to_all(partial, 'row', 0, 0)]
    pallas_call x1, Pallas kernels: 2.69 us -> 1.74 us  [on_device(): pl.pallas_call(pick_rows, out_shape=jax.ShapeDtypeStruct((depth + seqs, g...]
    pallas_call x1, Pallas kernels: 1.53 us -> 0.74 us  [on_device(): pl.pallas_call(functools.partial(finish, float(group * rows * cols), cols...]
    unnamed x12 -> x8, local copies, waits for them, and re-layouts: 1.2 us -> 1.54 us
where the time goes in v2:
time: 43.4 us; the launch traced here: 43.2 us
  blocking collectives  20.7 us (48%)
  starting transfers between devices  8.91 us (21%)
  waiting for transfers between devices  7.32 us (17%)
  Pallas kernels  3.98 us (9%)
  local copies, waits for them, and re-layouts  1.54 us (4%)
  between operations  0.69 us (2%)
    all_gather x1, blocking collectives, on_device(): gathered = lax.all_gather(packed, 'row', axis=0)  11.6 us
    all_to_all x1, blocking collectives, on_device(): parts = lax.all_to_all(partial, 'row', 0, 0)  9.16 us
    ppermute x6, starting transfers between devices, swap(): lax.ppermute(x, axis, [(i, i ^ k) for i in range(count)])  8.91 us
    ppermute x6, waiting for transfers between devices, swap(): lax.ppermute(x, axis, [(i, i ^ k) for i in range(count)])  7.32 us
    pallas_call x1, Pallas kernels, on_device(): pl.pallas_call(pick_rows, out_shape=jax.ShapeDtypeStruct((depth + seqs, g...  1.74 us
    unnamed x8, local copies, waits for them, and re-layouts  1.54 us
    pallas_call x1, Pallas kernels, on_device(): pl.pallas_call(functools.partial(softmax_tile, steps, per_step), out_shap...  0.93 us
  transfers between devices with their start and end apart: 6, of which 4 were waited for; matrix products, arithmetic and copies ran while one was open for 0% of the time, Pallas kernels for 0%

profile of v2, /device:TPU:0, one launch (start us, length us, event | category | flops | bytes accessed | tf_op | source)
XLA Modules:
  0.0 43.2 jit_solution(2598027342162074233)
XLA Ops:
  0.6 0.0 copy-start
  0.6 0.0 copy-start.2
  0.7 0.9 %copy-done.2 = bf16[256,128]{1,0:T(8,128)(2,1)S(1)} copy-done((bf16[256,128]{1,0:T(8,128)(2,1)S(1)}, bf16[256,128]{1,0:T(8,128)(2,1)}, u32[]{:S(2)}) %copy-start.2) | copy-done | bytes 65560
  1.5 0.0 copy-start.3
  1.5 0.7 %copy-done.3 = s32[48]{0:T(128)S(1)} copy-done((s32[48]{0:T(128)S(1)}, s32[48]{0:T(128)}, u32[]{:S(2)}) %copy-start.3) | copy-done | bytes 216
  2.2 0.0 copy-start.1
  2.2 1.7 %pick_rows.1.own_ref = bf16[304,128]{1,0:T(8,128)(2,1)S(1)} custom-call(s32[48]{0:T(128)S(1)} %copy-done.3, bf16[16640,128]{1,0:T(8,128)(2,1)} %table_ref.1, bf16[256,128]{1,0:T(8,128)(2,1)S(1)} %copy-done.2), custom_call_target="tpu_custom_call" | custom-call | tf_op jit(solution)/shard_map/pick_rows/pallas_call | solution.py:138
  3.9 11.6 %all-gather = bf16[2432,128]{1,0:T(8,128)(2,1)S(1)} all-gather(bf16[304,128]{1,0:T(8,128)(2,1)S(1)} %pick_rows.1.own_ref), channel_id=2, replica_groups=mesh['row'=8,'col'=4] {'row'}, dimensions={0}, use_global_device_ids=true | all-gather | bytes 700416 | tf_op jit(solution)/shard_map/all_gather | solution.py:156
  15.5 0.0 copy-done
  15.5 0.9 %softmax_tile.1 = (bf16[8,128,512]{2,1,0:T(8,128)(2,1)S(1)}, f32[8,512]{1,0:T(8,128)S(1)}, f32[2,512]{1,0:T(2,128)S(1)}) custom-call(bf16[512,256]{1,0:T(8,128)(2,1)S(1)} %copy-done, bf16[8,304,128]{2,1,0:T(8,128)(2,1)S(1)} %bitcast.2), custom_call_target="tpu_custom_call" | custom-call | tf_op jit(solution)/shard_map/softmax_tile/pallas_call | solution.py:163
  16.4 1.7 %collective-permute-start = (f32[2,512]{1,0:T(2,128)S(1)}, f32[2,512]{1,0:T(2,128)S(1)}, u32[]{:S(2)}, u32[]{:S(2)}) collective-permute-start(f32[2,512]{1,0:T(2,128)S(1)} %get-tuple-element.5.refs_0_), channel_id=1, source_target_pairs={{0,1},{1,0},{2,3},{3,2},{4,5},{5,4},{6,7},{7,6},{8,9},{9,8},{10,11... | collective-permute-start | bytes 12296 | tf_op jit(solution)/shard_map/ppermute | solution.py:128
  18.1 2.6 %collective-permute-start.1 = (f32[2,512]{1,0:T(2,128)S(1)}, f32[2,512]{1,0:T(2,128)S(1)}, u32[]{:S(2)}, u32[]{:S(2)}) collective-permute-start(f32[2,512]{1,0:T(2,128)S(1)} %get-tuple-element.5.refs_0_), channel_id=1, source_target_pairs={{0,2},{1,3},{2,0},{3,1},{4,6},{5,7},{6,4},{7,5},{8,10},{9,11},{10,... | collective-permute-start | bytes 12296 | tf_op jit(solution)/shard_map/ppermute | solution.py:128
  20.7 0.2 collective-permute-start.2
  20.9 0.0 collective-permute-done.refs_1_
  20.9 1.7 %collective-permute-done.1.refs_2_ = f32[2,512]{1,0:T(2,128)S(1)} collective-permute-done((f32[2,512]{1,0:T(2,128)S(1)}, f32[2,512]{1,0:T(2,128)S(1)}, u32[]{:S(2)}, u32[]{:S(2)}) %collective-permute-start.1) | collective-permute-done | bytes 4128 | tf_op jit(solution)/shard_map/ppermute | solution.py:128
  22.6 3.5 %collective-permute-done.2.refs_3_ = f32[2,512]{1,0:T(2,128)S(1)} collective-permute-done((f32[2,512]{1,0:T(2,128)S(1)}, f32[2,512]{1,0:T(2,128)S(1)}, u32[]{:S(2)}, u32[]{:S(2)}) %collective-permute-start.2) | collective-permute-done | bytes 4128 | tf_op jit(solution)/shard_map/ppermute | solution.py:128
  26.1 0.0 copy-done.1
  26.1 0.6 %carry_tile.1 = f32[8,56,128]{2,1,0:T(8,128)S(1)} custom-call(f32[2,512]{1,0:T(2,128)S(1)} %get-tuple-element.5.refs_0_, f32[2,512]{1,0:T(2,128)S(1)} %collective-permute-done.refs_1_, f32[2,512]{1,0:T(2,128)S(1)} %collective-permute-done.1.refs_2_, f32[2,512]{1,0:T(2,128)S(1)} %collective-permute-done.2.refs_3_, f32[48,512]{1,0:T(8,128)S(1)} %copy-done.1, ...), custom_call_target="tpu_custom_call" | custom-call | tf_op jit(solution)/shard_map/carry_tile/pallas_call | solution.py:180
  26.7 9.2 %all_to_all.5.parts_ref = f32[8,56,128]{2,1,0:T(8,128)S(1)} all-to-all(f32[8,56,128]{2,1,0:T(8,128)S(1)} %carry_tile.1), channel_id=1, replica_groups=mesh['row'=8,'col'=4] {'row'}, dimensions={0} | all-to-all | bytes 458752 | tf_op jit(solution)/shard_map/all_to_all | solution.py:194
  35.8 0.1 collective-permute-start.3
  35.9 0.8 %collective-permute-start.4 = (f32[56,128]{1,0:T(8,128)S(1)}, f32[56,128]{1,0:T(8,128)S(1)}, u32[]{:S(2)}, u32[]{:S(2)}) collective-permute-start(f32[56,128]{1,0:T(8,128)S(1)} %emit_block.1.refs_1_), channel_id=1, source_target_pairs={{0,2},{1,3},{2,0},{3,1},{4,6},{5,7},{6,4},{7,5},{8,10},{9,11},{10,... | collective-permute-start | bytes 86024 | tf_op jit(solution)/shard_map/ppermute | solution.py:128
  36.7 3.6 %collective-permute-start.5 = (f32[56,128]{1,0:T(8,128)S(1)}, f32[56,128]{1,0:T(8,128)S(1)}, u32[]{:S(2)}, u32[]{:S(2)}) collective-permute-start(f32[56,128]{1,0:T(8,128)S(1)} %emit_block.1.refs_1_), channel_id=1, source_target_pairs={{0,3},{1,2},{2,1},{3,0},{4,7},{5,6},{6,5},{7,4},{8,11},{9,10},{10,... | collective-permute-start | bytes 86024 | tf_op jit(solution)/shard_map/ppermute | solution.py:128
  40.3 0.0 collective-permute-done.3.refs_2_
  40.3 0.6 %collective-permute-done.4.refs_3_ = f32[56,128]{1,0:T(8,128)S(1)} collective-permute-done((f32[56,128]{1,0:T(8,128)S(1)}, f32[56,128]{1,0:T(8,128)S(1)}, u32[]{:S(2)}, u32[]{:S(2)}) %collective-permute-start.4) | collective-permute-done | bytes 28704 | tf_op jit(solution)/shard_map/ppermute | solution.py:128
  40.9 1.6 %collective-permute-done.5.refs_4_ = f32[56,128]{1,0:T(8,128)S(1)} collective-permute-done((f32[56,128]{1,0:T(8,128)S(1)}, f32[56,128]{1,0:T(8,128)S(1)}, u32[]{:S(2)}, u32[]{:S(2)}) %collective-permute-start.5) | collective-permute-done | bytes 28704 | tf_op jit(solution)/shard_map/ppermute | solution.py:128
  42.4 0.7 %finish.1 = (f32[48,512]{1,0:T(8,128)}, f32[48]{0:T(128)}) custom-call(s32[1]{0:T(128)} %bitcast.refs_0_, f32[56,128]{1,0:T(8,128)S(1)} %emit_block.1.refs_1_, f32[56,128]{1,0:T(8,128)S(1)} %collective-permute-done.3.refs_2_, f32[56,128]{1,0:T(8,128)S(1)} %collective-permute-done.4.refs_3_, f32[56,128]{1,0:T(8,128)S(1)} %collective-permute-done.5.refs_4_), custom_call_target="tpu_custom_call" | custom-call | tf_op jit(solution)/shard_map/finish/pallas_call | solution.py:206
  (1 shorter events, 0.0 us)
Async XLA Ops:
  0.6 14.9 %copy-start = (bf16[512,256]{1,0:T(8,128)(2,1)S(1)}, bf16[512,256]{1,0:T(8,128)(2,1)}, u32[]{:S(2)}) copy-start(bf16[512,256]{1,0:T(8,128)(2,1)} %src_ref.1) | copy-start | bytes 786436
  0.6 0.9 %copy-start.2 = (bf16[256,128]{1,0:T(8,128)(2,1)S(1)}, bf16[256,128]{1,0:T(8,128)(2,1)}, u32[]{:S(2)}) copy-start(bf16[256,128]{1,0:T(8,128)(2,1)} %dst_ref.1) | copy-start | bytes 196612
  1.5 0.7 %copy-start.3 = (s32[48]{0:T(128)S(1)}, s32[48]{0:T(128)}, u32[]{:S(2)}) copy-start(s32[48]{0:T(128)} %tokens_ref.1) | copy-start | bytes 580
  2.2 23.9 %copy-start.1 = (f32[48,512]{1,0:T(8,128)S(1)}, f32[48,512]{1,0:T(8,128)}, u32[]{:S(2)}) copy-start(f32[48,512]{1,0:T(8,128)} %refs_4_.1) | copy-start | bytes 294916
  16.4 4.5 %collective-permute-start = (f32[2,512]{1,0:T(2,128)S(1)}, f32[2,512]{1,0:T(2,128)S(1)}, u32[]{:S(2)}, u32[]{:S(2)}) collective-permute-start(f32[2,512]{1,0:T(2,128)S(1)} %get-tuple-element.5.refs_0_), channel_id=1, source_target_pairs={{0,1},{1,0},{2,3},{3,2},{4,5},{5,4},{6,7},{7,6},{8,9},{9,8},{10,11... | collective-permute-start | bytes 12296 | tf_op jit(solution)/shard_map/ppermute | solution.py:128
  18.1 4.5 %collective-permute-start.1 = (f32[2,512]{1,0:T(2,128)S(1)}, f32[2,512]{1,0:T(2,128)S(1)}, u32[]{:S(2)}, u32[]{:S(2)}) collective-permute-start(f32[2,512]{1,0:T(2,128)S(1)} %get-tuple-element.5.refs_0_), channel_id=1, source_target_pairs={{0,2},{1,3},{2,0},{3,1},{4,6},{5,7},{6,4},{7,5},{8,10},{9,11},{10,... | collective-permute-start | bytes 12296 | tf_op jit(solution)/shard_map/ppermute | solution.py:128
  20.7 5.4 %collective-permute-start.2 = (f32[2,512]{1,0:T(2,128)S(1)}, f32[2,512]{1,0:T(2,128)S(1)}, u32[]{:S(2)}, u32[]{:S(2)}) collective-permute-start(f32[2,512]{1,0:T(2,128)S(1)} %get-tuple-element.5.refs_0_), channel_id=1, source_target_pairs={{0,3},{1,2},{2,1},{3,0},{4,7},{5,6},{6,5},{7,4},{8,11},{9,10},{10,... | collective-permute-start | bytes 12296 | tf_op jit(solution)/shard_map/ppermute | solution.py:128
  35.8 4.5 %collective-permute-start.3 = (f32[56,128]{1,0:T(8,128)S(1)}, f32[56,128]{1,0:T(8,128)S(1)}, u32[]{:S(2)}, u32[]{:S(2)}) collective-permute-start(f32[56,128]{1,0:T(8,128)S(1)} %emit_block.1.refs_1_), channel_id=1, source_target_pairs={{0,1},{1,0},{2,3},{3,2},{4,5},{5,4},{6,7},{7,6},{8,9},{9,8},{10,11... | collective-permute-start | bytes 86024 | tf_op jit(solution)/shard_map/ppermute | solution.py:128
  35.9 4.9 %collective-permute-start.4 = (f32[56,128]{1,0:T(8,128)S(1)}, f32[56,128]{1,0:T(8,128)S(1)}, u32[]{:S(2)}, u32[]{:S(2)}) collective-permute-start(f32[56,128]{1,0:T(8,128)S(1)} %emit_block.1.refs_1_), channel_id=1, source_target_pairs={{0,2},{1,3},{2,0},{3,1},{4,6},{5,7},{6,4},{7,5},{8,10},{9,11},{10,... | collective-permute-start | bytes 86024 | tf_op jit(solution)/shard_map/ppermute | solution.py:128
  36.7 5.8 %collective-permute-start.5 = (f32[56,128]{1,0:T(8,128)S(1)}, f32[56,128]{1,0:T(8,128)S(1)}, u32[]{:S(2)}, u32[]{:S(2)}) collective-permute-start(f32[56,128]{1,0:T(8,128)S(1)} %emit_block.1.refs_1_), channel_id=1, source_target_pairs={{0,3},{1,2},{2,1},{3,0},{4,7},{5,6},{6,5},{7,4},{8,11},{9,10},{10,... | collective-permute-start | bytes 86024 | tf_op jit(solution)/shard_map/ppermute | solution.py:128

commit v3 on v2

--- a/solution.py
+++ b/solution.py
@@ -28,30 +28,37 @@
     ]
 
 
-def pick_rows(tokens_ref, table_ref, dst_ref, out_ref, chunks, picked, sem):
+def pick_rows(tokens_ref, table_ref, dst_ref, out_ref, ids, chunks, picked, ids_sem, dst_sem, sem):
     seqs = picked.shape[0]
     depth = dst_ref.shape[0]
+    ids_copy = pltpu.make_async_copy(tokens_ref, ids, ids_sem)
+    dst_copy = pltpu.make_async_copy(dst_ref, out_ref.at[pl.ds(0, depth)], dst_sem)
+    ids_copy.start()
+    dst_copy.start()
+    ids_copy.wait()
     for b in range(seqs):
-        first = pl.multiple_of((tokens_ref[b] // CHUNK) * CHUNK, CHUNK)
+        first = pl.multiple_of((ids[b] // CHUNK) * CHUNK, CHUNK)
         pltpu.make_async_copy(
             table_ref.at[pl.ds(first, CHUNK)], chunks.at[pl.ds(b * CHUNK, CHUNK)], sem
         ).start()
-    out_ref[:depth] = dst_ref[...]
     pltpu.make_async_copy(table_ref.at[pl.ds(0, seqs * CHUNK)], chunks, sem).wait()
     rows = lax.broadcasted_iota(jnp.int32, (CHUNK, chunks.shape[1]), 0)
     for b in range(seqs):
         chunk = chunks[b * CHUNK : (b + 1) * CHUNK].astype(jnp.float32)
-        kept = jnp.where(rows == tokens_ref[b] % CHUNK, chunk, 0.0)
+        kept = jnp.where(rows == ids[b] % CHUNK, chunk, 0.0)
         picked[b : b + 1] = jnp.sum(kept, axis=0, keepdims=True)
     out_ref[depth:] = picked[...].astype(out_ref.dtype)
-
-
-def softmax_tile(steps, per_step, src_ref, dst_ref, expo_ref, peak_ref, stat_ref, total_ref):
+    dst_copy.wait()
+
+
+def softmax_tile(steps, per_step, src_ref, *refs):
+    dst_refs = refs[:-4]
+    expo_ref, peak_ref, stat_ref, total_ref = refs[-4:]
     step = pl.program_id(0) if steps > 1 else 0
     depth = src_ref.shape[1]
     for q in range(per_step):
         logits = lax.dot_general(
-            dst_ref[q, :depth], src_ref[...], (((0,), (1,)), ((), ())), preferred_element_type=jnp.float32
+            nth(dst_refs, q)[:depth], src_ref[...], (((0,), (1,)), ((), ())), preferred_element_type=jnp.float32
         )
         peak = jnp.max(logits, axis=0, keepdims=True)
         shifted = jnp.exp(logits - peak)
@@ -67,12 +74,15 @@
         stat_ref[1:2] = jnp.sum(total_ref[...] * jnp.exp(peak_ref[...] - local_peak), axis=0, keepdims=True)
 
 
-def carry_tile(steps, per_step, n_stats, *refs):
+def carry_tile(steps, per_step, n_stats, n_out, *refs):
     stat_refs = refs[:n_stats]
-    alpha_ref, expo_ref, peak_ref, emit_ref, out_ref, spread = refs[n_stats:]
+    alpha_ref, expo_ref, peak_ref = refs[n_stats : n_stats + 3]
+    emit_refs = refs[n_stats + 3 : -1 - n_out]
+    out_refs = refs[-1 - n_out : -1]
+    spread = refs[-1]
     step = pl.program_id(0) if steps > 1 else 0
     seqs = alpha_ref.shape[0]
-    depth = emit_ref.shape[1] - seqs
+    each = out_refs[0].shape[0]
 
     @pl.when(step == 0)
     def _():
@@ -87,15 +97,24 @@
         product = lax.dot_general(
             weights, expo_ref[q], (((1,), (1,)), ((), ())), preferred_element_type=jnp.float32
         )
-        out_ref[group, :seqs] = product
-        spread[:seqs] += product * emit_ref[q, depth:].astype(jnp.float32)
+        if steps > 1:
+            out_refs[0][group, :seqs] = product
+        else:
+            out_refs[q // each][q % each, :seqs] = product
+        emit_ref = nth(emit_refs, q)
+        spread[:seqs] += product * emit_ref[emit_ref.shape[0] - seqs :].astype(jnp.float32)
 
     @pl.when(step == steps - 1)
     def _():
         share = jnp.sum(spread[...].T, axis=0, keepdims=True)
         tail = jnp.broadcast_to(share, (TAIL, share.shape[1]))
-        for group in range(out_ref.shape[0]):
-            out_ref[group, seqs:] = tail
+        for out_ref in out_refs:
+            for group in range(each):
+                out_ref[group, seqs:] = tail
+
+
+def nth(refs, q):
+    return refs[q] if len(refs) > 1 else refs[0].at[q]
 
 
 def tree_sum(terms):
@@ -104,9 +123,18 @@
     return terms[0]
 
 
-def emit_block(parts_ref, own_ref, out_ref):
+def add_pair(kept_ref, given_ref, *out_refs):
+    for m, out_ref in enumerate(out_refs):
+        out_ref[...] = kept_ref[m] + given_ref[m]
+
+
+def emit_block(own_ref, *refs):
+    parts_refs, out_ref = refs[:-1], refs[-1]
     seqs = out_ref.shape[0] - TAIL
-    sums = jnp.sum(parts_ref[...], axis=0)
+    if len(parts_refs) > 1:
+        sums = tree_sum([r[...] for r in parts_refs])
+    else:
+        sums = jnp.sum(parts_refs[0][...], axis=0)
     out_ref[:seqs] = sums[:seqs] * own_ref[own_ref.shape[0] - seqs :].astype(jnp.float32)
     out_ref[seqs:] = sums[seqs:]
 
@@ -124,8 +152,12 @@
         alpha_ref[:, pl.ds(start, cols)] = block_refs[k][:seqs] * scale
 
 
+def hop(x, axis, count, k):
+    return lax.ppermute(x, axis, [(i, i ^ k) for i in range(count)])
+
+
 def swap(x, axis, count):
-    return [x] + [lax.ppermute(x, axis, [(i, i ^ k) for i in range(count)]) for k in range(1, count)]
+    return [x] + [hop(x, axis, count, k) for k in range(1, count)]
 
 
 def on_device(alpha_prev, tokens, src_emb, dst_emb, emission):
@@ -138,27 +170,31 @@
     packed = pl.pallas_call(
         pick_rows,
         out_shape=jax.ShapeDtypeStruct((depth + seqs, group), jnp.bfloat16),
-        in_specs=[
-            pl.BlockSpec(memory_space=SMEM),
-            pl.BlockSpec(memory_space=HBM),
-            pl.BlockSpec(memory_space=VMEM),
-        ],
+        in_specs=[pl.BlockSpec(memory_space=HBM)] * 3,
         out_specs=pl.BlockSpec(memory_space=VMEM),
         scratch_shapes=[
+            pltpu.SMEM((seqs,), jnp.int32),
             pltpu.VMEM((seqs * CHUNK, group), jnp.bfloat16),
             pltpu.VMEM((seqs, group), f32),
+            pltpu.SemaphoreType.DMA,
+            pltpu.SemaphoreType.DMA,
             pltpu.SemaphoreType.DMA,
         ],
         name="pick_rows",
         compiler_params=room(8),
-    )(tokens, pltpu.with_memory_space_constraint(emission, HBM), dst_emb)
-
-    gathered = lax.all_gather(packed, "row", axis=0)
+    )(*[pltpu.with_memory_space_constraint(x, HBM) for x in (tokens, emission, dst_emb)])
+
+    paired = rows == 8
+    if paired:
+        like = [packed] + [hop(packed, "row", rows, k) for k in range(2, rows, 2)]
+        arrived = like + [hop(x, "row", rows, 1) for x in like]
+    else:
+        arrived = [lax.all_gather(packed, "row", axis=0)]
 
     per_step = math.gcd(rows, 8)
     steps = rows // per_step
     grid = (steps,) if steps > 1 else ()
-    arrived = ((per_step, depth + seqs, group), True)
+    arrived_blocks = [((per_step, depth + seqs, group), True)] * len(arrived)
     tile = ((per_step, group, sources), True)
     expo, peak, stat = pl.pallas_call(
         functools.partial(softmax_tile, steps, per_step),
@@ -168,38 +204,51 @@
             jax.ShapeDtypeStruct((2, sources), f32),
         ),
         grid=grid,
-        in_specs=block_specs(steps, [((sources, depth), False), arrived]),
+        in_specs=block_specs(steps, [((sources, depth), False)] + arrived_blocks),
         out_specs=block_specs(steps, [tile, ((rows, sources), False), ((2, sources), False)]),
         scratch_shapes=[pltpu.VMEM((rows, sources), f32)],
         name="softmax_tile",
         compiler_params=room(16),
-    )(src_emb, gathered)
+    )(src_emb, *arrived)
 
     stats = swap(stat, "col", cols)
     stat_block = ((2, sources), False)
-    (partial,) = pl.pallas_call(
-        functools.partial(carry_tile, steps, per_step, cols),
-        out_shape=(jax.ShapeDtypeStruct((rows, seqs + TAIL, group), f32),),
+    n_out = 2 if paired else 1
+    partial = pl.pallas_call(
+        functools.partial(carry_tile, steps, per_step, cols, n_out),
+        out_shape=(jax.ShapeDtypeStruct((rows // n_out, seqs + TAIL, group), f32),) * n_out,
         grid=grid,
         in_specs=block_specs(
             steps,
-            [stat_block] * cols + [((seqs, sources), False), tile, ((rows, sources), False), arrived],
+            [stat_block] * cols + [((seqs, sources), False), tile, ((rows, sources), False)] + arrived_blocks,
         ),
-        out_specs=block_specs(steps, [((rows, seqs + TAIL, group), False)]),
+        out_specs=block_specs(steps, [((rows // n_out, seqs + TAIL, group), False)] * n_out),
         scratch_shapes=[pltpu.VMEM((group, group), f32)],
         name="carry_tile",
         compiler_params=room(16),
-    )(*stats, alpha_prev, expo, peak, gathered)
-
-    parts = lax.all_to_all(partial, "row", 0, 0)
+    )(*stats, alpha_prev, expo, peak, *arrived)
+
+    if paired:
+        given = hop(partial[1], "row", rows, 1)
+        sums = pl.pallas_call(
+            add_pair,
+            out_shape=(jax.ShapeDtypeStruct((seqs + TAIL, group), f32),) * (rows // 2),
+            in_specs=[pl.BlockSpec(memory_space=VMEM)] * 2,
+            out_specs=(pl.BlockSpec(memory_space=VMEM),) * (rows // 2),
+            name="add_pair",
+            compiler_params=room(8),
+        )(partial[0], given)
+        parts = [sums[0]] + [hop(sums[m], "row", rows, 2 * m) for m in range(1, rows // 2)]
+    else:
+        parts = [lax.all_to_all(partial[0], "row", 0, 0)]
     block = pl.pallas_call(
         emit_block,
         out_shape=jax.ShapeDtypeStruct((seqs + TAIL, group), f32),
-        in_specs=[pl.BlockSpec(memory_space=VMEM)] * 2,
+        in_specs=[pl.BlockSpec(memory_space=VMEM)] * (1 + len(parts)),
         out_specs=pl.BlockSpec(memory_space=VMEM),
         name="emit_block",
         compiler_params=room(8),
-    )(parts, packed)
+    )(packed, *parts)
 
     blocks = swap(block, "col", cols)
     place = lax.axis_index("col").astype(jnp.int32).reshape(1)

time: 43.4 us -> 40 us (0.922)
  blocking collectives: 20.7 us -> 0 us
  waiting for transfers between devices: 7.32 us -> 17.8 us
  starting transfers between devices: 8.91 us -> 17.1 us
  local copies, waits for them, and re-layouts: 1.54 us -> 0.01 us
    all_gather x1 -> x0, blocking collectives: 11.6 us -> none  [on_device(): gathered = lax.all_gather(packed, 'row', axis=0)]
    ppermute x6 -> x17, waiting for transfers between devices: 7.32 us -> 17.8 us  [hop(): return lax.ppermute(x, axis, [(i, i ^ k) for i in range(count)])]
    all_to_all x1 -> x0, blocking collectives: 9.16 us -> none  [on_device(): parts = lax.all_to_all(partial, 'row', 0, 0)]
    ppermute x6 -> x17, starting transfers between devices: 8.91 us -> 17.1 us  [hop(): return lax.ppermute(x, axis, [(i, i ^ k) for i in range(count)])]
    unnamed x8 -> x4, local copies, waits for them, and re-layouts: 1.54 us -> 0.01 us
  transfers between devices with their start and end apart: 6 -> 17, of which waited for: 4 -> 12; matrix products, arithmetic and copies ran while one was open for 0% -> 0% of each run, Pallas kernels for 0% -> 0%
where the time goes in v3:
time: 40 us; the launch traced here: 39.9 us
  waiting for transfers between devices  17.8 us (44%)
  starting transfers between devices  17.1 us (43%)
  Pallas kernels  4.3 us (11%)
  between operations  0.72 us (2%)
    ppermute x17, waiting for transfers between devices, hop(): return lax.ppermute(x, axis, [(i, i ^ k) for i in range(count)])  17.8 us
    ppermute x17, starting transfers between devices, hop(): return lax.ppermute(x, axis, [(i, i ^ k) for i in range(count)])  17.1 us
    pallas_call x1, Pallas kernels, on_device(): pl.pallas_call(pick_rows, out_shape=jax.ShapeDtypeStruct((depth + seqs, g...  2.01 us
    pallas_call x1, Pallas kernels, on_device(): pl.pallas_call(functools.partial(softmax_tile, steps, per_step), out_shap...  0.95 us
  transfers between devices with their start and end apart: 17, of which 12 were waited for; matrix products, arithmetic and copies ran while one was open for 0% of the time, Pallas kernels for 0%

profile of v3, /device:TPU:0, one launch (start us, length us, event | category | flops | bytes accessed | tf_op | source)
XLA Modules:
  0.0 39.9 jit_solution(592737753944381014)
XLA Ops:
  0.6 0.0 copy-start
  0.6 0.0 copy-start.1
  0.7 2.0 %pick_rows.1.refs_0_.refs_7_.own_ref = bf16[304,128]{1,0:T(8,128)(2,1)S(1)} custom-call(s32[48]{0:T(128)} %tokens_ref.1, bf16[16640,128]{1,0:T(8,128)(2,1)} %table_ref.1, bf16[256,128]{1,0:T(8,128)(2,1)} %dst_ref.1), custom_call_target="tpu_custom_call" | custom-call | tf_op jit(solution)/shard_map/pick_rows/pallas_call | solution.py:170
  2.7 3.0 %collective-permute-start = (bf16[304,128]{1,0:T(8,128)(2,1)S(1)}, bf16[304,128]{1,0:T(8,128)(2,1)S(1)}, u32[]{:S(2)}, u32[]{:S(2)}) collective-permute-start(bf16[304,128]{1,0:T(8,128)(2,1)S(1)} %pick_rows.1.refs_0_.refs_7_.own_ref), channel_id=1, source_target_pairs={{0,8},{4,12},{8,0},{12,4},{16,24},{20,28},{24,16},{28,20},{1,9},{5... | collective-permute-start | bytes 233480 | tf_op jit(solution)/shard_map/ppermute | solution.py:156
  5.7 1.5 %collective-permute-start.1 = (bf16[304,128]{1,0:T(8,128)(2,1)S(1)}, bf16[304,128]{1,0:T(8,128)(2,1)S(1)}, u32[]{:S(2)}, u32[]{:S(2)}) collective-permute-start(bf16[304,128]{1,0:T(8,128)(2,1)S(1)} %pick_rows.1.refs_0_.refs_7_.own_ref), channel_id=1, source_target_pairs={{0,16},{4,20},{8,24},{12,28},{16,0},{20,4},{24,8},{28,12},{1,17},{... | collective-permute-start | bytes 233480 | tf_op jit(solution)/shard_map/ppermute | solution.py:156
  7.2 0.0 collective-permute-start.2
  7.2 0.0 collective-permute-start.3
  7.2 1.1 %collective-permute-done.refs_1_.refs_8_ = bf16[304,128]{1,0:T(8,128)(2,1)S(1)} collective-permute-done((bf16[304,128]{1,0:T(8,128)(2,1)S(1)}, bf16[304,128]{1,0:T(8,128)(2,1)S(1)}, u32[]{:S(2)}, u32[]{:S(2)}) %collective-permute-start) | collective-permute-done | bytes 77856 | tf_op jit(solution)/shard_map/ppermute | solution.py:156
  8.3 0.0 collective-permute-start.4
  8.3 2.6 %collective-permute-done.1.refs_2_.refs_9_ = bf16[304,128]{1,0:T(8,128)(2,1)S(1)} collective-permute-done((bf16[304,128]{1,0:T(8,128)(2,1)S(1)}, bf16[304,128]{1,0:T(8,128)(2,1)S(1)}, u32[]{:S(2)}, u32[]{:S(2)}) %collective-permute-start.1) | collective-permute-done | bytes 77856 | tf_op jit(solution)/shard_map/ppermute | solution.py:156
  10.9 0.0 collective-permute-start.5
  10.9 1.6 %collective-permute-done.2.refs_3_.refs_10_ = bf16[304,128]{1,0:T(8,128)(2,1)S(1)} collective-permute-done((bf16[304,128]{1,0:T(8,128)(2,1)S(1)}, bf16[304,128]{1,0:T(8,128)(2,1)S(1)}, u32[]{:S(2)}, u32[]{:S(2)}) %collective-permute-start.2) | collective-permute-done | bytes 77856 | tf_op jit(solution)/shard_map/ppermute | solution.py:156
  12.5 0.0 collective-permute-start.6
  12.5 0.0 collective-permute-done.3.refs_4_.refs_11_
  12.5 0.0 collective-permute-done.4.refs_5_.refs_12_
  12.5 0.0 collective-permute-done.5.refs_6_.refs_13_
  12.5 1.2 %collective-permute-done.6.refs_7_.refs_14_ = bf16[304,128]{1,0:T(8,128)(2,1)S(1)} collective-permute-done((bf16[304,128]{1,0:T(8,128)(2,1)S(1)}, bf16[304,128]{1,0:T(8,128)(2,1)S(1)}, u32[]{:S(2)}, u32[]{:S(2)}) %collective-permute-start.6) | collective-permute-done | bytes 77856 | tf_op jit(solution)/shard_map/ppermute | solution.py:156
  13.8 0.0 copy-done
  13.8 0.9 %softmax_tile.1 = (bf16[8,128,512]{2,1,0:T(8,128)(2,1)S(1)}, f32[8,512]{1,0:T(8,128)S(1)}, f32[2,512]{1,0:T(2,128)S(1)}) custom-call(bf16[512,256]{1,0:T(8,128)(2,1)S(1)} %copy-done, bf16[304,128]{1,0:T(8,128)(2,1)S(1)} %pick_rows.1.refs_0_.refs_7_.own_ref, bf16[304,128]{1,0:T(8,128)(2,1)S(1)} %collective-permute-done.refs_1_.refs_8_, ...), custom_call_target="tpu_custom_call" | custom-call | tf_op jit(solution)/shard_map/softmax_tile/pallas_call | solution.py:199
  14.7 1.6 %collective-permute-start.7 = (f32[2,512]{1,0:T(2,128)S(1)}, f32[2,512]{1,0:T(2,128)S(1)}, u32[]{:S(2)}, u32[]{:S(2)}) collective-permute-start(f32[2,512]{1,0:T(2,128)S(1)} %get-tuple-element.11.refs_0_), channel_id=1, source_target_pairs={{0,1},{1,0},{2,3},{3,2},{4,5},{5,4},{6,7},{7,6},{8,9},{9,8},{10,11... | collective-permute-start | bytes 12296 | tf_op jit(solution)/shard_map/ppermute | solution.py:156
  16.4 2.6 %collective-permute-start.8 = (f32[2,512]{1,0:T(2,128)S(1)}, f32[2,512]{1,0:T(2,128)S(1)}, u32[]{:S(2)}, u32[]{:S(2)}) collective-permute-start(f32[2,512]{1,0:T(2,128)S(1)} %get-tuple-element.11.refs_0_), channel_id=1, source_target_pairs={{0,2},{1,3},{2,0},{3,1},{4,6},{5,7},{6,4},{7,5},{8,10},{9,11},{10,... | collective-permute-start | bytes 12296 | tf_op jit(solution)/shard_map/ppermute | solution.py:156
  19.0 0.2 collective-permute-start.9
  19.2 0.0 collective-permute-done.7.refs_1_
  19.2 1.7 %collective-permute-done.8.refs_2_ = f32[2,512]{1,0:T(2,128)S(1)} collective-permute-done((f32[2,512]{1,0:T(2,128)S(1)}, f32[2,512]{1,0:T(2,128)S(1)}, u32[]{:S(2)}, u32[]{:S(2)}) %collective-permute-start.8) | collective-permute-done | bytes 4128 | tf_op jit(solution)/shard_map/ppermute | solution.py:156
  20.9 3.5 %collective-permute-done.9.refs_3_ = f32[2,512]{1,0:T(2,128)S(1)} collective-permute-done((f32[2,512]{1,0:T(2,128)S(1)}, f32[2,512]{1,0:T(2,128)S(1)}, u32[]{:S(2)}, u32[]{:S(2)}) %collective-permute-start.9) | collective-permute-done | bytes 4128 | tf_op jit(solution)/shard_map/ppermute | solution.py:156
  24.4 0.0 copy-done.1
  24.4 0.6 %carry_tile.1 = (f32[4,56,128]{2,1,0:T(8,128)S(1)}, f32[4,56,128]{2,1,0:T(8,128)S(1)}) custom-call(f32[2,512]{1,0:T(2,128)S(1)} %get-tuple-element.11.refs_0_, f32[2,512]{1,0:T(2,128)S(1)} %collective-permute-done.7.refs_1_, f32[2,512]{1,0:T(2,128)S(1)} %collective-permute-done.8.refs_2_, f32[2,512]{1,0:T(2,128)S(1)} %collective-permute-done.9.refs_3_, ...), custom_call_target="tpu_custom_call" | custom-call | tf_op jit(solution)/shard_map/carry_tile/pallas_call | solution.py:217
  24.9 0.1 collective-permute-start.10
  25.0 1.3 %collective-permute-done.10.given_ref = f32[4,56,128]{2,1,0:T(8,128)S(1)} collective-permute-done((f32[4,56,128]{2,1,0:T(8,128)S(1)}, f32[4,56,128]{2,1,0:T(8,128)S(1)}, u32[]{:S(2)}, u32[]{:S(2)}) %collective-permute-start.10) | collective-permute-done | bytes 114720 | tf_op jit(solution)/shard_map/ppermute | solution.py:156
  26.3 0.6 %collective-permute-start.11 = (f32[56,128]{1,0:T(8,128)S(1)}, f32[56,128]{1,0:T(8,128)S(1)}, u32[]{:S(2)}, u32[]{:S(2)}) collective-permute-start(f32[56,128]{1,0:T(8,128)S(1)} %get-tuple-element.17), channel_id=1, source_target_pairs={{0,8},{4,12},{8,0},{12,4},{16,24},{20,28},{24,16},{28,20},{1,9},{5... | collective-permute-start | bytes 86024 | tf_op jit(solution)/shard_map/ppermute | solution.py:156
  26.9 0.8 %collective-permute-start.12 = (f32[56,128]{1,0:T(8,128)S(1)}, f32[56,128]{1,0:T(8,128)S(1)}, u32[]{:S(2)}, u32[]{:S(2)}) collective-permute-start(f32[56,128]{1,0:T(8,128)S(1)} %get-tuple-element.18), channel_id=1, source_target_pairs={{0,16},{4,20},{8,24},{12,28},{16,0},{20,4},{24,8},{28,12},{1,17},{... | collective-permute-start | bytes 86024 | tf_op jit(solution)/shard_map/ppermute | solution.py:156
  27.7 2.2 %collective-permute-start.13 = (f32[56,128]{1,0:T(8,128)S(1)}, f32[56,128]{1,0:T(8,128)S(1)}, u32[]{:S(2)}, u32[]{:S(2)}) collective-permute-start(f32[56,128]{1,0:T(8,128)S(1)} %get-tuple-element.19), channel_id=1, source_target_pairs={{0,24},{4,28},{8,16},{12,20},{16,8},{20,12},{24,0},{28,4},{1,25},{... | collective-permute-start | bytes 86024 | tf_op jit(solution)/shard_map/ppermute | solution.py:156
  29.9 0.4 collective-permute-done.11.refs_1_
  30.3 0.5 %collective-permute-done.12.refs_2_ = f32[56,128]{1,0:T(8,128)S(1)} collective-permute-done((f32[56,128]{1,0:T(8,128)S(1)}, f32[56,128]{1,0:T(8,128)S(1)}, u32[]{:S(2)}, u32[]{:S(2)}) %collective-permute-start.12) | collective-permute-done | bytes 28704 | tf_op jit(solution)/shard_map/ppermute | solution.py:156
  30.8 1.7 %collective-permute-done.13.refs_3_ = f32[56,128]{1,0:T(8,128)S(1)} collective-permute-done((f32[56,128]{1,0:T(8,128)S(1)}, f32[56,128]{1,0:T(8,128)S(1)}, u32[]{:S(2)}, u32[]{:S(2)}) %collective-permute-start.13) | collective-permute-done | bytes 28704 | tf_op jit(solution)/shard_map/ppermute | solution.py:156
  32.5 0.1 collective-permute-start.14
  32.6 0.7 %collective-permute-start.15 = (f32[56,128]{1,0:T(8,128)S(1)}, f32[56,128]{1,0:T(8,128)S(1)}, u32[]{:S(2)}, u32[]{:S(2)}) collective-permute-start(f32[56,128]{1,0:T(8,128)S(1)} %emit_block.1.refs_1_), channel_id=1, source_target_pairs={{0,2},{1,3},{2,0},{3,1},{4,6},{5,7},{6,4},{7,5},{8,10},{9,11},{10,... | collective-permute-start | bytes 86024 | tf_op jit(solution)/shard_map/ppermute | solution.py:156
  33.3 3.7 %collective-permute-start.16 = (f32[56,128]{1,0:T(8,128)S(1)}, f32[56,128]{1,0:T(8,128)S(1)}, u32[]{:S(2)}, u32[]{:S(2)}) collective-permute-start(f32[56,128]{1,0:T(8,128)S(1)} %emit_block.1.refs_1_), channel_id=1, source_target_pairs={{0,3},{1,2},{2,1},{3,0},{4,7},{5,6},{6,5},{7,4},{8,11},{9,10},{10,... | collective-permute-start | bytes 86024 | tf_op jit(solution)/shard_map/ppermute | solution.py:156
  37.0 0.0 collective-permute-done.14.refs_2_
  37.0 0.5 %collective-permute-done.15.refs_3_ = f32[56,128]{1,0:T(8,128)S(1)} collective-permute-done((f32[56,128]{1,0:T(8,128)S(1)}, f32[56,128]{1,0:T(8,128)S(1)}, u32[]{:S(2)}, u32[]{:S(2)}) %collective-permute-start.15) | collective-permute-done | bytes 28704 | tf_op jit(solution)/shard_map/ppermute | solution.py:156
  37.4 1.7 %collective-permute-done.16.refs_4_ = f32[56,128]{1,0:T(8,128)S(1)} collective-permute-done((f32[56,128]{1,0:T(8,128)S(1)}, f32[56,128]{1,0:T(8,128)S(1)}, u32[]{:S(2)}, u32[]{:S(2)}) %collective-permute-start.16) | collective-permute-done | bytes 28704 | tf_op jit(solution)/shard_map/ppermute | solution.py:156
  39.1 0.7 %finish.1 = (f32[48,512]{1,0:T(8,128)}, f32[48]{0:T(128)}) custom-call(s32[1]{0:T(128)} %bitcast.refs_0_, f32[56,128]{1,0:T(8,128)S(1)} %emit_block.1.refs_1_, f32[56,128]{1,0:T(8,128)S(1)} %collective-permute-done.14.refs_2_, f32[56,128]{1,0:T(8,128)S(1)} %collective-permute-done.15.refs_3_, f32[56,128]{1,0:T(8,128)S(1)} %collective-permute-done.16.refs_4_), custom_call_target="tpu_custom_call" | custom-call | tf_op jit(solution)/shard_map/finish/pallas_call | solution.py:255
  (2 shorter events, 0.0 us)
Async XLA Ops:
  0.6 13.1 %copy-start = (bf16[512,256]{1,0:T(8,128)(2,1)S(1)}, bf16[512,256]{1,0:T(8,128)(2,1)}, u32[]{:S(2)}) copy-start(bf16[512,256]{1,0:T(8,128)(2,1)} %src_ref.1) | copy-start | bytes 786436
  0.6 23.7 %copy-start.1 = (f32[48,512]{1,0:T(8,128)S(1)}, f32[48,512]{1,0:T(8,128)}, u32[]{:S(2)}) copy-start(f32[48,512]{1,0:T(8,128)} %refs_4_.1) | copy-start | bytes 294916
  2.7 5.6 %collective-permute-start = (bf16[304,128]{1,0:T(8,128)(2,1)S(1)}, bf16[304,128]{1,0:T(8,128)(2,1)S(1)}, u32[]{:S(2)}, u32[]{:S(2)}) collective-permute-start(bf16[304,128]{1,0:T(8,128)(2,1)S(1)} %pick_rows.1.refs_0_.refs_7_.own_ref), channel_id=1, source_target_pairs={{0,8},{4,12},{8,0},{12,4},{16,24},{20,28},{24,16},{28,20},{1,9},{5... | collective-permute-start | bytes 233480 | tf_op jit(solution)/shard_map/ppermute | solution.py:156
  5.7 5.2 %collective-permute-start.1 = (bf16[304,128]{1,0:T(8,128)(2,1)S(1)}, bf16[304,128]{1,0:T(8,128)(2,1)S(1)}, u32[]{:S(2)}, u32[]{:S(2)}) collective-permute-start(bf16[304,128]{1,0:T(8,128)(2,1)S(1)} %pick_rows.1.refs_0_.refs_7_.own_ref), channel_id=1, source_target_pairs={{0,16},{4,20},{8,24},{12,28},{16,0},{20,4},{24,8},{28,12},{1,17},{... | collective-permute-start | bytes 233480 | tf_op jit(solution)/shard_map/ppermute | solution.py:156
  7.2 5.3 %collective-permute-start.2 = (bf16[304,128]{1,0:T(8,128)(2,1)S(1)}, bf16[304,128]{1,0:T(8,128)(2,1)S(1)}, u32[]{:S(2)}, u32[]{:S(2)}) collective-permute-start(bf16[304,128]{1,0:T(8,128)(2,1)S(1)} %pick_rows.1.refs_0_.refs_7_.own_ref), channel_id=1, source_target_pairs={{0,24},{4,28},{8,16},{12,20},{16,8},{20,12},{24,0},{28,4},{1,25},{... | collective-permute-start | bytes 233480 | tf_op jit(solution)/shard_map/ppermute | solution.py:156
  7.2 5.3 %collective-permute-start.3 = (bf16[304,128]{1,0:T(8,128)(2,1)S(1)}, bf16[304,128]{1,0:T(8,128)(2,1)S(1)}, u32[]{:S(2)}, u32[]{:S(2)}) collective-permute-start(bf16[304,128]{1,0:T(8,128)(2,1)S(1)} %pick_rows.1.refs_0_.refs_7_.own_ref), channel_id=1, source_target_pairs={{0,4},{4,0},{8,12},{12,8},{16,20},{20,16},{24,28},{28,24},{1,5},{5... | collective-permute-start | bytes 233480 | tf_op jit(solution)/shard_map/ppermute | solution.py:156
  8.3 4.2 %collective-permute-start.4 = (bf16[304,128]{1,0:T(8,128)(2,1)S(1)}, bf16[304,128]{1,0:T(8,128)(2,1)S(1)}, u32[]{:S(2)}, u32[]{:S(2)}) collective-permute-start(bf16[304,128]{1,0:T(8,128)(2,1)S(1)} %collective-permute-done.refs_1_.refs_8_), channel_id=1, source_target_pairs={{0,4},{4,0},{8,12},{12,8},{16,20},{20,16},{24,28},{28,24},{1,5},{5... | collective-permute-start | bytes 233480 | tf_op jit(solution)/shard_map/ppermute | solution.py:156
  10.9 1.6 %collective-permute-start.5 = (bf16[304,128]{1,0:T(8,128)(2,1)S(1)}, bf16[304,128]{1,0:T(8,128)(2,1)S(1)}, u32[]{:S(2)}, u32[]{:S(2)}) collective-permute-start(bf16[304,128]{1,0:T(8,128)(2,1)S(1)} %collective-permute-done.1.refs_2_.refs_9_), channel_id=1, source_target_pairs={{0,4},{4,0},{8,12},{12,8},{16,20},{20,16},{24,28},{28,24},{1,5},{5... | collective-permute-start | bytes 233480 | tf_op jit(solution)/shard_map/ppermute | solution.py:156
  12.5 1.3 %collective-permute-start.6 = (bf16[304,128]{1,0:T(8,128)(2,1)S(1)}, bf16[304,128]{1,0:T(8,128)(2,1)S(1)}, u32[]{:S(2)}, u32[]{:S(2)}) collective-permute-start(bf16[304,128]{1,0:T(8,128)(2,1)S(1)} %collective-permute-done.2.refs_3_.refs_10_), channel_id=1, source_target_pairs={{0,4},{4,0},{8,12},{12,8},{16,20},{20,16},{24,28},{28,24},{1,5},{5... | collective-permute-start | bytes 233480 | tf_op jit(solution)/shard_map/ppermute | solution.py:156
  14.7 4.5 %collective-permute-start.7 = (f32[2,512]{1,0:T(2,128)S(1)}, f32[2,512]{1,0:T(2,128)S(1)}, u32[]{:S(2)}, u32[]{:S(2)}) collective-permute-start(f32[2,512]{1,0:T(2,128)S(1)} %get-tuple-element.11.refs_0_), channel_id=1, source_target_pairs={{0,1},{1,0},{2,3},{3,2},{4,5},{5,4},{6,7},{7,6},{8,9},{9,8},{10,11... | collective-permute-start | bytes 12296 | tf_op jit(solution)/shard_map/ppermute | solution.py:156
  16.4 4.5 %collective-permute-start.8 = (f32[2,512]{1,0:T(2,128)S(1)}, f32[2,512]{1,0:T(2,128)S(1)}, u32[]{:S(2)}, u32[]{:S(2)}) collective-permute-start(f32[2,512]{1,0:T(2,128)S(1)} %get-tuple-element.11.refs_0_), channel_id=1, source_target_pairs={{0,2},{1,3},{2,0},{3,1},{4,6},{5,7},{6,4},{7,5},{8,10},{9,11},{10,... | collective-permute-start | bytes 12296 | tf_op jit(solution)/shard_map/ppermute | solution.py:156
  19.0 5.4 %collective-permute-start.9 = (f32[2,512]{1,0:T(2,128)S(1)}, f32[2,512]{1,0:T(2,128)S(1)}, u32[]{:S(2)}, u32[]{:S(2)}) collective-permute-start(f32[2,512]{1,0:T(2,128)S(1)} %get-tuple-element.11.refs_0_), channel_id=1, source_target_pairs={{0,3},{1,2},{2,1},{3,0},{4,7},{5,6},{6,5},{7,4},{8,11},{9,10},{10,... | collective-permute-start | bytes 12296 | tf_op jit(solution)/shard_map/ppermute | solution.py:156
  24.9 1.4 %collective-permute-start.10 = (f32[4,56,128]{2,1,0:T(8,128)S(1)}, f32[4,56,128]{2,1,0:T(8,128)S(1)}, u32[]{:S(2)}, u32[]{:S(2)}) collective-permute-start(f32[4,56,128]{2,1,0:T(8,128)S(1)} %get-tuple-element.15), channel_id=1, source_target_pairs={{0,4},{4,0},{8,12},{12,8},{16,20},{20,16},{24,28},{28,24},{1,5},{5... | collective-permute-start | bytes 344072 | tf_op jit(solution)/shard_map/ppermute | solution.py:156
  26.3 3.9 %collective-permute-start.11 = (f32[56,128]{1,0:T(8,128)S(1)}, f32[56,128]{1,0:T(8,128)S(1)}, u32[]{:S(2)}, u32[]{:S(2)}) collective-permute-start(f32[56,128]{1,0:T(8,128)S(1)} %get-tuple-element.17), channel_id=1, source_target_pairs={{0,8},{4,12},{8,0},{12,4},{16,24},{20,28},{24,16},{28,20},{1,9},{5... | collective-permute-start | bytes 86024 | tf_op jit(solution)/shard_map/ppermute | solution.py:156
  26.9 3.9 %collective-permute-start.12 = (f32[56,128]{1,0:T(8,128)S(1)}, f32[56,128]{1,0:T(8,128)S(1)}, u32[]{:S(2)}, u32[]{:S(2)}) collective-permute-start(f32[56,128]{1,0:T(8,128)S(1)} %get-tuple-element.18), channel_id=1, source_target_pairs={{0,16},{4,20},{8,24},{12,28},{16,0},{20,4},{24,8},{28,12},{1,17},{... | collective-permute-start | bytes 86024 | tf_op jit(solution)/shard_map/ppermute | solution.py:156
  27.7 4.8 %collective-permute-start.13 = (f32[56,128]{1,0:T(8,128)S(1)}, f32[56,128]{1,0:T(8,128)S(1)}, u32[]{:S(2)}, u32[]{:S(2)}) collective-permute-start(f32[56,128]{1,0:T(8,128)S(1)} %get-tuple-element.19), channel_id=1, source_target_pairs={{0,24},{4,28},{8,16},{12,20},{16,8},{20,12},{24,0},{28,4},{1,25},{... | collective-permute-start | bytes 86024 | tf_op jit(solution)/shard_map/ppermute | solution.py:156
  32.5 4.5 %collective-permute-start.14 = (f32[56,128]{1,0:T(8,128)S(1)}, f32[56,128]{1,0:T(8,128)S(1)}, u32[]{:S(2)}, u32[]{:S(2)}) collective-permute-start(f32[56,128]{1,0:T(8,128)S(1)} %emit_block.1.refs_1_), channel_id=1, source_target_pairs={{0,1},{1,0},{2,3},{3,2},{4,5},{5,4},{6,7},{7,6},{8,9},{9,8},{10,11... | collective-permute-start | bytes 86024 | tf_op jit(solution)/shard_map/ppermute | solution.py:156
  32.6 4.8 %collective-permute-start.15 = (f32[56,128]{1,0:T(8,128)S(1)}, f32[56,128]{1,0:T(8,128)S(1)}, u32[]{:S(2)}, u32[]{:S(2)}) collective-permute-start(f32[56,128]{1,0:T(8,128)S(1)} %emit_block.1.refs_1_), channel_id=1, source_target_pairs={{0,2},{1,3},{2,0},{3,1},{4,6},{5,7},{6,4},{7,5},{8,10},{9,11},{10,... | collective-permute-start | bytes 86024 | tf_op jit(solution)/shard_map/ppermute | solution.py:156
  33.3 5.8 %collective-permute-start.16 = (f32[56,128]{1,0:T(8,128)S(1)}, f32[56,128]{1,0:T(8,128)S(1)}, u32[]{:S(2)}, u32[]{:S(2)}) collective-permute-start(f32[56,128]{1,0:T(8,128)S(1)} %emit_block.1.refs_1_), channel_id=1, source_target_pairs={{0,3},{1,2},{2,1},{3,0},{4,7},{5,6},{6,5},{7,4},{8,11},{9,10},{10,... | collective-permute-start | bytes 86024 | tf_op jit(solution)/shard_map/ppermute | solution.py:156

commit v4 on v3

v4 whole, which is shorter than its diff:
```python
import functools
import math

import jax
import jax.numpy as jnp
from jax import lax
from jax.experimental import pallas as pl
from jax.experimental.pallas import tpu as pltpu
from jax.sharding import PartitionSpec as P

VMEM = pltpu.MemorySpace.VMEM
SMEM = pltpu.MemorySpace.SMEM
HBM = pltpu.MemorySpace.HBM
TAIL = 8
CHUNK = 8


def room(mebibytes):
    return pltpu.CompilerParams(vmem_limit_bytes=mebibytes << 20)


def block_specs(steps, shapes):
    if steps == 1:
        return [pl.BlockSpec(memory_space=VMEM) for _ in shapes]
    return [
        pl.BlockSpec(shape, lambda s, n=len(shape), moves=moves: (s if moves else 0,) + (0,) * (n - 1))
        for shape, moves in shapes
    ]


def pick_rows(tokens_ref, table_ref, dst_ref, out_ref, ids, chunks, picked, ids_sem, dst_sem, sem):
    seqs = picked.shape[0]
    depth = dst_ref.shape[0]
    ids_copy = pltpu.make_async_copy(tokens_ref, ids, ids_sem)
    dst_copy = pltpu.make_async_copy(dst_ref, out_ref.at[pl.ds(0, depth)], dst_sem)
    ids_copy.start()
    dst_copy.start()
    ids_copy.wait()
    for b in range(seqs):
        first = pl.multiple_of((ids[b] // CHUNK) * CHUNK, CHUNK)
        pltpu.make_async_copy(
            table_ref.at[pl.ds(first, CHUNK)], chunks.at[pl.ds(b * CHUNK, CHUNK)], sem
        ).start()
    pltpu.make_async_copy(table_ref.at[pl.ds(0, seqs * CHUNK)], chunks, sem).wait()
    rows = lax.broadcasted_iota(jnp.int32, (CHUNK, chunks.shape[1]), 0)
    for b in range(seqs):
        chunk = chunks[b * CHUNK : (b + 1) * CHUNK].astype(jnp.float32)
        kept = jnp.where(rows == ids[b] % CHUNK, chunk, 0.0)
        picked[b : b + 1] = jnp.sum(kept, axis=0, keepdims=True)
    out_ref[depth:] = picked[...].astype(out_ref.dtype)
    dst_copy.wait()


def merge(first, second):
    peak = jnp.maximum(first[0], second[0])
    return peak, first[1] * jnp.exp(first[0] - peak) + second[1] * jnp.exp(second[0] - peak)


def softmax_tile(steps, per_step, n_src, n_dst, *refs):
    src_refs, dst_refs = refs[:n_src], pieces(refs[n_src : n_src + n_dst])
    earlier = refs[n_src + n_dst : -3]
    expo_ref, peak_ref, stat_ref = refs[-3:]
    step = pl.program_id(0) if steps > 1 else 0
    depth = src_refs[0].shape[1]
    for h, src_ref in enumerate(src_refs):
        lanes = slice(h * src_ref.shape[0], (h + 1) * src_ref.shape[0])
        stats = []
        for q in range(per_step):
            logits = lax.dot_general(
                dst_refs[q][:depth], src_ref[...], (((0,), (1,)), ((), ())), preferred_element_type=jnp.float32
            )
            peak = jnp.max(logits, axis=0, keepdims=True)
            shifted = jnp.exp(logits - peak)
            peak_ref[pl.ds(step * per_step + q, 1), lanes] = peak
            stats.append((peak, jnp.sum(shifted, axis=0, keepdims=True)))
            expo_ref[q, :, lanes] = shifted.astype(expo_ref.dtype)
        local_peak = functools.reduce(jnp.maximum, [p for p, _ in stats])
        local_total = functools.reduce(jnp.add, [t * jnp.exp(p - local_peak) for p, t in stats])

        def put(pair, lanes=lanes):
            stat_ref[0:1, lanes], stat_ref[1:2, lanes] = pair

        if earlier:
            put(merge((local_peak, local_total), (earlier[0][0:1, lanes], earlier[0][1:2, lanes])))
        elif steps == 1:
            put((local_peak, local_total))
        else:

            @pl.when(step == 0)
            def _(put=put, pair=(local_peak, local_total)):
                put(pair)

            @pl.when(step > 0)
            def _(put=put, pair=(local_peak, local_total), lanes=lanes):
                put(merge((stat_ref[0:1, lanes], stat_ref[1:2, lanes]), pair))


def carry_tile(steps, per_step, n_stats, n_src, n_tiles, n_out, *refs):
    stat_refs, refs = refs[:n_stats], refs[n_stats:]
    alpha_refs, refs = refs[:n_src], refs[n_src:]
    expo_refs, refs = refs[:n_tiles], refs[n_tiles:]
    peak_refs, refs = refs[:n_tiles], refs[n_tiles:]
    emit_refs, out_refs, spread = pieces(refs[: -1 - n_out]), refs[-1 - n_out : -1], refs[-1]
    step = pl.program_id(0) if steps > 1 else 0
    seqs, sources = alpha_refs[0].shape
    each = per_step // n_tiles

    @pl.when(step == 0)
    def _():
        spread[...] = jnp.zeros_like(spread)

    scales = []
    for h in range(n_src):
        lanes = slice(h * sources, (h + 1) * sources)
        row_peak = functools.reduce(jnp.maximum, [s[0:1, lanes] for s in stat_refs])
        scales.append((lanes, row_peak, tree_sum([s[1:2, lanes] * jnp.exp(s[0:1, lanes] - row_peak) for s in stat_refs])))
    shares = []
    for t in range(n_tiles):
        terms = []
        for i in range(each):
            slot = step * each + i
            product = []
            for alpha_ref, (lanes, row_peak, row_total) in zip(alpha_refs, scales, strict=True):
                row_scale = jnp.exp(peak_refs[t][pl.ds(slot, 1), lanes] - row_peak) / row_total
                weights = (alpha_ref[...] * row_scale).astype(jnp.bfloat16)
                product.append(
                    lax.dot_general(
                        weights,
                        expo_refs[t][i, :, lanes],
                        (((1,), (1,)), ((), ())),
                        preferred_element_type=jnp.float32,
                    )
                )
            product = tree_sum(product)
            if len(out_refs[0].shape) == 3:
                out_refs[0][slot, :seqs] = product
            elif t == 0:
                out_refs[i][:seqs] = product
            emit_ref = emit_refs[t * each + i]
            terms.append(product * emit_ref[emit_ref.shape[0] - seqs :].astype(jnp.float32))
        shares.append(functools.reduce(jnp.add, terms))
    spread[:seqs] += tree_sum(shares)

    @pl.when(step == steps - 1)
    def _():
        share = jnp.sum(spread[...].T, axis=0, keepdims=True)
        tail = jnp.broadcast_to(share, (TAIL, share.shape[1]))
        for out_ref in out_refs:
            if len(out_ref.shape) == 3:
                for group in range(out_ref.shape[0]):
                    out_ref[group, seqs:] = tail
            else:
                out_ref[seqs:] = tail


def pieces(refs):
    views = [[r.at[i] for i in range(r.shape[0])] if len(r.shape) == 3 else [r] for r in refs]
    return sum(views, [])


def stack(*refs):
    for i, ref in enumerate(refs[:-1]):
        refs[-1][i] = ref[...]


def tree_sum(terms):
    while len(terms) > 1:
        terms = [a + b for a, b in zip(terms[::2], terms[1::2], strict=True)]
    return terms[0]


def emit_block(own_ref, *refs):
    parts_refs, out_ref = refs[:-1], refs[-1]
    seqs = out_ref.shape[0] - TAIL
    if len(parts_refs) > 1:
        sums = tree_sum([r[...] for r in parts_refs])
    else:
        sums = jnp.sum(parts_refs[0][...], axis=0)
    out_ref[:seqs] = sums[:seqs] * own_ref[own_ref.shape[0] - seqs :].astype(jnp.float32)
    out_ref[seqs:] = sums[seqs:]


def finish(states, n_blocks, *refs):
    place_ref = refs[0]
    block_refs = refs[1 : 1 + n_blocks]
    alpha_ref, log_ref = refs[1 + n_blocks :]
    seqs, cols = alpha_ref.shape[0], block_refs[0].shape[1]
    total = tree_sum([b[seqs:] for b in block_refs])
    log_ref[...] = jnp.log(total[0, :seqs])
    scale = (states / jnp.broadcast_to(total[0:1], (cols, cols)).T)[:seqs]
    for k in range(n_blocks):
        start = pl.multiple_of((place_ref[0] ^ (0, 3, 2, 1)[k]) * cols, cols)
        alpha_ref[:, pl.ds(start, cols)] = block_refs[k][:seqs] * scale


def hop(x, axis, count, k):
    return lax.ppermute(x, axis, [(i, i ^ k) for i in range(count)])


def swap(x, axis, count):
    return [x] + [hop(x, axis, count, k) for k in (3, 2, 1)]


def on_device(alpha_prev, tokens, src_emb, dst_emb, emission):
    rows = lax.axis_size("row")
    cols = lax.axis_size("col")
    seqs, sources = alpha_prev.shape
    depth, group = dst_emb.shape
    f32 = jnp.float32

    packed = pl.pallas_call(
        pick_rows,
        out_shape=jax.ShapeDtypeStruct((depth + seqs, group), jnp.bfloat16),
        in_specs=[pl.BlockSpec(memory_space=HBM)] * 3,
        out_specs=pl.BlockSpec(memory_space=VMEM),
        scratch_shapes=[
            pltpu.SMEM((seqs,), jnp.int32),
            pltpu.VMEM((seqs * CHUNK, group), jnp.bfloat16),
            pltpu.VMEM((seqs, group), f32),
            pltpu.SemaphoreType.DMA,
            pltpu.SemaphoreType.DMA,
            pltpu.SemaphoreType.DMA,
        ],
        name="pick_rows",
        compiler_params=room(8),
    )(*[pltpu.with_memory_space_constraint(x, HBM) for x in (tokens, emission, dst_emb)])

    paired = rows == 8
    if paired:
        half = rows // 2
        srcs = [src_emb, hop(src_emb, "row", rows, 1)]
        alphas = [alpha_prev, hop(alpha_prev, "row", rows, 1)]
        ready = lax.optimization_barrier((packed, srcs[1]))
        srcs[1] = ready[1]
        like = [packed] + [hop(ready[0], "row", rows, 2 * m) for m in range(1, half)]
        pile = pl.pallas_call(
            stack,
            out_shape=jax.ShapeDtypeStruct((half,) + packed.shape, packed.dtype),
            in_specs=[pl.BlockSpec(memory_space=VMEM)] * half,
            out_specs=pl.BlockSpec(memory_space=VMEM),
            name="stack",
            compiler_params=room(8),
        )(*like)
        arrived = [like, [hop(pile, "row", rows, 1)]]
        sums_shape = (jax.ShapeDtypeStruct((seqs + TAIL, group), f32),) * half
        sums_block = [((seqs + TAIL, group), False)] * half
    else:
        srcs, alphas = [src_emb], [alpha_prev]
        arrived = [[lax.all_gather(packed, "row", axis=0)]]
        sums_shape = (jax.ShapeDtypeStruct((rows, seqs + TAIL, group), f32),)
        sums_block = [((rows, seqs + TAIL, group), False)]

    halves, tiles = len(srcs), len(arrived)
    wide = halves * sources
    tile_rows = rows // tiles
    per_step = math.gcd(tile_rows, 8)
    steps = tile_rows // per_step
    grid = (steps,) if steps > 1 else ()
    dst_block = ((per_step, depth + seqs, group), True)
    expo_block = ((per_step, group, wide), True)
    peak_block = ((tile_rows, wide), False)
    stat_block = ((2, wide), False)
    expos, peaks, stats = [], [], []
    for blocks in arrived:
        expo, peak, stat = pl.pallas_call(
            functools.partial(softmax_tile, steps, per_step, halves, len(blocks)),
            out_shape=(
                jax.ShapeDtypeStruct((tile_rows, group, wide), jnp.bfloat16),
                jax.ShapeDtypeStruct((tile_rows, wide), f32),
                jax.ShapeDtypeStruct((2, wide), f32),
            ),
            grid=grid,
            in_specs=block_specs(
                steps,
                [((sources, depth), False)] * halves + [dst_block] * len(blocks) + [stat_block] * len(stats),
            ),
            out_specs=block_specs(steps, [expo_block, peak_block, stat_block]),
            name="softmax_tile",
            compiler_params=room(16),
        )(*srcs, *blocks, *stats)
        expos.append(expo)
        peaks.append(peak)
        stats = [stat]

    flat = sum(arrived, [])
    partial = pl.pallas_call(
        functools.partial(carry_tile, steps, per_step * tiles, cols, halves, tiles, len(sums_shape)),
        out_shape=sums_shape,
        grid=grid,
        in_specs=block_specs(
            steps,
            [stat_block] * cols
            + [((seqs, sources), False)] * halves
            + [expo_block] * tiles
            + [peak_block] * tiles
            + [dst_block] * len(flat),
        ),
        out_specs=block_specs(steps, sums_block),
        scratch_shapes=[pltpu.VMEM((group, group), f32)],
        name="carry_tile",
        compiler_params=room(16),
    )(*swap(stats[0], "col", cols), *alphas, *expos, *peaks, *flat)

    if paired:
        parts = [partial[0]] + [hop(partial[m], "row", rows, 2 * m) for m in range(1, half)]
    else:
        parts = [lax.all_to_all(partial[0], "row", 0, 0)]
    block = pl.pallas_call(
        emit_block,
        out_shape=jax.ShapeDtypeStruct((seqs + TAIL, group), f32),
        in_specs=[pl.BlockSpec(memory_space=VMEM)] * (1 + len(parts)),
        out_specs=pl.BlockSpec(memory_space=VMEM),
        name="emit_block",
        compiler_params=room(8),
    )(packed, *parts)

    blocks = swap(block, "col", cols)
    place = lax.axis_index("col").astype(jnp.int32).reshape(1)
    return pl.pallas_call(
        functools.partial(finish, float(group * rows * cols), cols),
        out_shape=(jax.ShapeDtypeStruct((seqs, group * cols), f32), jax.ShapeDtypeStruct((seqs,), f32)),
        in_specs=[pl.BlockSpec(memory_space=SMEM)] + [pl.BlockSpec(memory_space=VMEM)] * cols,
        out_specs=(pl.BlockSpec(memory_space=VMEM), pl.BlockSpec(memory_space=VMEM)),
        name="finish",
        compiler_params=room(8),
    )(place, *blocks)


def solution(mesh):
    placed = (P(None, "row"), P(), P("row", None), P(None, ("row", "col")), P(None, ("row", "col")))
    return jax.shard_map(
        on_device, mesh=mesh, in_specs=placed, out_specs=(P(None, "row"), P()), check_vma=False
    )
```

time: 40 us -> 37.9 us (0.948)
  waiting for transfers between devices: 17.8 us -> 13.7 us
  Pallas kernels: 4.3 us -> 5.47 us
  starting transfers between devices: 17.1 us -> 17.8 us
    ppermute x17 -> x15, waiting for transfers between devices: 17.8 us -> 13.7 us  [hop(): return lax.ppermute(x, axis, [(i, i ^ k) for i in range(count)])]
    pallas_call x3 -> x4, Pallas kernels: 1.54 us -> 2.85 us  [the longest x2 1.89 us: on_device(): pl.pallas_call(functools.partial(softmax_tile, steps, per_step, halves, l...]
    ppermute x17 -> x15, starting transfers between devices: 17.1 us -> 17.8 us  [hop(): return lax.ppermute(x, axis, [(i, i ^ k) for i in range(count)])]
  transfers between devices with their start and end apart: 17 -> 15, of which waited for: 12 -> 12; matrix products, arithmetic and copies ran while one was open for 0% -> 0% of each run, Pallas kernels for 0% -> 10%
where the time goes in v4:
time: 37.9 us; the launch traced here: 37.7 us
  starting transfers between devices  17.8 us (47%)
  waiting for transfers between devices  13.7 us (36%)
  Pallas kernels  5.47 us (14%)
  between operations  0.7 us (2%)
    ppermute x15, starting transfers between devices, hop(): return lax.ppermute(x, axis, [(i, i ^ k) for i in range(count)])  17.8 us
    ppermute x15, waiting for transfers between devices, hop(): return lax.ppermute(x, axis, [(i, i ^ k) for i in range(count)])  13.7 us
    pallas_call x2, Pallas kernels, on_device(): pl.pallas_call(functools.partial(softmax_tile, steps, per_step, halves, l...  1.89 us
    pallas_call x1, Pallas kernels, on_device(): pl.pallas_call(pick_rows, out_shape=jax.ShapeDtypeStruct((depth + seqs, g...  1.88 us
    pallas_call x1, Pallas kernels, on_device(): pl.pallas_call(functools.partial(carry_tile, steps, per_step * tiles, col...  0.94 us
  transfers between devices with their start and end apart: 15, of which 12 were waited for; matrix products, arithmetic and copies ran while one was open for 0% of the time, Pallas kernels for 10%

profile of v4, /device:TPU:0, one launch (start us, length us, event | category | flops | bytes accessed | tf_op | source)
XLA Modules:
  0.0 37.7 jit_solution(70289791138778795)
XLA Ops:
  0.6 0.0 copy-start
  0.6 0.0 copy-start.1
  0.7 0.5 %collective-permute-start = (bf16[512,256]{1,0:T(8,128)(2,1)}, bf16[512,256]{1,0:T(8,128)(2,1)S(1)}, u32[]{:S(2)}, u32[]{:S(2)}) collective-permute-start(bf16[512,256]{1,0:T(8,128)(2,1)} %refs_0_.3), channel_id=1, source_target_pairs={{0,4},{4,0},{8,12},{12,8},{16,20},{20,16},{24,28},{28,24},{1,5},{5... | collective-permute-start | bytes 786440 | tf_op jit(solution)/shard_map/ppermute | solution.py:197
  1.2 1.9 %pick_rows.1.refs_0_.refs_2_.refs_10_.own_ref = bf16[304,128]{1,0:T(8,128)(2,1)S(1)} custom-call(s32[48]{0:T(128)} %tokens_ref.1, bf16[16640,128]{1,0:T(8,128)(2,1)} %table_ref.1, bf16[256,128]{1,0:T(8,128)(2,1)} %dst_ref.1), custom_call_target="tpu_custom_call" | custom-call | tf_op jit(solution)/shard_map/pick_rows/pallas_call | solution.py:211
  3.1 0.0 collective-permute-done.refs_1_
  3.1 2.7 %collective-permute-start.1 = (bf16[304,128]{1,0:T(8,128)(2,1)S(1)}, bf16[304,128]{1,0:T(8,128)(2,1)S(1)}, u32[]{:S(2)}, u32[]{:S(2)}) collective-permute-start(bf16[304,128]{1,0:T(8,128)(2,1)S(1)} %pick_rows.1.refs_0_.refs_2_.refs_10_.own_ref), channel_id=1, source_target_pairs={{0,8},{4,12},{8,0},{12,4},{16,24},{20,28},{24,16},{28,20},{1,9},{5... | collective-permute-start | bytes 233480 | tf_op jit(solution)/shard_map/ppermute | solution.py:197
  5.8 1.5 %collective-permute-start.2 = (bf16[304,128]{1,0:T(8,128)(2,1)S(1)}, bf16[304,128]{1,0:T(8,128)(2,1)S(1)}, u32[]{:S(2)}, u32[]{:S(2)}) collective-permute-start(bf16[304,128]{1,0:T(8,128)(2,1)S(1)} %pick_rows.1.refs_0_.refs_2_.refs_10_.own_ref), channel_id=1, source_target_pairs={{0,16},{4,20},{8,24},{12,28},{16,0},{20,4},{24,8},{28,12},{1,17},{... | collective-permute-start | bytes 233480 | tf_op jit(solution)/shard_map/ppermute | solution.py:197
  7.3 0.0 collective-permute-start.3
  7.3 1.3 %collective-permute-done.1.refs_1_.refs_3_.refs_11_ = bf16[304,128]{1,0:T(8,128)(2,1)S(1)} collective-permute-done((bf16[304,128]{1,0:T(8,128)(2,1)S(1)}, bf16[304,128]{1,0:T(8,128)(2,1)S(1)}, u32[]{:S(2)}, u32[]{:S(2)}) %collective-permute-start.1) | collective-permute-done | bytes 77856 | tf_op jit(solution)/shard_map/ppermute | solution.py:197
  8.6 2.3 %collective-permute-done.2.refs_2_.refs_4_.refs_12_ = bf16[304,128]{1,0:T(8,128)(2,1)S(1)} collective-permute-done((bf16[304,128]{1,0:T(8,128)(2,1)S(1)}, bf16[304,128]{1,0:T(8,128)(2,1)S(1)}, u32[]{:S(2)}, u32[]{:S(2)}) %collective-permute-start.2) | collective-permute-done | bytes 77856 | tf_op jit(solution)/shard_map/ppermute | solution.py:197
  10.9 1.7 %collective-permute-done.3.refs_3_.refs_5_.refs_13_ = bf16[304,128]{1,0:T(8,128)(2,1)S(1)} collective-permute-done((bf16[304,128]{1,0:T(8,128)(2,1)S(1)}, bf16[304,128]{1,0:T(8,128)(2,1)S(1)}, u32[]{:S(2)}, u32[]{:S(2)}) %collective-permute-start.3) | collective-permute-done | bytes 77856 | tf_op jit(solution)/shard_map/ppermute | solution.py:197
  12.6 0.1 collective-permute-start.4
  12.7 0.0 copy-done.1
  12.7 0.5 %collective-permute-start.8 = (f32[48,512]{1,0:T(8,128)S(1)}, f32[48,512]{1,0:T(8,128)S(1)}, u32[]{:S(2)}, u32[]{:S(2)}) collective-permute-start(f32[48,512]{1,0:T(8,128)S(1)} %copy-done.1), channel_id=1, source_target_pairs={{0,4},{4,0},{8,12},{12,8},{16,20},{20,16},{24,28},{28,24},{1,5},{5... | collective-permute-start | bytes 294920 | tf_op jit(solution)/shard_map/ppermute | solution.py:197
  13.2 0.0 copy-done
  13.2 0.9 %softmax_tile.2 = (bf16[4,128,1024]{2,1,0:T(8,128)(2,1)S(1)}, f32[4,1024]{1,0:T(4,128)S(1)}, f32[2,1024]{1,0:T(2,128)S(1)}) custom-call(bf16[512,256]{1,0:T(8,128)(2,1)S(1)} %copy-done, bf16[512,256]{1,0:T(8,128)(2,1)S(1)} %collective-permute-done.refs_1_, bf16[304,128]{1,0:T(8,128)(2,1)S(1)} %pick_rows.1.refs_0_.refs_2_.refs_10_.own_ref, ...), custom_call_target="tpu_custom_call" | custom-call | tf_op jit(solution)/shard_map/softmax_tile/pallas_call | solution.py:265
  14.1 0.2 collective-permute-done.4.refs_2_.refs_14_
  14.3 0.9 %softmax_tile.3 = (bf16[4,128,1024]{2,1,0:T(8,128)(2,1)S(1)}, f32[4,1024]{1,0:T(4,128)S(1)}, f32[2,1024]{1,0:T(2,128)S(1)}) custom-call(bf16[512,256]{1,0:T(8,128)(2,1)S(1)} %copy-done, bf16[512,256]{1,0:T(8,128)(2,1)S(1)} %collective-permute-done.refs_1_, bf16[4,304,128]{2,1,0:T(8,128)(2,1)S(1)} %collective-permute-done.4.refs_2_.refs_14_, ...), custom_call_target="tpu_custom_call" | custom-call | tf_op jit(solution)/shard_map/softmax_tile/pallas_call | solution.py:265
  15.2 3.7 %collective-permute-start.5 = (f32[2,1024]{1,0:T(2,128)S(1)}, f32[2,1024]{1,0:T(2,128)S(1)}, u32[]{:S(2)}, u32[]{:S(2)}) collective-permute-start(f32[2,1024]{1,0:T(2,128)S(1)} %get-tuple-element.17.refs_0_), channel_id=1, source_target_pairs={{0,3},{1,2},{2,1},{3,0},{4,7},{5,6},{6,5},{7,4},{8,11},{9,10},{10,... | collective-permute-start | bytes 24584 | tf_op jit(solution)/shard_map/ppermute | solution.py:197
  18.9 0.0 collective-permute-start.6
  18.9 0.8 %collective-permute-start.7 = (f32[2,1024]{1,0:T(2,128)S(1)}, f32[2,1024]{1,0:T(2,128)S(1)}, u32[]{:S(2)}, u32[]{:S(2)}) collective-permute-start(f32[2,1024]{1,0:T(2,128)S(1)} %get-tuple-element.17.refs_0_), channel_id=1, source_target_pairs={{0,1},{1,0},{2,3},{3,2},{4,5},{5,4},{6,7},{7,6},{8,9},{9,8},{10,11... | collective-permute-start | bytes 24584 | tf_op jit(solution)/shard_map/ppermute | solution.py:197
  19.7 0.0 collective-permute-done.8.refs_5_
  19.7 1.1 %collective-permute-done.5.refs_1_ = f32[2,1024]{1,0:T(2,128)S(1)} collective-permute-done((f32[2,1024]{1,0:T(2,128)S(1)}, f32[2,1024]{1,0:T(2,128)S(1)}, u32[]{:S(2)}, u32[]{:S(2)}) %collective-permute-start.5) | collective-permute-done | bytes 8224 | tf_op jit(solution)/shard_map/ppermute | solution.py:197
  20.8 2.7 %collective-permute-done.6.refs_2_ = f32[2,1024]{1,0:T(2,128)S(1)} collective-permute-done((f32[2,1024]{1,0:T(2,128)S(1)}, f32[2,1024]{1,0:T(2,128)S(1)}, u32[]{:S(2)}, u32[]{:S(2)}) %collective-permute-start.6) | collective-permute-done | bytes 8224 | tf_op jit(solution)/shard_map/ppermute | solution.py:197
  23.5 0.0 collective-permute-done.7.refs_3_
  23.5 0.9 %carry_tile.1 = (f32[56,128]{1,0:T(8,128)S(1)}, f32[56,128]{1,0:T(8,128)S(1)}, f32[56,128]{1,0:T(8,128)S(1)}, f32[56,128]{1,0:T(8,128)S(1)}) custom-call(f32[2,1024]{1,0:T(2,128)S(1)} %get-tuple-element.17.refs_0_, f32[2,1024]{1,0:T(2,128)S(1)} %collective-permute-done.5.refs_1_, f32[2,1024]{1,0:T(2,128)S(1)} %collective-permute-done.6.refs_2_, ...), custom_call_target="tpu_custom_call" | custom-call | tf_op jit(solution)/shard_map/carry_tile/pallas_call | solution.py:286
  24.4 0.8 %collective-permute-start.10 = (f32[56,128]{1,0:T(8,128)S(1)}, f32[56,128]{1,0:T(8,128)S(1)}, u32[]{:S(2)}, u32[]{:S(2)}) collective-permute-start(f32[56,128]{1,0:T(8,128)S(1)} %get-tuple-element.24), channel_id=1, source_target_pairs={{0,16},{4,20},{8,24},{12,28},{16,0},{20,4},{24,8},{28,12},{1,17},{... | collective-permute-start | bytes 86024 | tf_op jit(solution)/shard_map/ppermute | solution.py:197
  25.2 1.2 %collective-permute-start.11 = (f32[56,128]{1,0:T(8,128)S(1)}, f32[56,128]{1,0:T(8,128)S(1)}, u32[]{:S(2)}, u32[]{:S(2)}) collective-permute-start(f32[56,128]{1,0:T(8,128)S(1)} %get-tuple-element.25), channel_id=1, source_target_pairs={{0,24},{4,28},{8,16},{12,20},{16,8},{20,12},{24,0},{28,4},{1,25},{... | collective-permute-start | bytes 86024 | tf_op jit(solution)/shard_map/ppermute | solution.py:197
  26.5 1.5 %collective-permute-start.9 = (f32[56,128]{1,0:T(8,128)S(1)}, f32[56,128]{1,0:T(8,128)S(1)}, u32[]{:S(2)}, u32[]{:S(2)}) collective-permute-start(f32[56,128]{1,0:T(8,128)S(1)} %get-tuple-element.23), channel_id=1, source_target_pairs={{0,8},{4,12},{8,0},{12,4},{16,24},{20,28},{24,16},{28,20},{1,9},{5... | collective-permute-start | bytes 86024 | tf_op jit(solution)/shard_map/ppermute | solution.py:197
  28.0 0.4 %collective-permute-done.10.refs_2_ = f32[56,128]{1,0:T(8,128)S(1)} collective-permute-done((f32[56,128]{1,0:T(8,128)S(1)}, f32[56,128]{1,0:T(8,128)S(1)}, u32[]{:S(2)}, u32[]{:S(2)}) %collective-permute-start.10) | collective-permute-done | bytes 28704 | tf_op jit(solution)/shard_map/ppermute | solution.py:197
  28.3 1.7 %collective-permute-done.11.refs_3_ = f32[56,128]{1,0:T(8,128)S(1)} collective-permute-done((f32[56,128]{1,0:T(8,128)S(1)}, f32[56,128]{1,0:T(8,128)S(1)}, u32[]{:S(2)}, u32[]{:S(2)}) %collective-permute-start.11) | collective-permute-done | bytes 28704 | tf_op jit(solution)/shard_map/ppermute | solution.py:197
  30.0 0.3 collective-permute-done.9.refs_1_
  30.4 1.5 %collective-permute-start.12 = (f32[56,128]{1,0:T(8,128)S(1)}, f32[56,128]{1,0:T(8,128)S(1)}, u32[]{:S(2)}, u32[]{:S(2)}) collective-permute-start(f32[56,128]{1,0:T(8,128)S(1)} %emit_block.1.refs_1_), channel_id=1, source_target_pairs={{0,3},{1,2},{2,1},{3,0},{4,7},{5,6},{6,5},{7,4},{8,11},{9,10},{10,... | collective-permute-start | bytes 86024 | tf_op jit(solution)/shard_map/ppermute | solution.py:197
  31.9 0.6 %collective-permute-start.13 = (f32[56,128]{1,0:T(8,128)S(1)}, f32[56,128]{1,0:T(8,128)S(1)}, u32[]{:S(2)}, u32[]{:S(2)}) collective-permute-start(f32[56,128]{1,0:T(8,128)S(1)} %emit_block.1.refs_1_), channel_id=1, source_target_pairs={{0,2},{1,3},{2,0},{3,1},{4,6},{5,7},{6,4},{7,5},{8,10},{9,11},{10,... | collective-permute-start | bytes 86024 | tf_op jit(solution)/shard_map/ppermute | solution.py:197
  32.5 2.3 %collective-permute-start.14 = (f32[56,128]{1,0:T(8,128)S(1)}, f32[56,128]{1,0:T(8,128)S(1)}, u32[]{:S(2)}, u32[]{:S(2)}) collective-permute-start(f32[56,128]{1,0:T(8,128)S(1)} %emit_block.1.refs_1_), channel_id=1, source_target_pairs={{0,1},{1,0},{2,3},{3,2},{4,5},{5,4},{6,7},{7,6},{8,9},{9,8},{10,11... | collective-permute-start | bytes 86024 | tf_op jit(solution)/shard_map/ppermute | solution.py:197
  34.8 1.3 %collective-permute-done.12.refs_2_ = f32[56,128]{1,0:T(8,128)S(1)} collective-permute-done((f32[56,128]{1,0:T(8,128)S(1)}, f32[56,128]{1,0:T(8,128)S(1)}, u32[]{:S(2)}, u32[]{:S(2)}) %collective-permute-start.12) | collective-permute-done | bytes 28704 | tf_op jit(solution)/shard_map/ppermute | solution.py:197
  36.1 0.6 %collective-permute-done.13.refs_3_ = f32[56,128]{1,0:T(8,128)S(1)} collective-permute-done((f32[56,128]{1,0:T(8,128)S(1)}, f32[56,128]{1,0:T(8,128)S(1)}, u32[]{:S(2)}, u32[]{:S(2)}) %collective-permute-start.13) | collective-permute-done | bytes 28704 | tf_op jit(solution)/shard_map/ppermute | solution.py:197
  36.7 0.3 collective-permute-done.14.refs_4_
  37.0 0.7 %finish.1 = (f32[48,512]{1,0:T(8,128)}, f32[48]{0:T(128)}) custom-call(s32[1]{0:T(128)} %bitcast.refs_0_, f32[56,128]{1,0:T(8,128)S(1)} %emit_block.1.refs_1_, f32[56,128]{1,0:T(8,128)S(1)} %collective-permute-done.12.refs_2_, f32[56,128]{1,0:T(8,128)S(1)} %collective-permute-done.13.refs_3_, f32[56,128]{1,0:T(8,128)S(1)} %collective-permute-done.14.refs_4_), custom_call_target="tpu_custom_call" | custom-call | tf_op jit(solution)/shard_map/finish/pallas_call | solution.py:319
  (2 shorter events, 0.0 us)
Async XLA Ops:
  0.6 12.6 %copy-start = (bf16[512,256]{1,0:T(8,128)(2,1)S(1)}, bf16[512,256]{1,0:T(8,128)(2,1)}, u32[]{:S(2)}) copy-start(bf16[512,256]{1,0:T(8,128)(2,1)} %refs_0_.3) | copy-start | bytes 786436
  0.6 12.1 %copy-start.1 = (f32[48,512]{1,0:T(8,128)S(1)}, f32[48,512]{1,0:T(8,128)}, u32[]{:S(2)}) copy-start(f32[48,512]{1,0:T(8,128)} %refs_4_.1) | copy-start | bytes 294916
  0.7 2.4 %collective-permute-start = (bf16[512,256]{1,0:T(8,128)(2,1)}, bf16[512,256]{1,0:T(8,128)(2,1)S(1)}, u32[]{:S(2)}, u32[]{:S(2)}) collective-permute-start(bf16[512,256]{1,0:T(8,128)(2,1)} %refs_0_.3), channel_id=1, source_target_pairs={{0,4},{4,0},{8,12},{12,8},{16,20},{20,16},{24,28},{28,24},{1,5},{5... | collective-permute-start | bytes 786440 | tf_op jit(solution)/shard_map/ppermute | solution.py:197
  3.1 5.6 %collective-permute-start.1 = (bf16[304,128]{1,0:T(8,128)(2,1)S(1)}, bf16[304,128]{1,0:T(8,128)(2,1)S(1)}, u32[]{:S(2)}, u32[]{:S(2)}) collective-permute-start(bf16[304,128]{1,0:T(8,128)(2,1)S(1)} %pick_rows.1.refs_0_.refs_2_.refs_10_.own_ref), channel_id=1, source_target_pairs={{0,8},{4,12},{8,0},{12,4},{16,24},{20,28},{24,16},{28,20},{1,9},{5... | collective-permute-start | bytes 233480 | tf_op jit(solution)/shard_map/ppermute | solution.py:197
  5.8 5.1 %collective-permute-start.2 = (bf16[304,128]{1,0:T(8,128)(2,1)S(1)}, bf16[304,128]{1,0:T(8,128)(2,1)S(1)}, u32[]{:S(2)}, u32[]{:S(2)}) collective-permute-start(bf16[304,128]{1,0:T(8,128)(2,1)S(1)} %pick_rows.1.refs_0_.refs_2_.refs_10_.own_ref), channel_id=1, source_target_pairs={{0,16},{4,20},{8,24},{12,28},{16,0},{20,4},{24,8},{28,12},{1,17},{... | collective-permute-start | bytes 233480 | tf_op jit(solution)/shard_map/ppermute | solution.py:197
  7.3 5.3 %collective-permute-start.3 = (bf16[304,128]{1,0:T(8,128)(2,1)S(1)}, bf16[304,128]{1,0:T(8,128)(2,1)S(1)}, u32[]{:S(2)}, u32[]{:S(2)}) collective-permute-start(bf16[304,128]{1,0:T(8,128)(2,1)S(1)} %pick_rows.1.refs_0_.refs_2_.refs_10_.own_ref), channel_id=1, source_target_pairs={{0,24},{4,28},{8,16},{12,20},{16,8},{20,12},{24,0},{28,4},{1,25},{... | collective-permute-start | bytes 233480 | tf_op jit(solution)/shard_map/ppermute | solution.py:197
  12.6 1.7 %collective-permute-start.4 = (bf16[4,304,128]{2,1,0:T(8,128)(2,1)S(1)}, bf16[4,304,128]{2,1,0:T(8,128)(2,1)S(1)}, u32[]{:S(2)}, u32[]{:S(2)}) collective-permute-start(bf16[4,304,128]{2,1,0:T(8,128)(2,1)S(1)} %stack.1), channel_id=1, source_target_pairs={{0,4},{4,0},{8,12},{12,8},{16,20},{20,16},{24,28},{28,24},{1,5},{5... | collective-permute-start | bytes 933896 | tf_op jit(solution)/shard_map/ppermute | solution.py:197
  12.7 7.0 %collective-permute-start.8 = (f32[48,512]{1,0:T(8,128)S(1)}, f32[48,512]{1,0:T(8,128)S(1)}, u32[]{:S(2)}, u32[]{:S(2)}) collective-permute-start(f32[48,512]{1,0:T(8,128)S(1)} %copy-done.1), channel_id=1, source_target_pairs={{0,4},{4,0},{8,12},{12,8},{16,20},{20,16},{24,28},{28,24},{1,5},{5... | collective-permute-start | bytes 294920 | tf_op jit(solution)/shard_map/ppermute | solution.py:197
  15.2 5.5 %collective-permute-start.5 = (f32[2,1024]{1,0:T(2,128)S(1)}, f32[2,1024]{1,0:T(2,128)S(1)}, u32[]{:S(2)}, u32[]{:S(2)}) collective-permute-start(f32[2,1024]{1,0:T(2,128)S(1)} %get-tuple-element.17.refs_0_), channel_id=1, source_target_pairs={{0,3},{1,2},{2,1},{3,0},{4,7},{5,6},{6,5},{7,4},{8,11},{9,10},{10,... | collective-permute-start | bytes 24584 | tf_op jit(solution)/shard_map/ppermute | solution.py:197
  18.9 4.5 %collective-permute-start.6 = (f32[2,1024]{1,0:T(2,128)S(1)}, f32[2,1024]{1,0:T(2,128)S(1)}, u32[]{:S(2)}, u32[]{:S(2)}) collective-permute-start(f32[2,1024]{1,0:T(2,128)S(1)} %get-tuple-element.17.refs_0_), channel_id=1, source_target_pairs={{0,2},{1,3},{2,0},{3,1},{4,6},{5,7},{6,4},{7,5},{8,10},{9,11},{10,... | collective-permute-start | bytes 24584 | tf_op jit(solution)/shard_map/ppermute | solution.py:197
  18.9 4.5 %collective-permute-start.7 = (f32[2,1024]{1,0:T(2,128)S(1)}, f32[2,1024]{1,0:T(2,128)S(1)}, u32[]{:S(2)}, u32[]{:S(2)}) collective-permute-start(f32[2,1024]{1,0:T(2,128)S(1)} %get-tuple-element.17.refs_0_), channel_id=1, source_target_pairs={{0,1},{1,0},{2,3},{3,2},{4,5},{5,4},{6,7},{7,6},{8,9},{9,8},{10,11... | collective-permute-start | bytes 24584 | tf_op jit(solution)/shard_map/ppermute | solution.py:197
  24.4 3.9 %collective-permute-start.10 = (f32[56,128]{1,0:T(8,128)S(1)}, f32[56,128]{1,0:T(8,128)S(1)}, u32[]{:S(2)}, u32[]{:S(2)}) collective-permute-start(f32[56,128]{1,0:T(8,128)S(1)} %get-tuple-element.24), channel_id=1, source_target_pairs={{0,16},{4,20},{8,24},{12,28},{16,0},{20,4},{24,8},{28,12},{1,17},{... | collective-permute-start | bytes 86024 | tf_op jit(solution)/shard_map/ppermute | solution.py:197
  25.2 4.8 %collective-permute-start.11 = (f32[56,128]{1,0:T(8,128)S(1)}, f32[56,128]{1,0:T(8,128)S(1)}, u32[]{:S(2)}, u32[]{:S(2)}) collective-permute-start(f32[56,128]{1,0:T(8,128)S(1)} %get-tuple-element.25), channel_id=1, source_target_pairs={{0,24},{4,28},{8,16},{12,20},{16,8},{20,12},{24,0},{28,4},{1,25},{... | collective-permute-start | bytes 86024 | tf_op jit(solution)/shard_map/ppermute | solution.py:197
  26.5 3.9 %collective-permute-start.9 = (f32[56,128]{1,0:T(8,128)S(1)}, f32[56,128]{1,0:T(8,128)S(1)}, u32[]{:S(2)}, u32[]{:S(2)}) collective-permute-start(f32[56,128]{1,0:T(8,128)S(1)} %get-tuple-element.23), channel_id=1, source_target_pairs={{0,8},{4,12},{8,0},{12,4},{16,24},{20,28},{24,16},{28,20},{1,9},{5... | collective-permute-start | bytes 86024 | tf_op jit(solution)/shard_map/ppermute | solution.py:197
  30.4 5.7 %collective-permute-start.12 = (f32[56,128]{1,0:T(8,128)S(1)}, f32[56,128]{1,0:T(8,128)S(1)}, u32[]{:S(2)}, u32[]{:S(2)}) collective-permute-start(f32[56,128]{1,0:T(8,128)S(1)} %emit_block.1.refs_1_), channel_id=1, source_target_pairs={{0,3},{1,2},{2,1},{3,0},{4,7},{5,6},{6,5},{7,4},{8,11},{9,10},{10,... | collective-permute-start | bytes 86024 | tf_op jit(solution)/shard_map/ppermute | solution.py:197
  31.9 4.8 %collective-permute-start.13 = (f32[56,128]{1,0:T(8,128)S(1)}, f32[56,128]{1,0:T(8,128)S(1)}, u32[]{:S(2)}, u32[]{:S(2)}) collective-permute-start(f32[56,128]{1,0:T(8,128)S(1)} %emit_block.1.refs_1_), channel_id=1, source_target_pairs={{0,2},{1,3},{2,0},{3,1},{4,6},{5,7},{6,4},{7,5},{8,10},{9,11},{10,... | collective-permute-start | bytes 86024 | tf_op jit(solution)/shard_map/ppermute | solution.py:197
  32.5 4.4 %collective-permute-start.14 = (f32[56,128]{1,0:T(8,128)S(1)}, f32[56,128]{1,0:T(8,128)S(1)}, u32[]{:S(2)}, u32[]{:S(2)}) collective-permute-start(f32[56,128]{1,0:T(8,128)S(1)} %emit_block.1.refs_1_), channel_id=1, source_target_pairs={{0,1},{1,0},{2,3},{3,2},{4,5},{5,4},{6,7},{7,6},{8,9},{9,8},{10,11... | collective-permute-start | bytes 86024 | tf_op jit(solution)/shard_map/ppermute | solution.py:197

commit v5 on v4

--- a/solution.py
+++ b/solution.py
@@ -12,6 +12,7 @@
 SMEM = pltpu.MemorySpace.SMEM
 HBM = pltpu.MemorySpace.HBM
 TAIL = 8
+JOINT = 2
 CHUNK = 8
 
 
@@ -65,15 +66,20 @@
     for h, src_ref in enumerate(src_refs):
         lanes = slice(h * src_ref.shape[0], (h + 1) * src_ref.shape[0])
         stats = []
-        for q in range(per_step):
-            logits = lax.dot_general(
-                dst_refs[q][:depth], src_ref[...], (((0,), (1,)), ((), ())), preferred_element_type=jnp.float32
+        width = dst_refs[0].shape[1]
+        for first in range(0, per_step, JOINT):
+            some = range(first, min(first + JOINT, per_step))
+            columns = jnp.concatenate([dst_refs[q][:depth] for q in some], axis=1)
+            tall = lax.dot_general(
+                columns, src_ref[...], (((0,), (1,)), ((), ())), preferred_element_type=jnp.float32
             )
-            peak = jnp.max(logits, axis=0, keepdims=True)
-            shifted = jnp.exp(logits - peak)
-            peak_ref[pl.ds(step * per_step + q, 1), lanes] = peak
-            stats.append((peak, jnp.sum(shifted, axis=0, keepdims=True)))
-            expo_ref[q, :, lanes] = shifted.astype(expo_ref.dtype)
+            for q in some:
+                logits = tall[(q - first) * width : (q - first + 1) * width]
+                peak = jnp.max(logits, axis=0, keepdims=True)
+                shifted = jnp.exp(logits - peak)
+                peak_ref[pl.ds(step * per_step + q, 1), lanes] = peak
+                stats.append((peak, jnp.sum(shifted, axis=0, keepdims=True)))
+                expo_ref[q, :, lanes] = shifted.astype(expo_ref.dtype)
         local_peak = functools.reduce(jnp.maximum, [p for p, _ in stats])
         local_total = functools.reduce(jnp.add, [t * jnp.exp(p - local_peak) for p, t in stats])
 
@@ -96,6 +102,8 @@
 
 
 def carry_tile(steps, per_step, n_stats, n_src, n_tiles, n_out, *refs):
+    if n_out > 1:
+        core_ref, refs = refs[0], refs[1:]
     stat_refs, refs = refs[:n_stats], refs[n_stats:]
     alpha_refs, refs = refs[:n_src], refs[n_src:]
     expo_refs, refs = refs[:n_tiles], refs[n_tiles:]
@@ -112,8 +120,10 @@
     scales = []
     for h in range(n_src):
         lanes = slice(h * sources, (h + 1) * sources)
-        row_peak = functools.reduce(jnp.maximum, [s[0:1, lanes] for s in stat_refs])
-        scales.append((lanes, row_peak, tree_sum([s[1:2, lanes] * jnp.exp(s[0:1, lanes] - row_peak) for s in stat_refs])))
+        turned = slice((n_src - 1 - h) * sources, (n_src - h) * sources)
+        known = [(s[0:1, at], s[1:2, at]) for s, at in zip(stat_refs, [lanes] * (n_stats - 1) + [turned], strict=True)]
+        row_peak = functools.reduce(jnp.maximum, [p for p, _ in known])
+        scales.append((lanes, row_peak, tree_sum([t * jnp.exp(p - row_peak) for p, t in known])))
     shares = []
     for t in range(n_tiles):
         terms = []
@@ -132,10 +142,14 @@
                     )
                 )
             product = tree_sum(product)
-            if len(out_refs[0].shape) == 3:
+            if n_out == 1:
                 out_refs[0][slot, :seqs] = product
-            elif t == 0:
-                out_refs[i][:seqs] = product
+            elif i in (0, 3):
+                out_refs[i // 3][t, :seqs] = product
+            elif i == 1:
+                beside = product
+            else:
+                out_refs[2][t, :seqs] = jnp.where(core_ref[0] == 0, beside, product)
             emit_ref = emit_refs[t * each + i]
             terms.append(product * emit_ref[emit_ref.shape[0] - seqs :].astype(jnp.float32))
         shares.append(functools.reduce(jnp.add, terms))
@@ -146,11 +160,8 @@
         share = jnp.sum(spread[...].T, axis=0, keepdims=True)
         tail = jnp.broadcast_to(share, (TAIL, share.shape[1]))
         for out_ref in out_refs:
-            if len(out_ref.shape) == 3:
-                for group in range(out_ref.shape[0]):
-                    out_ref[group, seqs:] = tail
-            else:
-                out_ref[seqs:] = tail
+            for group in range(out_ref.shape[0]):
+                out_ref[group, seqs:] = tail
 
 
 def pieces(refs):
@@ -169,36 +180,48 @@
     return terms[0]
 
 
-def emit_block(own_ref, *refs):
-    parts_refs, out_ref = refs[:-1], refs[-1]
+def emit_block(parts_ref, own_ref, out_ref):
     seqs = out_ref.shape[0] - TAIL
-    if len(parts_refs) > 1:
-        sums = tree_sum([r[...] for r in parts_refs])
-    else:
-        sums = jnp.sum(parts_refs[0][...], axis=0)
+    sums = jnp.sum(parts_ref[...], axis=0)
     out_ref[:seqs] = sums[:seqs] * own_ref[own_ref.shape[0] - seqs :].astype(jnp.float32)
     out_ref[seqs:] = sums[seqs:]
 
 
+def emit_pair(own_ref, corner_ref, asked_ref, told_ref, mine_ref, theirs_ref, out_ref):
+    seqs = out_ref.shape[1] - TAIL
+    for t, emit_ref in enumerate((mine_ref, theirs_ref.at[0])):
+        sums = (own_ref[t] + corner_ref[t]) + (asked_ref[t] + told_ref[1 - t])
+        out_ref[t, :seqs] = sums[:seqs] * emit_ref[emit_ref.shape[0] - seqs :].astype(jnp.float32)
+        out_ref[t, seqs:] = sums[seqs:]
+
+
 def finish(states, n_blocks, *refs):
-    place_ref = refs[0]
-    block_refs = refs[1 : 1 + n_blocks]
-    alpha_ref, log_ref = refs[1 + n_blocks :]
-    seqs, cols = alpha_ref.shape[0], block_refs[0].shape[1]
-    total = tree_sum([b[seqs:] for b in block_refs])
+    place_refs, block_refs = refs[:n_blocks], refs[n_blocks : 2 * n_blocks]
+    alpha_ref, log_ref = refs[2 * n_blocks :]
+    seqs, cols = alpha_ref.shape[0], block_refs[0].shape[-1]
+    views = [b if len(b.shape) == 2 else b.at[k // 3] for k, b in enumerate(block_refs)]
+    total = tree_sum([b[seqs:] for b in views])
     log_ref[...] = jnp.log(total[0, :seqs])
     scale = (states / jnp.broadcast_to(total[0:1], (cols, cols)).T)[:seqs]
-    for k in range(n_blocks):
-        start = pl.multiple_of((place_ref[0] ^ (0, 3, 2, 1)[k]) * cols, cols)
-        alpha_ref[:, pl.ds(start, cols)] = block_refs[k][:seqs] * scale
+    for place_ref, block in zip(place_refs, views, strict=True):
+        start = pl.multiple_of(place_ref[0] * cols, cols)
+        alpha_ref[:, pl.ds(start, cols)] = block[:seqs] * scale
 
 
 def hop(x, axis, count, k):
     return lax.ppermute(x, axis, [(i, i ^ k) for i in range(count)])
 
 
-def swap(x, axis, count):
-    return [x] + [hop(x, axis, count, k) for k in (3, 2, 1)]
+def exchange(x, rows, cols, paired):
+    here = lax.axis_index("col").astype(jnp.int32)
+    if not paired:
+        turns = [0] + list(range(cols - 1, 0, -1))
+        return [x] + [hop(x, "col", cols, k) for k in turns[1:]], [here ^ k for k in turns]
+    odd = lax.axis_index("row").astype(jnp.int32) & 1
+    mixed = [(r * cols + c, r * cols + (c ^ (3 if r % 2 else 1))) for r in range(rows) for c in range(cols)]
+    asked = lax.ppermute(x, ("row", "col"), mixed)
+    arrays = [x, hop(x, "col", cols, 2), asked, hop(asked, "row", rows, 1)]
+    return arrays, [here, here ^ 2, here ^ (1 + 2 * odd), here ^ (3 - 2 * odd)]
 
 
 def on_device(alpha_prev, tokens, src_emb, dst_emb, emission):
@@ -225,7 +248,7 @@
         compiler_params=room(8),
     )(*[pltpu.with_memory_space_constraint(x, HBM) for x in (tokens, emission, dst_emb)])
 
-    paired = rows == 8
+    paired = rows == 8 and cols == 4
     if paired:
         half = rows // 2
         srcs = [src_emb, hop(src_emb, "row", rows, 1)]
@@ -242,8 +265,9 @@
             compiler_params=room(8),
         )(*like)
         arrived = [like, [hop(pile, "row", rows, 1)]]
-        sums_shape = (jax.ShapeDtypeStruct((seqs + TAIL, group), f32),) * half
-        sums_block = [((seqs + TAIL, group), False)] * half
+        core = (lax.axis_index("row").astype(jnp.int32) & 1).reshape(1)
+        sums_shape = (jax.ShapeDtypeStruct((2, seqs + TAIL, group), f32),) * 3
+        sums_block = [((2, seqs + TAIL, group), False)] * 3
     else:
         srcs, alphas = [src_emb], [alpha_prev]
         arrived = [[lax.all_gather(packed, "row", axis=0)]]
@@ -282,12 +306,14 @@
         peaks.append(peak)
         stats = [stat]
 
+    known, _ = exchange(stats[0], rows, cols, paired)
     flat = sum(arrived, [])
     partial = pl.pallas_call(
         functools.partial(carry_tile, steps, per_step * tiles, cols, halves, tiles, len(sums_shape)),
         out_shape=sums_shape,
         grid=grid,
-        in_specs=block_specs(
+        in_specs=[pl.BlockSpec(memory_space=SMEM)] * paired
+        + block_specs(
             steps,
             [stat_block] * cols
             + [((seqs, sources), False)] * halves
@@ -299,31 +325,36 @@
         scratch_shapes=[pltpu.VMEM((group, group), f32)],
         name="carry_tile",
         compiler_params=room(16),
-    )(*swap(stats[0], "col", cols), *alphas, *expos, *peaks, *flat)
+    )(*([core] if paired else []), *known, *alphas, *expos, *peaks, *flat)
 
     if paired:
-        parts = [partial[0]] + [hop(partial[m], "row", rows, 2 * m) for m in range(1, half)]
+        own, corner, turned = partial
+        asked = lax.ppermute(turned, "row", [(i, i ^ (4 if i % 2 else 2)) for i in range(rows)])
+        corner = hop(corner, "row", rows, rows - 2)
+        told = hop(asked, "row", rows, 1)
+        body, operands = emit_pair, (own, corner, asked, told, packed, arrived[1][0])
+        block_shape = (2, seqs + TAIL, group)
     else:
-        parts = [lax.all_to_all(partial[0], "row", 0, 0)]
+        body, operands = emit_block, (lax.all_to_all(partial[0], "row", 0, 0), packed)
+        block_shape = (seqs + TAIL, group)
     block = pl.pallas_call(
-        emit_block,
-        out_shape=jax.ShapeDtypeStruct((seqs + TAIL, group), f32),
-        in_specs=[pl.BlockSpec(memory_space=VMEM)] * (1 + len(parts)),
+        body,
+        out_shape=jax.ShapeDtypeStruct(block_shape, f32),
+        in_specs=[pl.BlockSpec(memory_space=VMEM)] * len(operands),
         out_specs=pl.BlockSpec(memory_space=VMEM),
         name="emit_block",
         compiler_params=room(8),
-    )(packed, *parts)
-
-    blocks = swap(block, "col", cols)
-    place = lax.axis_index("col").astype(jnp.int32).reshape(1)
+    )(*operands)
+
+    blocks, places = exchange(block, rows, cols, paired)
     return pl.pallas_call(
         functools.partial(finish, float(group * rows * cols), cols),
         out_shape=(jax.ShapeDtypeStruct((seqs, group * cols), f32), jax.ShapeDtypeStruct((seqs,), f32)),
-        in_specs=[pl.BlockSpec(memory_space=SMEM)] + [pl.BlockSpec(memory_space=VMEM)] * cols,
+        in_specs=[pl.BlockSpec(memory_space=SMEM)] * cols + [pl.BlockSpec(memory_space=VMEM)] * cols,
         out_specs=(pl.BlockSpec(memory_space=VMEM), pl.BlockSpec(memory_space=VMEM)),
         name="finish",
         compiler_params=room(8),
-    )(place, *blocks)
+    )(*[p.reshape(1) for p in places], *blocks)
 
 
 def solution(mesh):

time: 37.9 us -> 36 us (0.950)
  the two profiles are of different devices: /device:TPU:0 before, /device:TPU:1 now
where the time goes in v5:
time: 36 us; the launch traced here: 35.8 us
  waiting for transfers between devices  15.5 us (43%)
  starting transfers between devices  14.5 us (40%)
  Pallas kernels  5.15 us (14%)
  between operations  0.69 us (2%)
    ppermute x12, waiting for transfers between devices, hop(): return lax.ppermute(x, axis, [(i, i ^ k) for i in range(count)])  10.2 us
    ppermute x12, starting transfers between devices, hop(): return lax.ppermute(x, axis, [(i, i ^ k) for i in range(count)])  8.05 us
    ppermute x2, starting transfers between devices, exchange(): asked = lax.ppermute(x, ('row', 'col'), mixed)  5.89 us
    ppermute x2, waiting for transfers between devices, exchange(): asked = lax.ppermute(x, ('row', 'col'), mixed)  3.44 us
    ppermute x1, waiting for transfers between devices, on_device(): lax.ppermute(turned, 'row', [(i, i ^ (4 if i % 2 else 2)) for i in range(...  1.88 us
    pallas_call x1, Pallas kernels, on_device(): pl.pallas_call(pick_rows, out_shape=jax.ShapeDtypeStruct((depth + seqs, g...  1.88 us
    pallas_call x2, Pallas kernels, on_device(): pl.pallas_call(functools.partial(softmax_tile, steps, per_step, halves, l...  1.55 us
    pallas_call x1, Pallas kernels, on_device(): pl.pallas_call(functools.partial(carry_tile, steps, per_step * tiles, col...  0.94 us
  transfers between devices with their start and end apart: 15, of which 10 were waited for; matrix products, arithmetic and copies ran while one was open for 0% of the time, Pallas kernels for 10%

profile of v5, /device:TPU:1, one launch (start us, length us, event | category | flops | bytes accessed | tf_op | source)
XLA Modules:
  0.0 35.8 jit_solution(1789767019638835508)
XLA Ops:
  0.6 0.0 copy-start
  0.6 0.0 copy-start.1
  0.7 0.1 collective-permute-start
  0.8 1.9 %pick_rows.1.refs_0_.refs_2_.refs_11_.mine_ref = bf16[304,128]{1,0:T(8,128)(2,1)S(1)} custom-call(s32[48]{0:T(128)} %tokens_ref.1, bf16[16640,128]{1,0:T(8,128)(2,1)} %table_ref.1, bf16[256,128]{1,0:T(8,128)(2,1)} %dst_ref.1), custom_call_target="tpu_custom_call" | custom-call | tf_op jit(solution)/shard_map/pick_rows/pallas_call | solution.py:234
  2.7 0.0 collective-permute-done.refs_1_
  2.7 2.7 %collective-permute-start.1 = (bf16[304,128]{1,0:T(8,128)(2,1)S(1)}, bf16[304,128]{1,0:T(8,128)(2,1)S(1)}, u32[]{:S(2)}, u32[]{:S(2)}) collective-permute-start(bf16[304,128]{1,0:T(8,128)(2,1)S(1)} %pick_rows.1.refs_0_.refs_2_.refs_11_.mine_ref), channel_id=1, source_target_pairs={{0,8},{4,12},{8,0},{12,4},{16,24},{20,28},{24,16},{28,20},{1,9},{5... | collective-permute-start | bytes 233480 | tf_op jit(solution)/shard_map/ppermute | solution.py:212
  5.4 1.2 %collective-permute-start.2 = (bf16[304,128]{1,0:T(8,128)(2,1)S(1)}, bf16[304,128]{1,0:T(8,128)(2,1)S(1)}, u32[]{:S(2)}, u32[]{:S(2)}) collective-permute-start(bf16[304,128]{1,0:T(8,128)(2,1)S(1)} %pick_rows.1.refs_0_.refs_2_.refs_11_.mine_ref), channel_id=1, source_target_pairs={{0,16},{4,20},{8,24},{12,28},{16,0},{20,4},{24,8},{28,12},{1,17},{... | collective-permute-start | bytes 233480 | tf_op jit(solution)/shard_map/ppermute | solution.py:212
  6.6 0.0 collective-permute-start.3
  6.7 1.3 %collective-permute-done.1.refs_1_.refs_3_.refs_12_ = bf16[304,128]{1,0:T(8,128)(2,1)S(1)} collective-permute-done((bf16[304,128]{1,0:T(8,128)(2,1)S(1)}, bf16[304,128]{1,0:T(8,128)(2,1)S(1)}, u32[]{:S(2)}, u32[]{:S(2)}) %collective-permute-start.1) | collective-permute-done | bytes 77856 | tf_op jit(solution)/shard_map/ppermute | solution.py:212
  8.0 0.7 %collective-permute-done.2.refs_2_.refs_4_.refs_13_ = bf16[304,128]{1,0:T(8,128)(2,1)S(1)} collective-permute-done((bf16[304,128]{1,0:T(8,128)(2,1)S(1)}, bf16[304,128]{1,0:T(8,128)(2,1)S(1)}, u32[]{:S(2)}, u32[]{:S(2)}) %collective-permute-start.2) | collective-permute-done | bytes 77856 | tf_op jit(solution)/shard_map/ppermute | solution.py:212
  8.6 2.1 %collective-permute-done.3.refs_3_.refs_5_.refs_14_ = bf16[304,128]{1,0:T(8,128)(2,1)S(1)} collective-permute-done((bf16[304,128]{1,0:T(8,128)(2,1)S(1)}, bf16[304,128]{1,0:T(8,128)(2,1)S(1)}, u32[]{:S(2)}, u32[]{:S(2)}) %collective-permute-start.3) | collective-permute-done | bytes 77856 | tf_op jit(solution)/shard_map/ppermute | solution.py:212
  10.8 1.9 %collective-permute-start.4 = (bf16[4,304,128]{2,1,0:T(8,128)(2,1)S(1)}, bf16[4,304,128]{2,1,0:T(8,128)(2,1)S(1)}, u32[]{:S(2)}, u32[]{:S(2)}) collective-permute-start(bf16[4,304,128]{2,1,0:T(8,128)(2,1)S(1)} %stack.1), channel_id=1, source_target_pairs={{0,4},{4,0},{8,12},{12,8},{16,20},{20,16},{24,28},{28,24},{1,5},{5... | collective-permute-start | bytes 933896 | tf_op jit(solution)/shard_map/ppermute | solution.py:212
  12.7 0.0 copy-done.1
  12.7 0.1 collective-permute-start.8
  12.8 0.0 copy-done
  12.8 0.8 %softmax_tile.2 = (bf16[4,128,1024]{2,1,0:T(8,128)(2,1)S(1)}, f32[4,1024]{1,0:T(4,128)S(1)}, f32[2,1024]{1,0:T(2,128)S(1)}) custom-call(bf16[512,256]{1,0:T(8,128)(2,1)S(1)} %copy-done, bf16[512,256]{1,0:T(8,128)(2,1)S(1)} %collective-permute-done.refs_1_, bf16[304,128]{1,0:T(8,128)(2,1)S(1)} %pick_rows.1.refs_0_.refs_2_.refs_11_.mine_ref, ...), custom_call_target="tpu_custom_call" | custom-call | tf_op jit(solution)/shard_map/softmax_tile/pallas_call | solution.py:289
  13.6 0.4 %collective-permute-done.4.refs_2_.refs_15_.theirs_ref = bf16[4,304,128]{2,1,0:T(8,128)(2,1)S(1)} collective-permute-done((bf16[4,304,128]{2,1,0:T(8,128)(2,1)S(1)}, bf16[4,304,128]{2,1,0:T(8,128)(2,1)S(1)}, u32[]{:S(2)}, u32[]{:S(2)}) %collective-permute-start.4) | collective-permute-done | bytes 311328 | tf_op jit(solution)/shard_map/ppermute | solution.py:212
  14.0 0.8 %softmax_tile.3 = (bf16[4,128,1024]{2,1,0:T(8,128)(2,1)S(1)}, f32[4,1024]{1,0:T(4,128)S(1)}, f32[2,1024]{1,0:T(2,128)S(1)}) custom-call(bf16[512,256]{1,0:T(8,128)(2,1)S(1)} %copy-done, bf16[512,256]{1,0:T(8,128)(2,1)S(1)} %collective-permute-done.refs_1_, bf16[4,304,128]{2,1,0:T(8,128)(2,1)S(1)} %collective-permute-done.4.refs_2_.refs_15_.theirs_ref, ...), custom_call_target="tpu_custom_call" | custom-call | tf_op jit(solution)/shard_map/softmax_tile/pallas_call | solution.py:289
  14.8 3.4 %collective-permute-start.6 = (f32[2,1024]{1,0:T(2,128)S(1)}, f32[2,1024]{1,0:T(2,128)S(1)}, u32[]{:S(2)}, u32[]{:S(2)}) collective-permute-start(f32[2,1024]{1,0:T(2,128)S(1)} %get-tuple-element.16.refs_1_), channel_id=1, source_target_pairs={{0,1},{1,0},{2,3},{3,2},{4,7},{5,6},{6,5},{7,4},{8,9},{9,8},{10,11... | collective-permute-start | bytes 24584 | tf_op jit(solution)/shard_map/ppermute | solution.py:222
  18.1 0.0 collective-permute-start.5
  18.1 1.0 %collective-permute-done.6.refs_3_ = f32[2,1024]{1,0:T(2,128)S(1)} collective-permute-done((f32[2,1024]{1,0:T(2,128)S(1)}, f32[2,1024]{1,0:T(2,128)S(1)}, u32[]{:S(2)}, u32[]{:S(2)}) %collective-permute-start.6) | collective-permute-done | bytes 8224 | tf_op jit(solution)/shard_map/ppermute | solution.py:222
  19.2 0.2 collective-permute-start.7
  19.4 0.0 collective-permute-done.8.refs_6_
  19.4 2.2 %collective-permute-done.5.refs_2_ = f32[2,1024]{1,0:T(2,128)S(1)} collective-permute-done((f32[2,1024]{1,0:T(2,128)S(1)}, f32[2,1024]{1,0:T(2,128)S(1)}, u32[]{:S(2)}, u32[]{:S(2)}) %collective-permute-start.5) | collective-permute-done | bytes 8224 | tf_op jit(solution)/shard_map/ppermute | solution.py:212
  21.5 0.0 collective-permute-done.7.refs_4_
  21.5 0.9 %carry_tile.1 = (f32[2,56,128]{2,1,0:T(8,128)S(1)}, f32[2,56,128]{2,1,0:T(8,128)S(1)}, f32[2,56,128]{2,1,0:T(8,128)S(1)}) custom-call(s32[1]{0:T(128)} %bitcast.4.refs_0_, f32[2,1024]{1,0:T(2,128)S(1)} %get-tuple-element.16.refs_1_, f32[2,1024]{1,0:T(2,128)S(1)} %collective-permute-done.5.refs_2_, f32[2,1024]{1,0:T(2,128)S(1)} %collective-permute-done.6.refs_3_, ...), custom_call_target="tpu_custom_call" | custom-call | tf_op jit(solution)/shard_map/carry_tile/pallas_call | solution.py:311
  22.5 0.6 %collective-permute-start.10 = (f32[2,56,128]{2,1,0:T(8,128)S(1)}, f32[2,56,128]{2,1,0:T(8,128)S(1)}, u32[]{:S(2)}, u32[]{:S(2)}) collective-permute-start(f32[2,56,128]{2,1,0:T(8,128)S(1)} %get-tuple-element.23), channel_id=1, source_target_pairs={{0,8},{4,20},{8,0},{12,28},{16,24},{20,4},{24,16},{28,12},{1,9},{5... | collective-permute-start | bytes 172040 | tf_op jit(solution)/shard_map/ppermute | solution.py:332
  23.1 0.9 %collective-permute-start.9 = (f32[2,56,128]{2,1,0:T(8,128)S(1)}, f32[2,56,128]{2,1,0:T(8,128)S(1)}, u32[]{:S(2)}, u32[]{:S(2)}) collective-permute-start(f32[2,56,128]{2,1,0:T(8,128)S(1)} %get-tuple-element.22), channel_id=1, source_target_pairs={{0,24},{4,28},{8,16},{12,20},{16,8},{20,12},{24,0},{28,4},{1,25},{... | collective-permute-start | bytes 172040 | tf_op jit(solution)/shard_map/ppermute | solution.py:212
  24.0 1.9 %collective-permute-done.10.asked_ref = f32[2,56,128]{2,1,0:T(8,128)S(1)} collective-permute-done((f32[2,56,128]{2,1,0:T(8,128)S(1)}, f32[2,56,128]{2,1,0:T(8,128)S(1)}, u32[]{:S(2)}, u32[]{:S(2)}) %collective-permute-start.10) | collective-permute-done | bytes 57376 | tf_op jit(solution)/shard_map/ppermute | solution.py:332
  25.9 0.7 %collective-permute-start.11 = (f32[2,56,128]{2,1,0:T(8,128)S(1)}, f32[2,56,128]{2,1,0:T(8,128)S(1)}, u32[]{:S(2)}, u32[]{:S(2)}) collective-permute-start(f32[2,56,128]{2,1,0:T(8,128)S(1)} %collective-permute-done.10.asked_ref), channel_id=1, source_target_pairs={{0,4},{4,0},{8,12},{12,8},{16,20},{20,16},{24,28},{28,24},{1,5},{5... | collective-permute-start | bytes 172040 | tf_op jit(solution)/shard_map/ppermute | solution.py:212
  26.6 1.0 %collective-permute-done.9.corner_ref = f32[2,56,128]{2,1,0:T(8,128)S(1)} collective-permute-done((f32[2,56,128]{2,1,0:T(8,128)S(1)}, f32[2,56,128]{2,1,0:T(8,128)S(1)}, u32[]{:S(2)}, u32[]{:S(2)}) %collective-permute-start.9) | collective-permute-done | bytes 57376 | tf_op jit(solution)/shard_map/ppermute | solution.py:212
  27.5 0.0 collective-permute-done.11.told_ref
  27.6 2.5 %collective-permute-start.13 = (f32[2,56,128]{2,1,0:T(8,128)S(1)}, f32[2,56,128]{2,1,0:T(8,128)S(1)}, u32[]{:S(2)}, u32[]{:S(2)}) collective-permute-start(f32[2,56,128]{2,1,0:T(8,128)S(1)} %emit_block.1.refs_4_), channel_id=1, source_target_pairs={{0,1},{1,0},{2,3},{3,2},{4,7},{5,6},{6,5},{7,4},{8,9},{9,8},{10,11... | collective-permute-start | bytes 172040 | tf_op jit(solution)/shard_map/ppermute | solution.py:222
  30.1 0.0 collective-permute-start.12
  30.1 2.4 %collective-permute-done.13.refs_6_ = f32[2,56,128]{2,1,0:T(8,128)S(1)} collective-permute-done((f32[2,56,128]{2,1,0:T(8,128)S(1)}, f32[2,56,128]{2,1,0:T(8,128)S(1)}, u32[]{:S(2)}, u32[]{:S(2)}) %collective-permute-start.13) | collective-permute-done | bytes 57376 | tf_op jit(solution)/shard_map/ppermute | solution.py:222
  32.5 0.1 collective-permute-start.14
  32.6 2.5 %collective-permute-done.12.refs_5_ = f32[2,56,128]{2,1,0:T(8,128)S(1)} collective-permute-done((f32[2,56,128]{2,1,0:T(8,128)S(1)}, f32[2,56,128]{2,1,0:T(8,128)S(1)}, u32[]{:S(2)}, u32[]{:S(2)}) %collective-permute-start.12) | collective-permute-done | bytes 57376 | tf_op jit(solution)/shard_map/ppermute | solution.py:212
  35.1 0.0 collective-permute-done.14.refs_7_
  35.1 0.7 %finish.1 = (f32[48,512]{1,0:T(8,128)}, f32[48]{0:T(128)}) custom-call(s32[1]{0:T(128)} %bitcast.refs_0_, s32[1]{0:T(128)} %bitcast.1.refs_1_, s32[1]{0:T(128)} %bitcast.2.refs_2_, s32[1]{0:T(128)} %bitcast.3.refs_3_, f32[2,56,128]{2,1,0:T(8,128)S(1)} %emit_block.1.refs_4_, f32[2,56,128]{2,1,0:T(8,128)S(1)} %collective-permute-done.12.refs_5_, ...), custom_call_target="tpu_custom_call" | custom-call | tf_op jit(solution)/shard_map/finish/pallas_call | solution.py:350
  (2 shorter events, 0.0 us)
Async XLA Ops:
  0.6 12.2 %copy-start = (bf16[512,256]{1,0:T(8,128)(2,1)S(1)}, bf16[512,256]{1,0:T(8,128)(2,1)}, u32[]{:S(2)}) copy-start(bf16[512,256]{1,0:T(8,128)(2,1)} %refs_0_.3) | copy-start | bytes 786436
  0.6 12.1 %copy-start.1 = (f32[48,512]{1,0:T(8,128)S(1)}, f32[48,512]{1,0:T(8,128)}, u32[]{:S(2)}) copy-start(f32[48,512]{1,0:T(8,128)} %refs_5_.1) | copy-start | bytes 294916
  0.7 2.0 %collective-permute-start = (bf16[512,256]{1,0:T(8,128)(2,1)}, bf16[512,256]{1,0:T(8,128)(2,1)S(1)}, u32[]{:S(2)}, u32[]{:S(2)}) collective-permute-start(bf16[512,256]{1,0:T(8,128)(2,1)} %refs_0_.3), channel_id=1, source_target_pairs={{0,4},{4,0},{8,12},{12,8},{16,20},{20,16},{24,28},{28,24},{1,5},{5... | collective-permute-start | bytes 786440 | tf_op jit(solution)/shard_map/ppermute | solution.py:212
  2.7 5.3 %collective-permute-start.1 = (bf16[304,128]{1,0:T(8,128)(2,1)S(1)}, bf16[304,128]{1,0:T(8,128)(2,1)S(1)}, u32[]{:S(2)}, u32[]{:S(2)}) collective-permute-start(bf16[304,128]{1,0:T(8,128)(2,1)S(1)} %pick_rows.1.refs_0_.refs_2_.refs_11_.mine_ref), channel_id=1, source_target_pairs={{0,8},{4,12},{8,0},{12,4},{16,24},{20,28},{24,16},{28,20},{1,9},{5... | collective-permute-start | bytes 233480 | tf_op jit(solution)/shard_map/ppermute | solution.py:212
  5.4 3.2 %collective-permute-start.2 = (bf16[304,128]{1,0:T(8,128)(2,1)S(1)}, bf16[304,128]{1,0:T(8,128)(2,1)S(1)}, u32[]{:S(2)}, u32[]{:S(2)}) collective-permute-start(bf16[304,128]{1,0:T(8,128)(2,1)S(1)} %pick_rows.1.refs_0_.refs_2_.refs_11_.mine_ref), channel_id=1, source_target_pairs={{0,16},{4,20},{8,24},{12,28},{16,0},{20,4},{24,8},{28,12},{1,17},{... | collective-permute-start | bytes 233480 | tf_op jit(solution)/shard_map/ppermute | solution.py:212
  6.6 4.1 %collective-permute-start.3 = (bf16[304,128]{1,0:T(8,128)(2,1)S(1)}, bf16[304,128]{1,0:T(8,128)(2,1)S(1)}, u32[]{:S(2)}, u32[]{:S(2)}) collective-permute-start(bf16[304,128]{1,0:T(8,128)(2,1)S(1)} %pick_rows.1.refs_0_.refs_2_.refs_11_.mine_ref), channel_id=1, source_target_pairs={{0,24},{4,28},{8,16},{12,20},{16,8},{20,12},{24,0},{28,4},{1,25},{... | collective-permute-start | bytes 233480 | tf_op jit(solution)/shard_map/ppermute | solution.py:212
  10.8 3.2 %collective-permute-start.4 = (bf16[4,304,128]{2,1,0:T(8,128)(2,1)S(1)}, bf16[4,304,128]{2,1,0:T(8,128)(2,1)S(1)}, u32[]{:S(2)}, u32[]{:S(2)}) collective-permute-start(bf16[4,304,128]{2,1,0:T(8,128)(2,1)S(1)} %stack.1), channel_id=1, source_target_pairs={{0,4},{4,0},{8,12},{12,8},{16,20},{20,16},{24,28},{28,24},{1,5},{5... | collective-permute-start | bytes 933896 | tf_op jit(solution)/shard_map/ppermute | solution.py:212
  12.7 6.6 %collective-permute-start.8 = (f32[48,512]{1,0:T(8,128)S(1)}, f32[48,512]{1,0:T(8,128)S(1)}, u32[]{:S(2)}, u32[]{:S(2)}) collective-permute-start(f32[48,512]{1,0:T(8,128)S(1)} %copy-done.1), channel_id=1, source_target_pairs={{0,4},{4,0},{8,12},{12,8},{16,20},{20,16},{24,28},{28,24},{1,5},{5... | collective-permute-start | bytes 294920 | tf_op jit(solution)/shard_map/ppermute | solution.py:212
  14.8 4.4 %collective-permute-start.6 = (f32[2,1024]{1,0:T(2,128)S(1)}, f32[2,1024]{1,0:T(2,128)S(1)}, u32[]{:S(2)}, u32[]{:S(2)}) collective-permute-start(f32[2,1024]{1,0:T(2,128)S(1)} %get-tuple-element.16.refs_1_), channel_id=1, source_target_pairs={{0,1},{1,0},{2,3},{3,2},{4,7},{5,6},{6,5},{7,4},{8,9},{9,8},{10,11... | collective-permute-start | bytes 24584 | tf_op jit(solution)/shard_map/ppermute | solution.py:222
  18.1 3.4 %collective-permute-start.5 = (f32[2,1024]{1,0:T(2,128)S(1)}, f32[2,1024]{1,0:T(2,128)S(1)}, u32[]{:S(2)}, u32[]{:S(2)}) collective-permute-start(f32[2,1024]{1,0:T(2,128)S(1)} %get-tuple-element.16.refs_1_), channel_id=1, source_target_pairs={{0,2},{1,3},{2,0},{3,1},{4,6},{5,7},{6,4},{7,5},{8,10},{9,11},{10,... | collective-permute-start | bytes 24584 | tf_op jit(solution)/shard_map/ppermute | solution.py:212
  19.2 2.4 %collective-permute-start.7 = (f32[2,1024]{1,0:T(2,128)S(1)}, f32[2,1024]{1,0:T(2,128)S(1)}, u32[]{:S(2)}, u32[]{:S(2)}) collective-permute-start(f32[2,1024]{1,0:T(2,128)S(1)} %collective-permute-done.6.refs_3_), channel_id=1, source_target_pairs={{0,4},{4,0},{8,12},{12,8},{16,20},{20,16},{24,28},{28,24},{1,5},{5... | collective-permute-start | bytes 24584 | tf_op jit(solution)/shard_map/ppermute | solution.py:212
  22.5 3.4 %collective-permute-start.10 = (f32[2,56,128]{2,1,0:T(8,128)S(1)}, f32[2,56,128]{2,1,0:T(8,128)S(1)}, u32[]{:S(2)}, u32[]{:S(2)}) collective-permute-start(f32[2,56,128]{2,1,0:T(8,128)S(1)} %get-tuple-element.23), channel_id=1, source_target_pairs={{0,8},{4,20},{8,0},{12,28},{16,24},{20,4},{24,16},{28,12},{1,9},{5... | collective-permute-start | bytes 172040 | tf_op jit(solution)/shard_map/ppermute | solution.py:332
  23.1 4.5 %collective-permute-start.9 = (f32[2,56,128]{2,1,0:T(8,128)S(1)}, f32[2,56,128]{2,1,0:T(8,128)S(1)}, u32[]{:S(2)}, u32[]{:S(2)}) collective-permute-start(f32[2,56,128]{2,1,0:T(8,128)S(1)} %get-tuple-element.22), channel_id=1, source_target_pairs={{0,24},{4,28},{8,16},{12,20},{16,8},{20,12},{24,0},{28,4},{1,25},{... | collective-permute-start | bytes 172040 | tf_op jit(solution)/shard_map/ppermute | solution.py:212
  25.9 1.7 %collective-permute-start.11 = (f32[2,56,128]{2,1,0:T(8,128)S(1)}, f32[2,56,128]{2,1,0:T(8,128)S(1)}, u32[]{:S(2)}, u32[]{:S(2)}) collective-permute-start(f32[2,56,128]{2,1,0:T(8,128)S(1)} %collective-permute-done.10.asked_ref), channel_id=1, source_target_pairs={{0,4},{4,0},{8,12},{12,8},{16,20},{20,16},{24,28},{28,24},{1,5},{5... | collective-permute-start | bytes 172040 | tf_op jit(solution)/shard_map/ppermute | solution.py:212
  27.6 4.9 %collective-permute-start.13 = (f32[2,56,128]{2,1,0:T(8,128)S(1)}, f32[2,56,128]{2,1,0:T(8,128)S(1)}, u32[]{:S(2)}, u32[]{:S(2)}) collective-permute-start(f32[2,56,128]{2,1,0:T(8,128)S(1)} %emit_block.1.refs_4_), channel_id=1, source_target_pairs={{0,1},{1,0},{2,3},{3,2},{4,7},{5,6},{6,5},{7,4},{8,9},{9,8},{10,11... | collective-permute-start | bytes 172040 | tf_op jit(solution)/shard_map/ppermute | solution.py:222
  30.1 5.0 %collective-permute-start.12 = (f32[2,56,128]{2,1,0:T(8,128)S(1)}, f32[2,56,128]{2,1,0:T(8,128)S(1)}, u32[]{:S(2)}, u32[]{:S(2)}) collective-permute-start(f32[2,56,128]{2,1,0:T(8,128)S(1)} %emit_block.1.refs_4_), channel_id=1, source_target_pairs={{0,2},{1,3},{2,0},{3,1},{4,6},{5,7},{6,4},{7,5},{8,10},{9,11},{10,... | collective-permute-start | bytes 172040 | tf_op jit(solution)/shard_map/ppermute | solution.py:212
  32.5 2.6 %collective-permute-start.14 = (f32[2,56,128]{2,1,0:T(8,128)S(1)}, f32[2,56,128]{2,1,0:T(8,128)S(1)}, u32[]{:S(2)}, u32[]{:S(2)}) collective-permute-start(f32[2,56,128]{2,1,0:T(8,128)S(1)} %collective-permute-done.13.refs_6_), channel_id=1, source_target_pairs={{0,4},{4,0},{8,12},{12,8},{16,20},{20,16},{24,28},{28,24},{1,5},{5... | collective-permute-start | bytes 172040 | tf_op jit(solution)/shard_map/ppermute | solution.py:212

commit v6 on v5

--- a/solution.py
+++ b/solution.py
@@ -102,8 +102,6 @@
 
 
 def carry_tile(steps, per_step, n_stats, n_src, n_tiles, n_out, *refs):
-    if n_out > 1:
-        core_ref, refs = refs[0], refs[1:]
     stat_refs, refs = refs[:n_stats], refs[n_stats:]
     alpha_refs, refs = refs[:n_src], refs[n_src:]
     expo_refs, refs = refs[:n_tiles], refs[n_tiles:]
@@ -146,10 +144,8 @@
                 out_refs[0][slot, :seqs] = product
             elif i in (0, 3):
                 out_refs[i // 3][t, :seqs] = product
-            elif i == 1:
-                beside = product
-            else:
-                out_refs[2][t, :seqs] = jnp.where(core_ref[0] == 0, beside, product)
+            elif i == 1 + t:
+                out_refs[2][t, :seqs] = product
             emit_ref = emit_refs[t * each + i]
             terms.append(product * emit_ref[emit_ref.shape[0] - seqs :].astype(jnp.float32))
         shares.append(functools.reduce(jnp.add, terms))
@@ -206,6 +202,10 @@
     for place_ref, block in zip(place_refs, views, strict=True):
         start = pl.multiple_of(place_ref[0] * cols, cols)
         alpha_ref[:, pl.ds(start, cols)] = block[:seqs] * scale
+
+
+def ask(x, count, even, odd):
+    return lax.ppermute(x, "row", [(i, i ^ (odd if i % 2 else even)) for i in range(count)])
 
 
 def hop(x, axis, count, k):
@@ -255,7 +255,7 @@
         alphas = [alpha_prev, hop(alpha_prev, "row", rows, 1)]
         ready = lax.optimization_barrier((packed, srcs[1]))
         srcs[1] = ready[1]
-        like = [packed] + [hop(ready[0], "row", rows, 2 * m) for m in range(1, half)]
+        like = [packed, ask(ready[0], rows, 2, 4), ask(ready[0], rows, 4, 2), hop(ready[0], "row", rows, rows - 2)]
         pile = pl.pallas_call(
             stack,
             out_shape=jax.ShapeDtypeStruct((half,) + packed.shape, packed.dtype),
@@ -265,7 +265,6 @@
             compiler_params=room(8),
         )(*like)
         arrived = [like, [hop(pile, "row", rows, 1)]]
-        core = (lax.axis_index("row").astype(jnp.int32) & 1).reshape(1)
         sums_shape = (jax.ShapeDtypeStruct((2, seqs + TAIL, group), f32),) * 3
         sums_block = [((2, seqs + TAIL, group), False)] * 3
     else:
@@ -312,8 +311,7 @@
         functools.partial(carry_tile, steps, per_step * tiles, cols, halves, tiles, len(sums_shape)),
         out_shape=sums_shape,
         grid=grid,
-        in_specs=[pl.BlockSpec(memory_space=SMEM)] * paired
-        + block_specs(
+        in_specs=block_specs(
             steps,
             [stat_block] * cols
             + [((seqs, sources), False)] * halves
@@ -325,11 +323,11 @@
         scratch_shapes=[pltpu.VMEM((group, group), f32)],
         name="carry_tile",
         compiler_params=room(16),
-    )(*([core] if paired else []), *known, *alphas, *expos, *peaks, *flat)
+    )(*known, *alphas, *expos, *peaks, *flat)
 
     if paired:
         own, corner, turned = partial
-        asked = lax.ppermute(turned, "row", [(i, i ^ (4 if i % 2 else 2)) for i in range(rows)])
+        asked = ask(turned, rows, 2, 4)
         corner = hop(corner, "row", rows, rows - 2)
         told = hop(asked, "row", rows, 1)
         body, operands = emit_pair, (own, corner, asked, told, packed, arrived[1][0])

time: 36 us -> 36 us (level)
    ppermute x1 -> x3, starting transfers between devices: 0.56 us -> 4.52 us  [ask(): lax.ppermute(x, 'row', [(i, i ^ (odd if i % 2 else even)) for i in range(...]
    ppermute x12 -> x10, starting transfers between devices: 8.05 us -> 4.22 us  [hop(): return lax.ppermute(x, axis, [(i, i ^ k) for i in range(count)])]
    ppermute x12 -> x10, waiting for transfers between devices: 10.2 us -> 8.1 us  [hop(): return lax.ppermute(x, axis, [(i, i ^ k) for i in range(count)])]
    ppermute x1 -> x3, waiting for transfers between devices: 1.88 us -> 3.74 us  [ask(): lax.ppermute(x, 'row', [(i, i ^ (odd if i % 2 else even)) for i in range(...]
where the time goes in v6:
time: 36 us; the launch traced here: 35.8 us
  waiting for transfers between devices  15.3 us (42%)
  starting transfers between devices  14.7 us (41%)
  Pallas kernels  5.17 us (14%)
  between operations  0.69 us (2%)
    ppermute x10, waiting for transfers between devices, hop(): return lax.ppermute(x, axis, [(i, i ^ k) for i in range(count)])  8.1 us
    ppermute x2, starting transfers between devices, exchange(): asked = lax.ppermute(x, ('row', 'col'), mixed)  5.94 us
    ppermute x3, starting transfers between devices, ask(): lax.ppermute(x, 'row', [(i, i ^ (odd if i % 2 else even)) for i in range(...  4.52 us
    ppermute x10, starting transfers between devices, hop(): return lax.ppermute(x, axis, [(i, i ^ k) for i in range(count)])  4.22 us
    ppermute x3, waiting for transfers between devices, ask(): lax.ppermute(x, 'row', [(i, i ^ (odd if i % 2 else even)) for i in range(...  3.74 us
    ppermute x2, waiting for transfers between devices, exchange(): asked = lax.ppermute(x, ('row', 'col'), mixed)  3.44 us
    pallas_call x1, Pallas kernels, on_device(): pl.pallas_call(pick_rows, out_shape=jax.ShapeDtypeStruct((depth + seqs, g...  1.88 us
    pallas_call x2, Pallas kernels, on_device(): pl.pallas_call(functools.partial(softmax_tile, steps, per_step, halves, l...  1.57 us
  transfers between devices with their start and end apart: 15, of which 10 were waited for; matrix products, arithmetic and copies ran while one was open for 0% of the time, Pallas kernels for 10%

profile of v6, /device:TPU:1, one launch (start us, length us, event | category | flops | bytes accessed | tf_op | source)
XLA Modules:
  0.0 35.8 jit_solution(7283223974085186951)
XLA Ops:
  0.6 0.0 copy-start
  0.6 0.0 copy-start.1
  0.7 0.1 collective-permute-start
  0.8 1.9 %pick_rows.1.refs_0_.refs_2_.refs_10_.mine_ref = bf16[304,128]{1,0:T(8,128)(2,1)S(1)} custom-call(s32[48]{0:T(128)} %tokens_ref.1, bf16[16640,128]{1,0:T(8,128)(2,1)} %table_ref.1, bf16[256,128]{1,0:T(8,128)(2,1)} %dst_ref.1), custom_call_target="tpu_custom_call" | custom-call | tf_op jit(solution)/shard_map/pick_rows/pallas_call | solution.py:234
  2.7 0.0 collective-permute-done.refs_1_
  2.7 2.8 %collective-permute-start.1 = (bf16[304,128]{1,0:T(8,128)(2,1)S(1)}, bf16[304,128]{1,0:T(8,128)(2,1)S(1)}, u32[]{:S(2)}, u32[]{:S(2)}) collective-permute-start(bf16[304,128]{1,0:T(8,128)(2,1)S(1)} %pick_rows.1.refs_0_.refs_2_.refs_10_.mine_ref), channel_id=1, source_target_pairs={{0,8},{4,20},{8,0},{12,28},{16,24},{20,4},{24,16},{28,12},{1,9},{5... | collective-permute-start | bytes 233480 | tf_op jit(solution)/shard_map/ppermute | solution.py:208
  5.4 1.2 %collective-permute-start.2 = (bf16[304,128]{1,0:T(8,128)(2,1)S(1)}, bf16[304,128]{1,0:T(8,128)(2,1)S(1)}, u32[]{:S(2)}, u32[]{:S(2)}) collective-permute-start(bf16[304,128]{1,0:T(8,128)(2,1)S(1)} %pick_rows.1.refs_0_.refs_2_.refs_10_.mine_ref), channel_id=1, source_target_pairs={{0,16},{4,12},{8,24},{12,4},{16,0},{20,28},{24,8},{28,20},{1,17},{... | collective-permute-start | bytes 233480 | tf_op jit(solution)/shard_map/ppermute | solution.py:208
  6.6 0.0 collective-permute-start.3
  6.7 0.8 %collective-permute-done.1.refs_1_.refs_3_.refs_11_ = bf16[304,128]{1,0:T(8,128)(2,1)S(1)} collective-permute-done((bf16[304,128]{1,0:T(8,128)(2,1)S(1)}, bf16[304,128]{1,0:T(8,128)(2,1)S(1)}, u32[]{:S(2)}, u32[]{:S(2)}) %collective-permute-start.1) | collective-permute-done | bytes 77856 | tf_op jit(solution)/shard_map/ppermute | solution.py:208
  7.5 1.2 %collective-permute-done.2.refs_2_.refs_4_.refs_12_ = bf16[304,128]{1,0:T(8,128)(2,1)S(1)} collective-permute-done((bf16[304,128]{1,0:T(8,128)(2,1)S(1)}, bf16[304,128]{1,0:T(8,128)(2,1)S(1)}, u32[]{:S(2)}, u32[]{:S(2)}) %collective-permute-start.2) | collective-permute-done | bytes 77856 | tf_op jit(solution)/shard_map/ppermute | solution.py:208
  8.7 2.1 %collective-permute-done.3.refs_3_.refs_5_.refs_13_ = bf16[304,128]{1,0:T(8,128)(2,1)S(1)} collective-permute-done((bf16[304,128]{1,0:T(8,128)(2,1)S(1)}, bf16[304,128]{1,0:T(8,128)(2,1)S(1)}, u32[]{:S(2)}, u32[]{:S(2)}) %collective-permute-start.3) | collective-permute-done | bytes 77856 | tf_op jit(solution)/shard_map/ppermute | solution.py:212
  10.8 1.9 %collective-permute-start.4 = (bf16[4,304,128]{2,1,0:T(8,128)(2,1)S(1)}, bf16[4,304,128]{2,1,0:T(8,128)(2,1)S(1)}, u32[]{:S(2)}, u32[]{:S(2)}) collective-permute-start(bf16[4,304,128]{2,1,0:T(8,128)(2,1)S(1)} %stack.1), channel_id=1, source_target_pairs={{0,4},{4,0},{8,12},{12,8},{16,20},{20,16},{24,28},{28,24},{1,5},{5... | collective-permute-start | bytes 933896 | tf_op jit(solution)/shard_map/ppermute | solution.py:212
  12.7 0.0 copy-done.1
  12.7 0.1 collective-permute-start.8
  12.8 0.0 copy-done
  12.8 0.8 %softmax_tile.2 = (bf16[4,128,1024]{2,1,0:T(8,128)(2,1)S(1)}, f32[4,1024]{1,0:T(4,128)S(1)}, f32[2,1024]{1,0:T(2,128)S(1)}) custom-call(bf16[512,256]{1,0:T(8,128)(2,1)S(1)} %copy-done, bf16[512,256]{1,0:T(8,128)(2,1)S(1)} %collective-permute-done.refs_1_, bf16[304,128]{1,0:T(8,128)(2,1)S(1)} %pick_rows.1.refs_0_.refs_2_.refs_10_.mine_ref, ...), custom_call_target="tpu_custom_call" | custom-call | tf_op jit(solution)/shard_map/softmax_tile/pallas_call | solution.py:288
  13.6 0.4 collective-permute-done.4.refs_2_.refs_14_.theirs_ref
  14.0 0.8 %softmax_tile.3 = (bf16[4,128,1024]{2,1,0:T(8,128)(2,1)S(1)}, f32[4,1024]{1,0:T(4,128)S(1)}, f32[2,1024]{1,0:T(2,128)S(1)}) custom-call(bf16[512,256]{1,0:T(8,128)(2,1)S(1)} %copy-done, bf16[512,256]{1,0:T(8,128)(2,1)S(1)} %collective-permute-done.refs_1_, bf16[4,304,128]{2,1,0:T(8,128)(2,1)S(1)} %collective-permute-done.4.refs_2_.refs_14_.theirs_ref, ...), custom_call_target="tpu_custom_call" | custom-call | tf_op jit(solution)/shard_map/softmax_tile/pallas_call | solution.py:288
  14.8 3.4 %collective-permute-start.6 = (f32[2,1024]{1,0:T(2,128)S(1)}, f32[2,1024]{1,0:T(2,128)S(1)}, u32[]{:S(2)}, u32[]{:S(2)}) collective-permute-start(f32[2,1024]{1,0:T(2,128)S(1)} %get-tuple-element.16.refs_0_), channel_id=1, source_target_pairs={{0,1},{1,0},{2,3},{3,2},{4,7},{5,6},{6,5},{7,4},{8,9},{9,8},{10,11... | collective-permute-start | bytes 24584 | tf_op jit(solution)/shard_map/ppermute | solution.py:222
  18.1 0.0 collective-permute-start.5
  18.1 1.0 %collective-permute-done.6.refs_2_ = f32[2,1024]{1,0:T(2,128)S(1)} collective-permute-done((f32[2,1024]{1,0:T(2,128)S(1)}, f32[2,1024]{1,0:T(2,128)S(1)}, u32[]{:S(2)}, u32[]{:S(2)}) %collective-permute-start.6) | collective-permute-done | bytes 8224 | tf_op jit(solution)/shard_map/ppermute | solution.py:222
  19.2 0.2 collective-permute-start.7
  19.4 0.0 collective-permute-done.8.refs_5_
  19.4 2.2 %collective-permute-done.5.refs_1_ = f32[2,1024]{1,0:T(2,128)S(1)} collective-permute-done((f32[2,1024]{1,0:T(2,128)S(1)}, f32[2,1024]{1,0:T(2,128)S(1)}, u32[]{:S(2)}, u32[]{:S(2)}) %collective-permute-start.5) | collective-permute-done | bytes 8224 | tf_op jit(solution)/shard_map/ppermute | solution.py:212
  21.5 0.0 collective-permute-done.7.refs_3_
  21.5 0.9 %carry_tile.1 = (f32[2,56,128]{2,1,0:T(8,128)S(1)}, f32[2,56,128]{2,1,0:T(8,128)S(1)}, f32[2,56,128]{2,1,0:T(8,128)S(1)}) custom-call(f32[2,1024]{1,0:T(2,128)S(1)} %get-tuple-element.16.refs_0_, f32[2,1024]{1,0:T(2,128)S(1)} %collective-permute-done.5.refs_1_, f32[2,1024]{1,0:T(2,128)S(1)} %collective-permute-done.6.refs_2_, ...), custom_call_target="tpu_custom_call" | custom-call | tf_op jit(solution)/shard_map/carry_tile/pallas_call | solution.py:310
  22.5 0.6 %collective-permute-start.10 = (f32[2,56,128]{2,1,0:T(8,128)S(1)}, f32[2,56,128]{2,1,0:T(8,128)S(1)}, u32[]{:S(2)}, u32[]{:S(2)}) collective-permute-start(f32[2,56,128]{2,1,0:T(8,128)S(1)} %get-tuple-element.23), channel_id=1, source_target_pairs={{0,8},{4,20},{8,0},{12,28},{16,24},{20,4},{24,16},{28,12},{1,9},{5... | collective-permute-start | bytes 172040 | tf_op jit(solution)/shard_map/ppermute | solution.py:208
  23.0 1.1 %collective-permute-start.9 = (f32[2,56,128]{2,1,0:T(8,128)S(1)}, f32[2,56,128]{2,1,0:T(8,128)S(1)}, u32[]{:S(2)}, u32[]{:S(2)}) collective-permute-start(f32[2,56,128]{2,1,0:T(8,128)S(1)} %get-tuple-element.22), channel_id=1, source_target_pairs={{0,24},{4,28},{8,16},{12,20},{16,8},{20,12},{24,0},{28,4},{1,25},{... | collective-permute-start | bytes 172040 | tf_op jit(solution)/shard_map/ppermute | solution.py:212
  24.1 1.8 %collective-permute-done.10.asked_ref = f32[2,56,128]{2,1,0:T(8,128)S(1)} collective-permute-done((f32[2,56,128]{2,1,0:T(8,128)S(1)}, f32[2,56,128]{2,1,0:T(8,128)S(1)}, u32[]{:S(2)}, u32[]{:S(2)}) %collective-permute-start.10) | collective-permute-done | bytes 57376 | tf_op jit(solution)/shard_map/ppermute | solution.py:208
  25.9 0.7 %collective-permute-start.11 = (f32[2,56,128]{2,1,0:T(8,128)S(1)}, f32[2,56,128]{2,1,0:T(8,128)S(1)}, u32[]{:S(2)}, u32[]{:S(2)}) collective-permute-start(f32[2,56,128]{2,1,0:T(8,128)S(1)} %collective-permute-done.10.asked_ref), channel_id=1, source_target_pairs={{0,4},{4,0},{8,12},{12,8},{16,20},{20,16},{24,28},{28,24},{1,5},{5... | collective-permute-start | bytes 172040 | tf_op jit(solution)/shard_map/ppermute | solution.py:212
  26.6 0.9 %collective-permute-done.9.corner_ref = f32[2,56,128]{2,1,0:T(8,128)S(1)} collective-permute-done((f32[2,56,128]{2,1,0:T(8,128)S(1)}, f32[2,56,128]{2,1,0:T(8,128)S(1)}, u32[]{:S(2)}, u32[]{:S(2)}) %collective-permute-start.9) | collective-permute-done | bytes 57376 | tf_op jit(solution)/shard_map/ppermute | solution.py:212
  27.5 0.0 collective-permute-done.11.told_ref
  27.5 2.6 %collective-permute-start.13 = (f32[2,56,128]{2,1,0:T(8,128)S(1)}, f32[2,56,128]{2,1,0:T(8,128)S(1)}, u32[]{:S(2)}, u32[]{:S(2)}) collective-permute-start(f32[2,56,128]{2,1,0:T(8,128)S(1)} %emit_block.1.refs_4_), channel_id=1, source_target_pairs={{0,1},{1,0},{2,3},{3,2},{4,7},{5,6},{6,5},{7,4},{8,9},{9,8},{10,11... | collective-permute-start | bytes 172040 | tf_op jit(solution)/shard_map/ppermute | solution.py:222
  30.1 0.0 collective-permute-start.12
  30.1 2.4 %collective-permute-done.13.refs_6_ = f32[2,56,128]{2,1,0:T(8,128)S(1)} collective-permute-done((f32[2,56,128]{2,1,0:T(8,128)S(1)}, f32[2,56,128]{2,1,0:T(8,128)S(1)}, u32[]{:S(2)}, u32[]{:S(2)}) %collective-permute-start.13) | collective-permute-done | bytes 57376 | tf_op jit(solution)/shard_map/ppermute | solution.py:222
  32.5 0.1 collective-permute-start.14
  32.6 2.5 %collective-permute-done.12.refs_5_ = f32[2,56,128]{2,1,0:T(8,128)S(1)} collective-permute-done((f32[2,56,128]{2,1,0:T(8,128)S(1)}, f32[2,56,128]{2,1,0:T(8,128)S(1)}, u32[]{:S(2)}, u32[]{:S(2)}) %collective-permute-start.12) | collective-permute-done | bytes 57376 | tf_op jit(solution)/shard_map/ppermute | solution.py:212
  35.1 0.0 collective-permute-done.14.refs_7_
  35.1 0.7 %finish.1 = (f32[48,512]{1,0:T(8,128)}, f32[48]{0:T(128)}) custom-call(s32[1]{0:T(128)} %bitcast.refs_0_, s32[1]{0:T(128)} %bitcast.1.refs_1_, s32[1]{0:T(128)} %bitcast.2.refs_2_, s32[1]{0:T(128)} %bitcast.3.refs_3_, f32[2,56,128]{2,1,0:T(8,128)S(1)} %emit_block.1.refs_4_, f32[2,56,128]{2,1,0:T(8,128)S(1)} %collective-permute-done.12.refs_5_, ...), custom_call_target="tpu_custom_call" | custom-call | tf_op jit(solution)/shard_map/finish/pallas_call | solution.py:348
  (2 shorter events, 0.0 us)
Async XLA Ops:
  0.6 12.2 %copy-start = (bf16[512,256]{1,0:T(8,128)(2,1)S(1)}, bf16[512,256]{1,0:T(8,128)(2,1)}, u32[]{:S(2)}) copy-start(bf16[512,256]{1,0:T(8,128)(2,1)} %refs_0_.3) | copy-start | bytes 786436
  0.6 12.1 %copy-start.1 = (f32[48,512]{1,0:T(8,128)S(1)}, f32[48,512]{1,0:T(8,128)}, u32[]{:S(2)}) copy-start(f32[48,512]{1,0:T(8,128)} %refs_4_.1) | copy-start | bytes 294916
  0.7 2.0 %collective-permute-start = (bf16[512,256]{1,0:T(8,128)(2,1)}, bf16[512,256]{1,0:T(8,128)(2,1)S(1)}, u32[]{:S(2)}, u32[]{:S(2)}) collective-permute-start(bf16[512,256]{1,0:T(8,128)(2,1)} %refs_0_.3), channel_id=1, source_target_pairs={{0,4},{4,0},{8,12},{12,8},{16,20},{20,16},{24,28},{28,24},{1,5},{5... | collective-permute-start | bytes 786440 | tf_op jit(solution)/shard_map/ppermute | solution.py:212
  2.7 4.8 %collective-permute-start.1 = (bf16[304,128]{1,0:T(8,128)(2,1)S(1)}, bf16[304,128]{1,0:T(8,128)(2,1)S(1)}, u32[]{:S(2)}, u32[]{:S(2)}) collective-permute-start(bf16[304,128]{1,0:T(8,128)(2,1)S(1)} %pick_rows.1.refs_0_.refs_2_.refs_10_.mine_ref), channel_id=1, source_target_pairs={{0,8},{4,20},{8,0},{12,28},{16,24},{20,4},{24,16},{28,12},{1,9},{5... | collective-permute-start | bytes 233480 | tf_op jit(solution)/shard_map/ppermute | solution.py:208
  5.4 3.2 %collective-permute-start.2 = (bf16[304,128]{1,0:T(8,128)(2,1)S(1)}, bf16[304,128]{1,0:T(8,128)(2,1)S(1)}, u32[]{:S(2)}, u32[]{:S(2)}) collective-permute-start(bf16[304,128]{1,0:T(8,128)(2,1)S(1)} %pick_rows.1.refs_0_.refs_2_.refs_10_.mine_ref), channel_id=1, source_target_pairs={{0,16},{4,12},{8,24},{12,4},{16,0},{20,28},{24,8},{28,20},{1,17},{... | collective-permute-start | bytes 233480 | tf_op jit(solution)/shard_map/ppermute | solution.py:208
  6.6 4.1 %collective-permute-start.3 = (bf16[304,128]{1,0:T(8,128)(2,1)S(1)}, bf16[304,128]{1,0:T(8,128)(2,1)S(1)}, u32[]{:S(2)}, u32[]{:S(2)}) collective-permute-start(bf16[304,128]{1,0:T(8,128)(2,1)S(1)} %pick_rows.1.refs_0_.refs_2_.refs_10_.mine_ref), channel_id=1, source_target_pairs={{0,24},{4,28},{8,16},{12,20},{16,8},{20,12},{24,0},{28,4},{1,25},{... | collective-permute-start | bytes 233480 | tf_op jit(solution)/shard_map/ppermute | solution.py:212
  10.8 3.2 %collective-permute-start.4 = (bf16[4,304,128]{2,1,0:T(8,128)(2,1)S(1)}, bf16[4,304,128]{2,1,0:T(8,128)(2,1)S(1)}, u32[]{:S(2)}, u32[]{:S(2)}) collective-permute-start(bf16[4,304,128]{2,1,0:T(8,128)(2,1)S(1)} %stack.1), channel_id=1, source_target_pairs={{0,4},{4,0},{8,12},{12,8},{16,20},{20,16},{24,28},{28,24},{1,5},{5... | collective-permute-start | bytes 933896 | tf_op jit(solution)/shard_map/ppermute | solution.py:212
  12.7 6.6 %collective-permute-start.8 = (f32[48,512]{1,0:T(8,128)S(1)}, f32[48,512]{1,0:T(8,128)S(1)}, u32[]{:S(2)}, u32[]{:S(2)}) collective-permute-start(f32[48,512]{1,0:T(8,128)S(1)} %copy-done.1), channel_id=1, source_target_pairs={{0,4},{4,0},{8,12},{12,8},{16,20},{20,16},{24,28},{28,24},{1,5},{5... | collective-permute-start | bytes 294920 | tf_op jit(solution)/shard_map/ppermute | solution.py:212
  14.8 4.4 %collective-permute-start.6 = (f32[2,1024]{1,0:T(2,128)S(1)}, f32[2,1024]{1,0:T(2,128)S(1)}, u32[]{:S(2)}, u32[]{:S(2)}) collective-permute-start(f32[2,1024]{1,0:T(2,128)S(1)} %get-tuple-element.16.refs_0_), channel_id=1, source_target_pairs={{0,1},{1,0},{2,3},{3,2},{4,7},{5,6},{6,5},{7,4},{8,9},{9,8},{10,11... | collective-permute-start | bytes 24584 | tf_op jit(solution)/shard_map/ppermute | solution.py:222
  18.1 3.4 %collective-permute-start.5 = (f32[2,1024]{1,0:T(2,128)S(1)}, f32[2,1024]{1,0:T(2,128)S(1)}, u32[]{:S(2)}, u32[]{:S(2)}) collective-permute-start(f32[2,1024]{1,0:T(2,128)S(1)} %get-tuple-element.16.refs_0_), channel_id=1, source_target_pairs={{0,2},{1,3},{2,0},{3,1},{4,6},{5,7},{6,4},{7,5},{8,10},{9,11},{10,... | collective-permute-start | bytes 24584 | tf_op jit(solution)/shard_map/ppermute | solution.py:212
  19.2 2.4 %collective-permute-start.7 = (f32[2,1024]{1,0:T(2,128)S(1)}, f32[2,1024]{1,0:T(2,128)S(1)}, u32[]{:S(2)}, u32[]{:S(2)}) collective-permute-start(f32[2,1024]{1,0:T(2,128)S(1)} %collective-permute-done.6.refs_2_), channel_id=1, source_target_pairs={{0,4},{4,0},{8,12},{12,8},{16,20},{20,16},{24,28},{28,24},{1,5},{5... | collective-permute-start | bytes 24584 | tf_op jit(solution)/shard_map/ppermute | solution.py:212
  22.5 3.4 %collective-permute-start.10 = (f32[2,56,128]{2,1,0:T(8,128)S(1)}, f32[2,56,128]{2,1,0:T(8,128)S(1)}, u32[]{:S(2)}, u32[]{:S(2)}) collective-permute-start(f32[2,56,128]{2,1,0:T(8,128)S(1)} %get-tuple-element.23), channel_id=1, source_target_pairs={{0,8},{4,20},{8,0},{12,28},{16,24},{20,4},{24,16},{28,12},{1,9},{5... | collective-permute-start | bytes 172040 | tf_op jit(solution)/shard_map/ppermute | solution.py:208
  23.0 4.4 %collective-permute-start.9 = (f32[2,56,128]{2,1,0:T(8,128)S(1)}, f32[2,56,128]{2,1,0:T(8,128)S(1)}, u32[]{:S(2)}, u32[]{:S(2)}) collective-permute-start(f32[2,56,128]{2,1,0:T(8,128)S(1)} %get-tuple-element.22), channel_id=1, source_target_pairs={{0,24},{4,28},{8,16},{12,20},{16,8},{20,12},{24,0},{28,4},{1,25},{... | collective-permute-start | bytes 172040 | tf_op jit(solution)/shard_map/ppermute | solution.py:212
  25.9 1.6 %collective-permute-start.11 = (f32[2,56,128]{2,1,0:T(8,128)S(1)}, f32[2,56,128]{2,1,0:T(8,128)S(1)}, u32[]{:S(2)}, u32[]{:S(2)}) collective-permute-start(f32[2,56,128]{2,1,0:T(8,128)S(1)} %collective-permute-done.10.asked_ref), channel_id=1, source_target_pairs={{0,4},{4,0},{8,12},{12,8},{16,20},{20,16},{24,28},{28,24},{1,5},{5... | collective-permute-start | bytes 172040 | tf_op jit(solution)/shard_map/ppermute | solution.py:212
  27.5 5.0 %collective-permute-start.13 = (f32[2,56,128]{2,1,0:T(8,128)S(1)}, f32[2,56,128]{2,1,0:T(8,128)S(1)}, u32[]{:S(2)}, u32[]{:S(2)}) collective-permute-start(f32[2,56,128]{2,1,0:T(8,128)S(1)} %emit_block.1.refs_4_), channel_id=1, source_target_pairs={{0,1},{1,0},{2,3},{3,2},{4,7},{5,6},{6,5},{7,4},{8,9},{9,8},{10,11... | collective-permute-start | bytes 172040 | tf_op jit(solution)/shard_map/ppermute | solution.py:222
  30.1 5.0 %collective-permute-start.12 = (f32[2,56,128]{2,1,0:T(8,128)S(1)}, f32[2,56,128]{2,1,0:T(8,128)S(1)}, u32[]{:S(2)}, u32[]{:S(2)}) collective-permute-start(f32[2,56,128]{2,1,0:T(8,128)S(1)} %emit_block.1.refs_4_), channel_id=1, source_target_pairs={{0,2},{1,3},{2,0},{3,1},{4,6},{5,7},{6,4},{7,5},{8,10},{9,11},{10,... | collective-permute-start | bytes 172040 | tf_op jit(solution)/shard_map/ppermute | solution.py:212
  32.5 2.6 %collective-permute-start.14 = (f32[2,56,128]{2,1,0:T(8,128)S(1)}, f32[2,56,128]{2,1,0:T(8,128)S(1)}, u32[]{:S(2)}, u32[]{:S(2)}) collective-permute-start(f32[2,56,128]{2,1,0:T(8,128)S(1)} %collective-permute-done.13.refs_6_), channel_id=1, source_target_pairs={{0,4},{4,0},{8,12},{12,8},{16,20},{20,16},{24,28},{28,24},{1,5},{5... | collective-permute-start | bytes 172040 | tf_op jit(solution)/shard_map/ppermute | solution.py:212

commit v7 on v5

--- a/solution.py
+++ b/solution.py
@@ -123,16 +123,17 @@
         turned = slice((n_src - 1 - h) * sources, (n_src - h) * sources)
         known = [(s[0:1, at], s[1:2, at]) for s, at in zip(stat_refs, [lanes] * (n_stats - 1) + [turned], strict=True)]
         row_peak = functools.reduce(jnp.maximum, [p for p, _ in known])
-        scales.append((lanes, row_peak, tree_sum([t * jnp.exp(p - row_peak) for p, t in known])))
+        share = 1.0 / tree_sum([t * jnp.exp(p - row_peak) for p, t in known])
+        rows_at = pl.ds(step * each, each)
+        scales.append((lanes, [jnp.exp(p[rows_at, lanes] - row_peak) * share for p in peak_refs]))
     shares = []
     for t in range(n_tiles):
         terms = []
         for i in range(each):
             slot = step * each + i
             product = []
-            for alpha_ref, (lanes, row_peak, row_total) in zip(alpha_refs, scales, strict=True):
-                row_scale = jnp.exp(peak_refs[t][pl.ds(slot, 1), lanes] - row_peak) / row_total
-                weights = (alpha_ref[...] * row_scale).astype(jnp.bfloat16)
+            for alpha_ref, (lanes, row_scales) in zip(alpha_refs, scales, strict=True):
+                weights = (alpha_ref[...] * row_scales[t][i : i + 1]).astype(jnp.bfloat16)
                 product.append(
                     lax.dot_general(
                         weights,

time: 36 us -> 36 us (level)
  no operation moved by 1% of the time
where the time goes in v7:
time: 36 us; the launch traced here: 35.8 us
  waiting for transfers between devices  15.5 us (43%)
  starting transfers between devices  14.5 us (40%)
  Pallas kernels  5.15 us (14%)
  between operations  0.69 us (2%)
    ppermute x12, waiting for transfers between devices, hop(): return lax.ppermute(x, axis, [(i, i ^ k) for i in range(count)])  10.2 us
    ppermute x12, starting transfers between devices, hop(): return lax.ppermute(x, axis, [(i, i ^ k) for i in range(count)])  8.04 us
    ppermute x2, starting transfers between devices, exchange(): asked = lax.ppermute(x, ('row', 'col'), mixed)  5.89 us
    ppermute x2, waiting for transfers between devices, exchange(): asked = lax.ppermute(x, ('row', 'col'), mixed)  3.44 us
    ppermute x1, waiting for transfers between devices, on_device(): lax.ppermute(turned, 'row', [(i, i ^ (4 if i % 2 else 2)) for i in range(...  1.88 us
    pallas_call x1, Pallas kernels, on_device(): pl.pallas_call(pick_rows, out_shape=jax.ShapeDtypeStruct((depth + seqs, g...  1.88 us
    pallas_call x2, Pallas kernels, on_device(): pl.pallas_call(functools.partial(softmax_tile, steps, per_step, halves, l...  1.55 us
    pallas_call x1, Pallas kernels, on_device(): pl.pallas_call(functools.partial(carry_tile, steps, per_step * tiles, col...  0.94 us
  transfers between devices with their start and end apart: 15, of which 10 were waited for; matrix products, arithmetic and copies ran while one was open for 0% of the time, Pallas kernels for 10%

profile of v7, /device:TPU:1, one launch (start us, length us, event | category | flops | bytes accessed | tf_op | source)
XLA Modules:
  0.0 35.8 jit_solution(4637949825211297887)
XLA Ops:
  0.6 0.0 copy-start
  0.6 0.0 copy-start.1
  0.7 0.1 collective-permute-start
  0.8 1.9 %pick_rows.1.refs_0_.refs_2_.refs_11_.mine_ref = bf16[304,128]{1,0:T(8,128)(2,1)S(1)} custom-call(s32[48]{0:T(128)} %tokens_ref.1, bf16[16640,128]{1,0:T(8,128)(2,1)} %table_ref.1, bf16[256,128]{1,0:T(8,128)(2,1)} %dst_ref.1), custom_call_target="tpu_custom_call" | custom-call | tf_op jit(solution)/shard_map/pick_rows/pallas_call | solution.py:235
  2.7 0.0 collective-permute-done.refs_1_
  2.7 2.7 %collective-permute-start.1 = (bf16[304,128]{1,0:T(8,128)(2,1)S(1)}, bf16[304,128]{1,0:T(8,128)(2,1)S(1)}, u32[]{:S(2)}, u32[]{:S(2)}) collective-permute-start(bf16[304,128]{1,0:T(8,128)(2,1)S(1)} %pick_rows.1.refs_0_.refs_2_.refs_11_.mine_ref), channel_id=1, source_target_pairs={{0,8},{4,12},{8,0},{12,4},{16,24},{20,28},{24,16},{28,20},{1,9},{5... | collective-permute-start | bytes 233480 | tf_op jit(solution)/shard_map/ppermute | solution.py:213
  5.4 1.2 %collective-permute-start.2 = (bf16[304,128]{1,0:T(8,128)(2,1)S(1)}, bf16[304,128]{1,0:T(8,128)(2,1)S(1)}, u32[]{:S(2)}, u32[]{:S(2)}) collective-permute-start(bf16[304,128]{1,0:T(8,128)(2,1)S(1)} %pick_rows.1.refs_0_.refs_2_.refs_11_.mine_ref), channel_id=1, source_target_pairs={{0,16},{4,20},{8,24},{12,28},{16,0},{20,4},{24,8},{28,12},{1,17},{... | collective-permute-start | bytes 233480 | tf_op jit(solution)/shard_map/ppermute | solution.py:213
  6.6 0.0 collective-permute-start.3
  6.7 1.3 %collective-permute-done.1.refs_1_.refs_3_.refs_12_ = bf16[304,128]{1,0:T(8,128)(2,1)S(1)} collective-permute-done((bf16[304,128]{1,0:T(8,128)(2,1)S(1)}, bf16[304,128]{1,0:T(8,128)(2,1)S(1)}, u32[]{:S(2)}, u32[]{:S(2)}) %collective-permute-start.1) | collective-permute-done | bytes 77856 | tf_op jit(solution)/shard_map/ppermute | solution.py:213
  8.0 0.7 %collective-permute-done.2.refs_2_.refs_4_.refs_13_ = bf16[304,128]{1,0:T(8,128)(2,1)S(1)} collective-permute-done((bf16[304,128]{1,0:T(8,128)(2,1)S(1)}, bf16[304,128]{1,0:T(8,128)(2,1)S(1)}, u32[]{:S(2)}, u32[]{:S(2)}) %collective-permute-start.2) | collective-permute-done | bytes 77856 | tf_op jit(solution)/shard_map/ppermute | solution.py:213
  8.6 2.1 %collective-permute-done.3.refs_3_.refs_5_.refs_14_ = bf16[304,128]{1,0:T(8,128)(2,1)S(1)} collective-permute-done((bf16[304,128]{1,0:T(8,128)(2,1)S(1)}, bf16[304,128]{1,0:T(8,128)(2,1)S(1)}, u32[]{:S(2)}, u32[]{:S(2)}) %collective-permute-start.3) | collective-permute-done | bytes 77856 | tf_op jit(solution)/shard_map/ppermute | solution.py:213
  10.8 1.9 %collective-permute-start.4 = (bf16[4,304,128]{2,1,0:T(8,128)(2,1)S(1)}, bf16[4,304,128]{2,1,0:T(8,128)(2,1)S(1)}, u32[]{:S(2)}, u32[]{:S(2)}) collective-permute-start(bf16[4,304,128]{2,1,0:T(8,128)(2,1)S(1)} %stack.1), channel_id=1, source_target_pairs={{0,4},{4,0},{8,12},{12,8},{16,20},{20,16},{24,28},{28,24},{1,5},{5... | collective-permute-start | bytes 933896 | tf_op jit(solution)/shard_map/ppermute | solution.py:213
  12.7 0.0 copy-done.1
  12.7 0.1 collective-permute-start.8
  12.8 0.0 copy-done
  12.8 0.8 %softmax_tile.2 = (bf16[4,128,1024]{2,1,0:T(8,128)(2,1)S(1)}, f32[4,1024]{1,0:T(4,128)S(1)}, f32[2,1024]{1,0:T(2,128)S(1)}) custom-call(bf16[512,256]{1,0:T(8,128)(2,1)S(1)} %copy-done, bf16[512,256]{1,0:T(8,128)(2,1)S(1)} %collective-permute-done.refs_1_, bf16[304,128]{1,0:T(8,128)(2,1)S(1)} %pick_rows.1.refs_0_.refs_2_.refs_11_.mine_ref, ...), custom_call_target="tpu_custom_call" | custom-call | tf_op jit(solution)/shard_map/softmax_tile/pallas_call | solution.py:290
  13.6 0.4 %collective-permute-done.4.refs_2_.refs_15_.theirs_ref = bf16[4,304,128]{2,1,0:T(8,128)(2,1)S(1)} collective-permute-done((bf16[4,304,128]{2,1,0:T(8,128)(2,1)S(1)}, bf16[4,304,128]{2,1,0:T(8,128)(2,1)S(1)}, u32[]{:S(2)}, u32[]{:S(2)}) %collective-permute-start.4) | collective-permute-done | bytes 311328 | tf_op jit(solution)/shard_map/ppermute | solution.py:213
  14.0 0.8 %softmax_tile.3 = (bf16[4,128,1024]{2,1,0:T(8,128)(2,1)S(1)}, f32[4,1024]{1,0:T(4,128)S(1)}, f32[2,1024]{1,0:T(2,128)S(1)}) custom-call(bf16[512,256]{1,0:T(8,128)(2,1)S(1)} %copy-done, bf16[512,256]{1,0:T(8,128)(2,1)S(1)} %collective-permute-done.refs_1_, bf16[4,304,128]{2,1,0:T(8,128)(2,1)S(1)} %collective-permute-done.4.refs_2_.refs_15_.theirs_ref, ...), custom_call_target="tpu_custom_call" | custom-call | tf_op jit(solution)/shard_map/softmax_tile/pallas_call | solution.py:290
  14.8 3.4 %collective-permute-start.6 = (f32[2,1024]{1,0:T(2,128)S(1)}, f32[2,1024]{1,0:T(2,128)S(1)}, u32[]{:S(2)}, u32[]{:S(2)}) collective-permute-start(f32[2,1024]{1,0:T(2,128)S(1)} %get-tuple-element.16.refs_1_), channel_id=1, source_target_pairs={{0,1},{1,0},{2,3},{3,2},{4,7},{5,6},{6,5},{7,4},{8,9},{9,8},{10,11... | collective-permute-start | bytes 24584 | tf_op jit(solution)/shard_map/ppermute | solution.py:223
  18.1 0.0 collective-permute-start.5
  18.1 1.0 %collective-permute-done.6.refs_3_ = f32[2,1024]{1,0:T(2,128)S(1)} collective-permute-done((f32[2,1024]{1,0:T(2,128)S(1)}, f32[2,1024]{1,0:T(2,128)S(1)}, u32[]{:S(2)}, u32[]{:S(2)}) %collective-permute-start.6) | collective-permute-done | bytes 8224 | tf_op jit(solution)/shard_map/ppermute | solution.py:223
  19.2 0.2 collective-permute-start.7
  19.4 0.0 collective-permute-done.8.refs_6_
  19.4 2.2 %collective-permute-done.5.refs_2_ = f32[2,1024]{1,0:T(2,128)S(1)} collective-permute-done((f32[2,1024]{1,0:T(2,128)S(1)}, f32[2,1024]{1,0:T(2,128)S(1)}, u32[]{:S(2)}, u32[]{:S(2)}) %collective-permute-start.5) | collective-permute-done | bytes 8224 | tf_op jit(solution)/shard_map/ppermute | solution.py:213
  21.5 0.0 collective-permute-done.7.refs_4_
  21.5 0.9 %carry_tile.1 = (f32[2,56,128]{2,1,0:T(8,128)S(1)}, f32[2,56,128]{2,1,0:T(8,128)S(1)}, f32[2,56,128]{2,1,0:T(8,128)S(1)}) custom-call(s32[1]{0:T(128)} %bitcast.4.refs_0_, f32[2,1024]{1,0:T(2,128)S(1)} %get-tuple-element.16.refs_1_, f32[2,1024]{1,0:T(2,128)S(1)} %collective-permute-done.5.refs_2_, f32[2,1024]{1,0:T(2,128)S(1)} %collective-permute-done.6.refs_3_, ...), custom_call_target="tpu_custom_call" | custom-call | tf_op jit(solution)/shard_map/carry_tile/pallas_call | solution.py:312
  22.5 0.6 %collective-permute-start.10 = (f32[2,56,128]{2,1,0:T(8,128)S(1)}, f32[2,56,128]{2,1,0:T(8,128)S(1)}, u32[]{:S(2)}, u32[]{:S(2)}) collective-permute-start(f32[2,56,128]{2,1,0:T(8,128)S(1)} %get-tuple-element.23), channel_id=1, source_target_pairs={{0,8},{4,20},{8,0},{12,28},{16,24},{20,4},{24,16},{28,12},{1,9},{5... | collective-permute-start | bytes 172040 | tf_op jit(solution)/shard_map/ppermute | solution.py:333
  23.0 0.9 %collective-permute-start.9 = (f32[2,56,128]{2,1,0:T(8,128)S(1)}, f32[2,56,128]{2,1,0:T(8,128)S(1)}, u32[]{:S(2)}, u32[]{:S(2)}) collective-permute-start(f32[2,56,128]{2,1,0:T(8,128)S(1)} %get-tuple-element.22), channel_id=1, source_target_pairs={{0,24},{4,28},{8,16},{12,20},{16,8},{20,12},{24,0},{28,4},{1,25},{... | collective-permute-start | bytes 172040 | tf_op jit(solution)/shard_map/ppermute | solution.py:213
  24.0 1.9 %collective-permute-done.10.asked_ref = f32[2,56,128]{2,1,0:T(8,128)S(1)} collective-permute-done((f32[2,56,128]{2,1,0:T(8,128)S(1)}, f32[2,56,128]{2,1,0:T(8,128)S(1)}, u32[]{:S(2)}, u32[]{:S(2)}) %collective-permute-start.10) | collective-permute-done | bytes 57376 | tf_op jit(solution)/shard_map/ppermute | solution.py:333
  25.9 0.7 %collective-permute-start.11 = (f32[2,56,128]{2,1,0:T(8,128)S(1)}, f32[2,56,128]{2,1,0:T(8,128)S(1)}, u32[]{:S(2)}, u32[]{:S(2)}) collective-permute-start(f32[2,56,128]{2,1,0:T(8,128)S(1)} %collective-permute-done.10.asked_ref), channel_id=1, source_target_pairs={{0,4},{4,0},{8,12},{12,8},{16,20},{20,16},{24,28},{28,24},{1,5},{5... | collective-permute-start | bytes 172040 | tf_op jit(solution)/shard_map/ppermute | solution.py:213
  26.6 1.0 %collective-permute-done.9.corner_ref = f32[2,56,128]{2,1,0:T(8,128)S(1)} collective-permute-done((f32[2,56,128]{2,1,0:T(8,128)S(1)}, f32[2,56,128]{2,1,0:T(8,128)S(1)}, u32[]{:S(2)}, u32[]{:S(2)}) %collective-permute-start.9) | collective-permute-done | bytes 57376 | tf_op jit(solution)/shard_map/ppermute | solution.py:213
  27.5 0.0 collective-permute-done.11.told_ref
  27.6 2.5 %collective-permute-start.13 = (f32[2,56,128]{2,1,0:T(8,128)S(1)}, f32[2,56,128]{2,1,0:T(8,128)S(1)}, u32[]{:S(2)}, u32[]{:S(2)}) collective-permute-start(f32[2,56,128]{2,1,0:T(8,128)S(1)} %emit_block.1.refs_4_), channel_id=1, source_target_pairs={{0,1},{1,0},{2,3},{3,2},{4,7},{5,6},{6,5},{7,4},{8,9},{9,8},{10,11... | collective-permute-start | bytes 172040 | tf_op jit(solution)/shard_map/ppermute | solution.py:223
  30.1 0.0 collective-permute-start.12
  30.1 2.4 %collective-permute-done.13.refs_6_ = f32[2,56,128]{2,1,0:T(8,128)S(1)} collective-permute-done((f32[2,56,128]{2,1,0:T(8,128)S(1)}, f32[2,56,128]{2,1,0:T(8,128)S(1)}, u32[]{:S(2)}, u32[]{:S(2)}) %collective-permute-start.13) | collective-permute-done | bytes 57376 | tf_op jit(solution)/shard_map/ppermute | solution.py:223
  32.5 0.1 collective-permute-start.14
  32.6 2.5 %collective-permute-done.12.refs_5_ = f32[2,56,128]{2,1,0:T(8,128)S(1)} collective-permute-done((f32[2,56,128]{2,1,0:T(8,128)S(1)}, f32[2,56,128]{2,1,0:T(8,128)S(1)}, u32[]{:S(2)}, u32[]{:S(2)}) %collective-permute-start.12) | collective-permute-done | bytes 57376 | tf_op jit(solution)/shard_map/ppermute | solution.py:213
  35.1 0.0 collective-permute-done.14.refs_7_
  35.1 0.7 %finish.1 = (f32[48,512]{1,0:T(8,128)}, f32[48]{0:T(128)}) custom-call(s32[1]{0:T(128)} %bitcast.refs_0_, s32[1]{0:T(128)} %bitcast.1.refs_1_, s32[1]{0:T(128)} %bitcast.2.refs_2_, s32[1]{0:T(128)} %bitcast.3.refs_3_, f32[2,56,128]{2,1,0:T(8,128)S(1)} %emit_block.1.refs_4_, f32[2,56,128]{2,1,0:T(8,128)S(1)} %collective-permute-done.12.refs_5_, ...), custom_call_target="tpu_custom_call" | custom-call | tf_op jit(solution)/shard_map/finish/pallas_call | solution.py:351
  (2 shorter events, 0.0 us)
Async XLA Ops:
  0.6 12.2 %copy-start = (bf16[512,256]{1,0:T(8,128)(2,1)S(1)}, bf16[512,256]{1,0:T(8,128)(2,1)}, u32[]{:S(2)}) copy-start(bf16[512,256]{1,0:T(8,128)(2,1)} %refs_0_.3) | copy-start | bytes 786436
  0.6 12.1 %copy-start.1 = (f32[48,512]{1,0:T(8,128)S(1)}, f32[48,512]{1,0:T(8,128)}, u32[]{:S(2)}) copy-start(f32[48,512]{1,0:T(8,128)} %refs_5_.1) | copy-start | bytes 294916
  0.7 2.0 %collective-permute-start = (bf16[512,256]{1,0:T(8,128)(2,1)}, bf16[512,256]{1,0:T(8,128)(2,1)S(1)}, u32[]{:S(2)}, u32[]{:S(2)}) collective-permute-start(bf16[512,256]{1,0:T(8,128)(2,1)} %refs_0_.3), channel_id=1, source_target_pairs={{0,4},{4,0},{8,12},{12,8},{16,20},{20,16},{24,28},{28,24},{1,5},{5... | collective-permute-start | bytes 786440 | tf_op jit(solution)/shard_map/ppermute | solution.py:213
  2.7 5.3 %collective-permute-start.1 = (bf16[304,128]{1,0:T(8,128)(2,1)S(1)}, bf16[304,128]{1,0:T(8,128)(2,1)S(1)}, u32[]{:S(2)}, u32[]{:S(2)}) collective-permute-start(bf16[304,128]{1,0:T(8,128)(2,1)S(1)} %pick_rows.1.refs_0_.refs_2_.refs_11_.mine_ref), channel_id=1, source_target_pairs={{0,8},{4,12},{8,0},{12,4},{16,24},{20,28},{24,16},{28,20},{1,9},{5... | collective-permute-start | bytes 233480 | tf_op jit(solution)/shard_map/ppermute | solution.py:213
  5.4 3.2 %collective-permute-start.2 = (bf16[304,128]{1,0:T(8,128)(2,1)S(1)}, bf16[304,128]{1,0:T(8,128)(2,1)S(1)}, u32[]{:S(2)}, u32[]{:S(2)}) collective-permute-start(bf16[304,128]{1,0:T(8,128)(2,1)S(1)} %pick_rows.1.refs_0_.refs_2_.refs_11_.mine_ref), channel_id=1, source_target_pairs={{0,16},{4,20},{8,24},{12,28},{16,0},{20,4},{24,8},{28,12},{1,17},{... | collective-permute-start | bytes 233480 | tf_op jit(solution)/shard_map/ppermute | solution.py:213
  6.6 4.1 %collective-permute-start.3 = (bf16[304,128]{1,0:T(8,128)(2,1)S(1)}, bf16[304,128]{1,0:T(8,128)(2,1)S(1)}, u32[]{:S(2)}, u32[]{:S(2)}) collective-permute-start(bf16[304,128]{1,0:T(8,128)(2,1)S(1)} %pick_rows.1.refs_0_.refs_2_.refs_11_.mine_ref), channel_id=1, source_target_pairs={{0,24},{4,28},{8,16},{12,20},{16,8},{20,12},{24,0},{28,4},{1,25},{... | collective-permute-start | bytes 233480 | tf_op jit(solution)/shard_map/ppermute | solution.py:213
  10.8 3.2 %collective-permute-start.4 = (bf16[4,304,128]{2,1,0:T(8,128)(2,1)S(1)}, bf16[4,304,128]{2,1,0:T(8,128)(2,1)S(1)}, u32[]{:S(2)}, u32[]{:S(2)}) collective-permute-start(bf16[4,304,128]{2,1,0:T(8,128)(2,1)S(1)} %stack.1), channel_id=1, source_target_pairs={{0,4},{4,0},{8,12},{12,8},{16,20},{20,16},{24,28},{28,24},{1,5},{5... | collective-permute-start | bytes 933896 | tf_op jit(solution)/shard_map/ppermute | solution.py:213
  12.7 6.6 %collective-permute-start.8 = (f32[48,512]{1,0:T(8,128)S(1)}, f32[48,512]{1,0:T(8,128)S(1)}, u32[]{:S(2)}, u32[]{:S(2)}) collective-permute-start(f32[48,512]{1,0:T(8,128)S(1)} %copy-done.1), channel_id=1, source_target_pairs={{0,4},{4,0},{8,12},{12,8},{16,20},{20,16},{24,28},{28,24},{1,5},{5... | collective-permute-start | bytes 294920 | tf_op jit(solution)/shard_map/ppermute | solution.py:213
  14.8 4.4 %collective-permute-start.6 = (f32[2,1024]{1,0:T(2,128)S(1)}, f32[2,1024]{1,0:T(2,128)S(1)}, u32[]{:S(2)}, u32[]{:S(2)}) collective-permute-start(f32[2,1024]{1,0:T(2,128)S(1)} %get-tuple-element.16.refs_1_), channel_id=1, source_target_pairs={{0,1},{1,0},{2,3},{3,2},{4,7},{5,6},{6,5},{7,4},{8,9},{9,8},{10,11... | collective-permute-start | bytes 24584 | tf_op jit(solution)/shard_map/ppermute | solution.py:223
  18.1 3.4 %collective-permute-start.5 = (f32[2,1024]{1,0:T(2,128)S(1)}, f32[2,1024]{1,0:T(2,128)S(1)}, u32[]{:S(2)}, u32[]{:S(2)}) collective-permute-start(f32[2,1024]{1,0:T(2,128)S(1)} %get-tuple-element.16.refs_1_), channel_id=1, source_target_pairs={{0,2},{1,3},{2,0},{3,1},{4,6},{5,7},{6,4},{7,5},{8,10},{9,11},{10,... | collective-permute-start | bytes 24584 | tf_op jit(solution)/shard_map/ppermute | solution.py:213
  19.2 2.4 %collective-permute-start.7 = (f32[2,1024]{1,0:T(2,128)S(1)}, f32[2,1024]{1,0:T(2,128)S(1)}, u32[]{:S(2)}, u32[]{:S(2)}) collective-permute-start(f32[2,1024]{1,0:T(2,128)S(1)} %collective-permute-done.6.refs_3_), channel_id=1, source_target_pairs={{0,4},{4,0},{8,12},{12,8},{16,20},{20,16},{24,28},{28,24},{1,5},{5... | collective-permute-start | bytes 24584 | tf_op jit(solution)/shard_map/ppermute | solution.py:213
  22.5 3.4 %collective-permute-start.10 = (f32[2,56,128]{2,1,0:T(8,128)S(1)}, f32[2,56,128]{2,1,0:T(8,128)S(1)}, u32[]{:S(2)}, u32[]{:S(2)}) collective-permute-start(f32[2,56,128]{2,1,0:T(8,128)S(1)} %get-tuple-element.23), channel_id=1, source_target_pairs={{0,8},{4,20},{8,0},{12,28},{16,24},{20,4},{24,16},{28,12},{1,9},{5... | collective-permute-start | bytes 172040 | tf_op jit(solution)/shard_map/ppermute | solution.py:333
  23.0 4.5 %collective-permute-start.9 = (f32[2,56,128]{2,1,0:T(8,128)S(1)}, f32[2,56,128]{2,1,0:T(8,128)S(1)}, u32[]{:S(2)}, u32[]{:S(2)}) collective-permute-start(f32[2,56,128]{2,1,0:T(8,128)S(1)} %get-tuple-element.22), channel_id=1, source_target_pairs={{0,24},{4,28},{8,16},{12,20},{16,8},{20,12},{24,0},{28,4},{1,25},{... | collective-permute-start | bytes 172040 | tf_op jit(solution)/shard_map/ppermute | solution.py:213
  25.9 1.7 %collective-permute-start.11 = (f32[2,56,128]{2,1,0:T(8,128)S(1)}, f32[2,56,128]{2,1,0:T(8,128)S(1)}, u32[]{:S(2)}, u32[]{:S(2)}) collective-permute-start(f32[2,56,128]{2,1,0:T(8,128)S(1)} %collective-permute-done.10.asked_ref), channel_id=1, source_target_pairs={{0,4},{4,0},{8,12},{12,8},{16,20},{20,16},{24,28},{28,24},{1,5},{5... | collective-permute-start | bytes 172040 | tf_op jit(solution)/shard_map/ppermute | solution.py:213
  27.6 4.9 %collective-permute-start.13 = (f32[2,56,128]{2,1,0:T(8,128)S(1)}, f32[2,56,128]{2,1,0:T(8,128)S(1)}, u32[]{:S(2)}, u32[]{:S(2)}) collective-permute-start(f32[2,56,128]{2,1,0:T(8,128)S(1)} %emit_block.1.refs_4_), channel_id=1, source_target_pairs={{0,1},{1,0},{2,3},{3,2},{4,7},{5,6},{6,5},{7,4},{8,9},{9,8},{10,11... | collective-permute-start | bytes 172040 | tf_op jit(solution)/shard_map/ppermute | solution.py:223
  30.1 5.0 %collective-permute-start.12 = (f32[2,56,128]{2,1,0:T(8,128)S(1)}, f32[2,56,128]{2,1,0:T(8,128)S(1)}, u32[]{:S(2)}, u32[]{:S(2)}) collective-permute-start(f32[2,56,128]{2,1,0:T(8,128)S(1)} %emit_block.1.refs_4_), channel_id=1, source_target_pairs={{0,2},{1,3},{2,0},{3,1},{4,6},{5,7},{6,4},{7,5},{8,10},{9,11},{10,... | collective-permute-start | bytes 172040 | tf_op jit(solution)/shard_map/ppermute | solution.py:213
  32.5 2.6 %collective-permute-start.14 = (f32[2,56,128]{2,1,0:T(8,128)S(1)}, f32[2,56,128]{2,1,0:T(8,128)S(1)}, u32[]{:S(2)}, u32[]{:S(2)}) collective-permute-start(f32[2,56,128]{2,1,0:T(8,128)S(1)} %collective-permute-done.13.refs_6_), channel_id=1, source_target_pairs={{0,4},{4,0},{8,12},{12,8},{16,20},{20,16},{24,28},{28,24},{1,5},{5... | collective-permute-start | bytes 172040 | tf_op jit(solution)/shard_map/ppermute | solution.py:213
